TPU v7x, 512 devices: a whole 4x8x8 slice. The times are simulated.
512 devices in a mesh: pw: 32 (over z, x_hi, core), band: 16 (over x_lo, y).
Axes of the slice: x: 4 (x_hi: 2, x_lo: 2; x = x_hi * 2 + x_lo), y: 8, z: 8, core: 2. Of those that a mesh axis runs over, the one named last changes fastest.
Arguments:
- wavefunctions: bfloat16 [2, 16384, 2048], P(None, 'pw', 'band'), may hold values from -0.046875 to 0.046875
- miller: int32 [3, 16384], P(None, 'pw'), may hold values from -16 to 16
- reciprocal: float32 [3, 3], replicated, may hold values from -0.15 to 1.15, as said below
- fractional: float32 [3, 128], replicated, may hold values from 0 to 1
- species: int32 [128], replicated, may hold values from 0 to 3
- atom_order: int32 [128], replicated, may hold values from 0 to 127, each once
- radial_widths: float32 [4, 4], replicated, may hold values from 0.003 to 0.02
- onsite_base: float32 [4, 8, 8], replicated, may hold values from -2 to 2
- coupling: float32 [4, 64, 64], replicated, may hold values from -0.75 to 0.75
- occupations: float32 [2048], P('band'), may hold values from 0 to 3, as said below
Outputs:
- applied: bfloat16 [2, 16384, 2048], P(None, 'pw', 'band')
- onsite_d: float32 [128, 8, 8], P('pw')
Inputs may be any that keep to these rules, and one draw needn't show every extreme that they name: `atom_order`: a permutation of the atoms. `reciprocal`: each diagonal entry is 0.85 or more and each other entry 0.15 or less in magnitude. `occupations`: positive.
All inputs are finite; a program needn't handle non-finite values.
Results may differ from a plain program's by a relative error of at most 0.008.
Values may be sent and summed in bfloat16 or wider, within the bound.
No kernel may reach another device: no remote copies, remote signals or barrier semaphores. Data moves between devices by JAX's collectives and lax.ppermute only.
A program may use at most 64 MiB of HBM per device.

v0:
```python
import math

import jax
import jax.numpy as jnp
from jax import lax
from jax.sharding import PartitionSpec as P

HIGH = lax.Precision.HIGHEST


def cut_along(shard, dim, peers):
    lengths = shard.shape
    parts = shard.reshape(*lengths[:dim], peers, lengths[dim] // peers, *lengths[dim + 1 :])
    return jnp.moveaxis(parts, dim, 0)


def sum_at_owner(shard, axis, dim):
    peers = lax.axis_size(axis)
    parts = lax.all_to_all(cut_along(shard, dim, peers), axis, 0, 0, tiled=True)
    return jnp.sum(parts.astype(jnp.float32), axis=0)


def sent_to_all(shard, axis):
    copies = jnp.broadcast_to(shard, (lax.axis_size(axis), *shard.shape))
    return lax.all_to_all(copies, axis, split_axis=0, concat_axis=0, tiled=True)


def taken_together(shard, axis):
    everything = sent_to_all(shard, axis)
    return jnp.sum(everything, axis=0)


def in_order(parts, dim):
    lengths = list(parts.shape[1:])
    lengths[dim] *= parts.shape[0]
    return jnp.moveaxis(parts, 0, dim).reshape(lengths)


def gather_directly(shard, axis, dim):
    return in_order(sent_to_all(shard, axis), dim)


def projector_tile(miller_cols, reciprocal, positions, atom_species, radial_widths):
    two_pi = 2.0 * math.pi
    miller_real = miller_cols.astype(jnp.float32)
    g_vectors = two_pi * jnp.dot(reciprocal, miller_real, precision=HIGH)
    g_square = jnp.sum(g_vectors * g_vectors, axis=0)
    phases = two_pi * jnp.dot(positions.T, miller_real, precision=HIGH)
    onehot = (
        atom_species[:, None] == jnp.arange(radial_widths.shape[0], dtype=jnp.int32)[None, :]
    ).astype(jnp.float32)
    widths = jnp.dot(onehot, radial_widths, precision=HIGH)
    radial = jnp.exp(-0.5 * g_square[None, None, :] * (widths * widths)[:, :, None])
    s_part = radial[:, 0:2, :]
    p_first = g_vectors[None, :, :] * (widths[:, 2, None, None] * radial[:, 2:3, :])
    p_second = g_vectors[None, :, :] * (widths[:, 3, None, None] * radial[:, 3:4, :])
    p_part = jnp.concatenate([p_first, p_second], axis=1)
    cosine = jnp.cos(phases)[:, None, :]
    sine = jnp.sin(phases)[:, None, :]
    beta_real = jnp.concatenate([s_part * cosine, -p_part * sine], axis=1)
    beta_imag = jnp.concatenate([-s_part * sine, -p_part * cosine], axis=1)
    rows = positions.shape[1] * 8
    return (
        beta_real.reshape(rows, -1).astype(jnp.bfloat16),
        beta_imag.reshape(rows, -1).astype(jnp.bfloat16),
    )


def project(beta_real, beta_imag, wave_real, wave_imag):
    proj_real = jnp.dot(beta_real, wave_real, preferred_element_type=jnp.float32) + jnp.dot(
        beta_imag, wave_imag, preferred_element_type=jnp.float32
    )
    proj_imag = jnp.dot(beta_real, wave_imag, preferred_element_type=jnp.float32) - jnp.dot(
        beta_imag, wave_real, preferred_element_type=jnp.float32
    )
    return jnp.stack([proj_real, proj_imag], axis=1)


def occupancy_terms(projections, weights):
    grouped = projections.reshape(projections.shape[0] // 8, 8, 2, projections.shape[2])
    return jnp.einsum("aicn,ajcn,n->aij", grouped, grouped, weights, precision=HIGH)


def onsite_matrix(occupancy, atom_species, onsite_base, coupling):
    holding = occupancy.shape[0]
    kinds = onsite_base.shape[0]
    onehot = (atom_species[:, None] == jnp.arange(kinds, dtype=jnp.int32)[None, :]).astype(
        jnp.float32
    )
    response = jnp.einsum("skl,al->ask", coupling, occupancy.reshape(holding, 64), precision=HIGH)
    base = jnp.einsum("as,sk->ak", onehot, onsite_base.reshape(kinds, 64), precision=HIGH)
    total = base + jnp.einsum("as,ask->ak", onehot, response, precision=HIGH)
    return total.reshape(holding, 8, 8)


def weigh(onsite, projections):
    grouped = projections.reshape(projections.shape[0] // 8, 8, 2, projections.shape[2])
    weighted = jnp.einsum("aij,ajcn->aicn", onsite, grouped, precision=HIGH)
    return weighted.reshape(projections.shape).astype(jnp.bfloat16)


def back_project(beta_real, beta_imag, weighted):
    dims = (((0,), (0,)), ((), ()))
    q_real = weighted[:, 0, :]
    q_imag = weighted[:, 1, :]
    out_real = lax.dot_general(
        beta_real, q_real, dims, preferred_element_type=jnp.float32
    ) - lax.dot_general(beta_imag, q_imag, dims, preferred_element_type=jnp.float32)
    out_imag = lax.dot_general(
        beta_real, q_imag, dims, preferred_element_type=jnp.float32
    ) + lax.dot_general(beta_imag, q_real, dims, preferred_element_type=jnp.float32)
    return jnp.stack([out_real, out_imag], axis=0)


def local(
    wavefunctions,
    miller,
    reciprocal,
    fractional,
    species,
    atom_order,
    radial_widths,
    onsite_base,
    coupling,
    occupations,
):
    sorted_species = species[atom_order]
    sorted_positions = fractional[:, atom_order]
    owned_atoms = atom_order.shape[0] // lax.axis_size("pw")
    owner_index = lax.axis_index("pw")
    weights = occupations / (occupations.shape[0] * lax.axis_size("band"))
    wave_real = wavefunctions[0]
    wave_imag = wavefunctions[1]
    positions = sorted_positions
    kinds = sorted_species
    beta_real, beta_imag = projector_tile(miller, reciprocal, positions, kinds, radial_widths)
    projections = sum_at_owner(
        project(beta_real, beta_imag, wave_real, wave_imag).astype(jnp.bfloat16), "pw", 0
    )
    own_species = lax.dynamic_slice_in_dim(
        sorted_species, owner_index * owned_atoms, owned_atoms, 0
    )
    occupancy = taken_together(occupancy_terms(projections, weights), "band")
    onsite_own = onsite_matrix(occupancy, own_species, onsite_base, coupling)
    weighted = weigh(onsite_own, projections)
    positions = sorted_positions
    kinds = sorted_species
    beta_real, beta_imag = projector_tile(miller, reciprocal, positions, kinds, radial_widths)
    applied = back_project(beta_real, beta_imag, gather_directly(weighted, "pw", 0))
    return (applied.astype(jnp.bfloat16), onsite_own)


def solution(mesh):
    placed = (P(None, "pw", "band"), P(None, "pw"), P(), P(), P(), P(), P(), P(), P(), P("band"))
    return jax.shard_map(
        local,
        mesh=mesh,
        in_specs=placed,
        out_specs=(P(None, "pw", "band"), P("pw", None, None)),
        check_vma=False,
    )
```

profile of v0, /device:TPU:1, one launch (start us, length us, event | category | flops | bytes accessed | tf_op | source)
XLA Modules:
  0.0 94.7 jit_solution(9335857225821633283)
XLA Ops:
  0.6 0.7 compare_select_fusion
  1.3 1.6 %gather_fusion = s32[128]{0:T(128)S(1)} fusion(s32[128]{0:T(128)} %param.14, s32[1024]{0:T(1024)S(1)} %pad_clamp_fusion), kind=kCustom, calls=%fused_computation | custom fusion | bytes 1536 | tf_op jit(solution)/shard_map/gather | solution.py:127
  2.9 0.9 fusion.34
  3.8 0.9 multiply_reduce_fusion
  4.9 0.8 copy.35
  6.3 3.1 %fusion.33 = (f32[128,512]{1,0:T(8,128)S(1)}, f32[128,512]{1,0:T(8,128)S(1)}) fusion(f32[128,3]{1,0:T(8,128)S(1)} %gather_fusion.1, s32[3,512]{1,0:T(4,128)} %param.11), kind=kOutput, calls=%fused_computation.73 | convolution fusion | flops 2426368 | bytes 531968 | tf_op jit(solution)/shard_map/dot_general | solution.py:48
  11.4 0.8 multiply_convert_fusion
  13.6 0.7 fusion.1
  15.0 0.8 pad_maximum_fusion
  15.9 14.6 %all-to-all-start = ((bf16[32,32,2,128]{3,1,2,0:T(8,128)(2,1)}), bf16[32,32,2,128]{3,1,2,0:T(8,128)(2,1)S(1)}, u32[]{:S(2)}, u32[]{:S(2)}) async-start(bf16[32,32,2,128]{3,1,2,0:T(8,128)(2,1)} %pad_maximum_fusion), calls=%async_computation | async-start | bytes 1048576 | tf_op jit(solution)/shard_map/all_to_all | solution.py:19
  30.5 16.9 %all-to-all-done = bf16[32,32,2,128]{3,1,2,0:T(8,128)(2,1)S(1)} async-done(((bf16[32,32,2,128]{3,1,2,0:T(8,128)(2,1)}), bf16[32,32,2,128]{3,1,2,0:T(8,128)(2,1)S(1)}, u32[]{:S(2)}, u32[]{:S(2)}) %all-to-all-start) | async-done | bytes 524320 | tf_op jit(solution)/shard_map/all_to_all | solution.py:19
  47.7 0.8 reshape.117
  48.5 7.0 %all-to-all-start.1 = ((f32[16,1,256]{2,1,0:T(1,128)}), f32[16,1,256]{2,1,0:T(1,128)S(1)}, u32[]{:S(2)}, u32[]{:S(2)}) async-start(f32[16,1,256]{2,1,0:T(1,128)} %reshape.117), calls=%async_computation.1 | async-start | bytes 32768 | tf_op jit(solution)/shard_map/all_to_all | solution.py:25
  55.6 7.2 %all-to-all-done.1 = f32[16,1,256]{2,1,0:T(1,128)S(1)} async-done(((f32[16,1,256]{2,1,0:T(1,128)}), f32[16,1,256]{2,1,0:T(1,128)S(1)}, u32[]{:S(2)}, u32[]{:S(2)}) %all-to-all-start.1) | async-done | bytes 16416 | tf_op jit(solution)/shard_map/all_to_all | solution.py:25
  63.3 0.7 reduce
  65.3 0.9 broadcast_in_dim.8
  66.2 7.7 %all-to-all-start.2 = ((bf16[32,32,2,128]{3,1,2,0:T(8,128)(2,1)}), bf16[32,32,2,128]{3,1,2,0:T(8,128)(2,1)S(1)}, u32[]{:S(2)}, u32[]{:S(2)}) async-start(bf16[32,32,2,128]{3,1,2,0:T(8,128)(2,1)} %broadcast_in_dim.8), calls=%async_computation.2 | async-start | bytes 1048576 | tf_op jit(solution)/shard_map/all_to_all | solution.py:25
  73.9 0.7 reshape.90
  74.6 16.3 %all-to-all-done.2 = bf16[32,32,2,128]{3,1,2,0:T(8,128)(2,1)S(1)} async-done(((bf16[32,32,2,128]{3,1,2,0:T(8,128)(2,1)}), bf16[32,32,2,128]{3,1,2,0:T(8,128)(2,1)S(1)}, u32[]{:S(2)}, u32[]{:S(2)}) %all-to-all-start.2) | async-done | bytes 524320 | tf_op jit(solution)/shard_map/all_to_all | solution.py:25
  91.0 0.7 fusion.7
  91.7 0.7 fusion.6
  92.4 0.8 fusion.5
  93.2 0.7 fusion.4
  94.0 0.7 pad_maximum_fusion.1
  (39 shorter events, 7.1 us)
Async XLA Ops:
  0.6 63.7 %copy-start = (f32[4,64,64]{2,1,0:T(8,128)S(1)}, f32[4,64,64]{2,1,0:T(8,128)}, u32[]{:S(2)}) copy-start(f32[4,64,64]{2,1,0:T(8,128)} %param.18) | copy-start | bytes 196612
  11.4 1.0 %copy-start.2 = (bf16[2,512,128]{2,1,0:T(8,128)(2,1)S(1)}, bf16[2,512,128]{2,1,0:T(8,128)(2,1)}, u32[]{:S(2)}) copy-start(bf16[2,512,128]{2,1,0:T(8,128)(2,1)} %param.10) | copy-start | bytes 786436
  15.0 15.5 %copy-start.3 = (f32[128]{0:T(128)S(1)}, f32[128]{0:T(128)}, u32[]{:S(2)}) copy-start(f32[128]{0:T(128)} %param.19) | copy-start | bytes 1540
  15.9 39.7 %copy-start.1 = (f32[4,8,8]{2,1,0:T(8,128)S(1)}, f32[4,8,8]{2,1,0:T(8,128)}, u32[]{:S(2)}) copy-start(f32[4,8,8]{2,1,0:T(8,128)} %param.17) | copy-start | bytes 3076
  15.9 31.6 %all-to-all-start = ((bf16[32,32,2,128]{3,1,2,0:T(8,128)(2,1)}), bf16[32,32,2,128]{3,1,2,0:T(8,128)(2,1)S(1)}, u32[]{:S(2)}, u32[]{:S(2)}) async-start(bf16[32,32,2,128]{3,1,2,0:T(8,128)(2,1)} %pad_maximum_fusion), calls=%async_computation | async-start | bytes 1048576 | tf_op jit(solution)/shard_map/all_to_all | solution.py:19
  48.5 14.3 %all-to-all-start.1 = ((f32[16,1,256]{2,1,0:T(1,128)}), f32[16,1,256]{2,1,0:T(1,128)S(1)}, u32[]{:S(2)}, u32[]{:S(2)}) async-start(f32[16,1,256]{2,1,0:T(1,128)} %reshape.117), calls=%async_computation.1 | async-start | bytes 32768 | tf_op jit(solution)/shard_map/all_to_all | solution.py:25
  66.2 24.7 %all-to-all-start.2 = ((bf16[32,32,2,128]{3,1,2,0:T(8,128)(2,1)}), bf16[32,32,2,128]{3,1,2,0:T(8,128)(2,1)S(1)}, u32[]{:S(2)}, u32[]{:S(2)}) async-start(bf16[32,32,2,128]{3,1,2,0:T(8,128)(2,1)} %broadcast_in_dim.8), calls=%async_computation.2 | async-start | bytes 1048576 | tf_op jit(solution)/shard_map/all_to_all | solution.py:25
where the time goes:
time: 95.3 us; the launch traced here: 94.7 us
  waiting for transfers between devices  40.4 us (42%)
  starting transfers between devices  29.2 us (31%)
  matrix products  11.6 us (12%)
  local copies, waits for them, and re-layouts  6.76 us (7%)
  other arithmetic  5.78 us (6%)
    all_to_all x2, waiting for transfers between devices, sent_to_all(): return lax.all_to_all(copies, axis, split_axis=0, concat_axis=0, tiled=True)  23.5 us
    all_to_all x1, waiting for transfers between devices, sum_at_owner(): parts = lax.all_to_all(cut_along(shard, dim, peers), axis, 0, 0, tiled=True)  16.9 us
    all_to_all x2, starting transfers between devices, sent_to_all(): return lax.all_to_all(copies, axis, split_axis=0, concat_axis=0, tiled=True)  14.7 us
    all_to_all x1, starting transfers between devices, sum_at_owner(): parts = lax.all_to_all(cut_along(shard, dim, peers), axis, 0, 0, tiled=True)  14.6 us
    dot_general x1, matrix products, projector_tile(): phases = two_pi * jnp.dot(positions.T, miller_real, precision=HIGH)  3.14 us
    unnamed x12, local copies, waits for them, and re-layouts  1.92 us
  transfers between devices with their start and end apart: 3, of which 3 were waited for; matrix products, arithmetic and copies ran while one was open for 1% of the time, Pallas kernels for 0%

commit v1 on v0

v1 whole, which is shorter than its diff:
```python
import math

import jax
import jax.numpy as jnp
from jax import lax
from jax.experimental import pallas as pl
from jax.experimental.pallas import tpu as pltpu
from jax.sharding import Mesh
from jax.sharding import PartitionSpec as P

HIGH = lax.Precision.HIGHEST
F32 = jnp.float32
BF16 = jnp.bfloat16
SIN = (6.283185005187988, -41.341590881347656, 81.59994506835938,
       -76.61447143554688, 41.3428840637207, -12.471243858337402)
COS = (1.0, -19.73920440673828, 64.93911743164062, -85.45014190673828,
       60.16762924194336, -25.967599868774414, 6.528658390045166)
NT = (((1,), (1,)), ((), ()))
NN = (((1,), (0,)), ((), ()))


def dot_high(left, right, dims):
    return lax.dot_general(left, right, dims, precision=HIGH, preferred_element_type=F32)


def iota(shape, dim):
    return lax.broadcasted_iota(jnp.int32, shape, dim)


def horner(coefficients, z):
    total = jnp.full_like(z, coefficients[-1])
    for c in coefficients[-2::-1]:
        total = total * z + c
    return total


def vmem():
    return pl.BlockSpec(memory_space=pltpu.VMEM)


def smem():
    return pl.BlockSpec(memory_space=pltpu.SMEM)


def tables_kernel(core_ref, recip_ref, widths_ref, wave_ref, miller_ref, frac_ref, species_ref,
                  order_ref, beta_ref, proj_ref, rhs_ref):
    core = core_ref[0]
    gcount = miller_ref.shape[1]
    natoms = order_ref.shape[1]
    owners = beta_ref.shape[0] // 32
    kinds = widths_ref.shape[0]
    spec = species_ref[...]
    rows = [frac_ref[d:d + 1, :] for d in range(3)]
    for c in range(4):
        row = jnp.zeros((1, natoms), F32)
        for s in range(kinds):
            row = jnp.where(spec == s, widths_ref[s, c], row)
        rows.append(row)
    rows.append(jnp.zeros((1, natoms), F32))
    by_atom = jnp.concatenate(rows, axis=0)
    pick = (iota((natoms, natoms), 0) == order_ref[...]).astype(F32)
    by_slot = dot_high(by_atom, pick, NN)
    row_id = iota((owners * 8, natoms), 0)
    slot = (row_id // 8) * 8 + core * 4 + row_id % 4
    expand = (iota((owners * 8, natoms), 1) == slot).astype(F32)
    by_row = dot_high(expand, by_slot, NT)

    mil = miller_ref[...].astype(F32)
    m = [mil[d:d + 1, :] for d in range(3)]
    two_pi = 2.0 * math.pi
    g = [two_pi * (recip_ref[d, 0] * m[0] + recip_ref[d, 1] * m[1] + recip_ref[d, 2] * m[2]) for d in range(3)]
    g2 = g[0] * g[0] + g[1] * g[1] + g[2] * g[2]
    wide = (8, gcount)
    m = [jnp.broadcast_to(a, wide) for a in m]
    g2 = jnp.broadcast_to(g2, wide)
    g = [jnp.broadcast_to(a, wide) for a in g]
    first = iota(wide, 0) < 4
    pair_g = (None, jnp.where(first, g[0], g[1]), jnp.where(first, g[2], g[0]), jnp.where(first, g[1], g[2]))
    first1 = iota((8, 1), 0) < 4

    for q in range(owners):
        par = by_row[q * 8:q * 8 + 8, :]
        col = [par[:, k:k + 1] for k in range(7)]
        turns = col[0] * m[0] + col[1] * m[1] + col[2] * m[2]
        r = turns - jnp.round(turns)
        z = r * r
        sin = horner(SIN, z) * r
        cos = horner(COS, z)
        minus_sin = -sin
        pair_w = (jnp.where(first1, col[3], col[4]), col[5], jnp.where(first1, col[5], col[6]), col[6])
        re, im = [], []
        for p in range(4):
            w = pair_w[p]
            decay = jnp.exp(g2 * (-0.5 * (w * w)))
            if p == 0:
                re.append(decay * cos)
                im.append(decay * minus_sin)
            else:
                amp = pair_g[p] * ((-w) * decay)
                re.append(amp * sin)
                im.append(amp * cos)
        beta_ref[q * 32:q * 32 + 32, 0:gcount] = jnp.concatenate(re, axis=0).astype(BF16)
        beta_ref[q * 32:q * 32 + 32, gcount:] = jnp.concatenate(im, axis=0).astype(BF16)

    nb = wave_ref.shape[2]
    real, imag = wave_ref[0], wave_ref[1]
    rhs_ref[0:gcount, 0:nb] = real
    rhs_ref[0:gcount, nb:] = imag
    rhs_ref[gcount:, 0:nb] = imag
    rhs_ref[gcount:, nb:] = -real
    proj_ref[...] = jnp.dot(beta_ref[...], rhs_ref[...], preferred_element_type=F32).astype(proj_ref.dtype)


def tables(core, kind, wavefunctions, miller, reciprocal, fractional, species, atom_order, radial_widths):
    gcount, nb = wavefunctions.shape[1:]
    nrows = atom_order.shape[1] * 4
    return pl.pallas_call(
        tables_kernel,
        out_shape=(jax.ShapeDtypeStruct((nrows, 2 * gcount), BF16), jax.ShapeDtypeStruct((nrows, 2 * nb), kind)),
        in_specs=[smem(), smem(), smem()] + [vmem()] * 5,
        out_specs=(vmem(), vmem()),
        scratch_shapes=[pltpu.VMEM((2 * gcount, 2 * nb), BF16)],
        compiler_params=pltpu.CompilerParams(vmem_limit_bytes=32 << 20),
        name="tables",
    )(core, reciprocal, radial_widths, wavefunctions, miller, fractional, species, atom_order)


def prepare_kernel(owner_ref, species_ref, order_ref, mine_ref, other_ref, coupling_ref, base_ref,
                   mine_t_ref, other_t_ref, couple_ref, base_rows_ref):
    for src, dst in ((mine_ref, mine_t_ref), (other_ref, other_t_ref)):
        nrows, width = src.shape[0], src.shape[1] // 2
        for part in range(2):
            block = src[:, part * width:(part + 1) * width]
            dst[:, part * nrows:(part + 1) * nrows] = block.T
    row = iota((32, 64), 0) % 4
    base = jnp.zeros((32, 64), F32)
    for a in range(4):
        s = species_ref[order_ref[owner_ref[0] * 4 + a]]
        couple_ref[:, a * 64:(a + 1) * 64] = coupling_ref[s]
        base = jnp.where(row == a, base_ref[pl.ds(s, 1), :], base)
    base_rows_ref[...] = base


def prepare(owner, species, atom_order, mine, other, coupling, base):
    nrows, width = mine.shape
    turned = jax.ShapeDtypeStruct((width // 2, 2 * nrows), BF16)
    return pl.pallas_call(
        prepare_kernel,
        out_shape=(turned, turned, jax.ShapeDtypeStruct((64, 256), F32), jax.ShapeDtypeStruct((32, 64), F32)),
        in_specs=[smem(), smem(), smem()] + [vmem()] * 4,
        out_specs=(vmem(),) * 4,
        compiler_params=pltpu.CompilerParams(vmem_limit_bytes=32 << 20),
        name="prepare",
    )(owner, species, atom_order, mine, other, coupling, base)


def occupancy_kernel(parts_ref, weights_ref, proj_ref, send_ref):
    total = parts_ref[0].astype(F32)
    for k in range(1, parts_ref.shape[0]):
        total = total + parts_ref[k].astype(F32)
    proj_ref[...] = total
    w = weights_ref[...]
    gram = dot_high(total * jnp.concatenate([w, w], axis=1), total, NT)
    gram = jnp.where(iota((32, 32), 0) % 4 == iota((32, 32), 1) % 4, gram, 0.0)
    lane = iota((32, 128), 1)
    spread = (iota((32, 128), 0) // 4 == lane % 8).astype(F32)
    wide = dot_high(gram, spread, NN)
    row = iota((32, 128), 0)
    wide = jnp.where(((lane // 8) % 8 == row // 4) & (lane // 64 == (row % 4) % 2), wide, 0.0)
    fold = ((iota((8, 32), 1) % 4) // 2 == iota((8, 32), 0)).astype(F32)
    flat = dot_high(fold, wide, NN)[0:2, :]
    for k in range(send_ref.shape[0]):
        send_ref[k] = flat


def occupancy_step(parts, weights, peers):
    _, nrows, width = parts.shape
    return pl.pallas_call(
        occupancy_kernel,
        out_shape=(jax.ShapeDtypeStruct((nrows, width), F32), jax.ShapeDtypeStruct((peers, 2, 128), F32)),
        in_specs=[vmem(), vmem()],
        out_specs=(vmem(), vmem()),
        name="occupancy",
    )(parts, weights)


def weigh_kernel(parts_ref, proj_ref, couple_ref, base_ref, onsite_ref, send_ref):
    occ = jnp.sum(parts_ref[...], axis=0)
    flat = jnp.concatenate([occ[0:1, :], occ[1:2, :]], axis=1)
    lane = iota((32, 256), 1)
    by_atom = jnp.where(lane // 64 == iota((32, 256), 0) % 4, flat, 0.0)
    onsite = dot_high(by_atom, couple_ref[...], NT) + base_ref[...]
    onsite_ref[...] = onsite[0:4, :]
    row = iota((32, 64), 0)
    onsite = jnp.where(iota((32, 64), 1) // 8 == row // 4, onsite, 0.0)
    spread = (iota((64, 32), 0) % 8 == iota((64, 32), 1) // 4).astype(F32)
    full = dot_high(onsite, spread, NN)
    full = jnp.where(iota((32, 32), 0) % 4 == iota((32, 32), 1) % 4, full, 0.0)
    weighted = dot_high(full, proj_ref[...], NN).astype(BF16)
    for k in range(send_ref.shape[0]):
        send_ref[k] = weighted


def weigh(parts, proj, couple, base_rows, peers):
    return pl.pallas_call(
        weigh_kernel,
        out_shape=(jax.ShapeDtypeStruct((4, 64), F32), jax.ShapeDtypeStruct((peers, *proj.shape), BF16)),
        in_specs=[vmem()] * 4,
        out_specs=(vmem(), vmem()),
        name="weigh",
    )(parts, proj, couple, base_rows)


def product_with(table_ref, weighted_ref):
    nrows, width = weighted_ref.shape
    real, imag = weighted_ref[:, :width // 2], weighted_ref[:, width // 2:]
    turned = jnp.concatenate([-imag, real], axis=1)
    return (jnp.dot(table_ref[:, :nrows], weighted_ref[...], preferred_element_type=F32)
            + jnp.dot(table_ref[:, nrows:], turned, preferred_element_type=F32))


def back_kernel(table_ref, weighted_ref, out_ref):
    out_ref[...] = product_with(table_ref, weighted_ref)


def back_last_kernel(table_ref, weighted_ref, before_ref, out_ref):
    total = before_ref[...] + product_with(table_ref, weighted_ref)
    half = total.shape[1] // 2
    out_ref[0] = total[:, :half].astype(BF16)
    out_ref[1] = total[:, half:].astype(BF16)


def back_project(table, weighted, before=None):
    gcount, width = table.shape[0], weighted.shape[1]
    if before is None:
        return pl.pallas_call(
            back_kernel,
            out_shape=jax.ShapeDtypeStruct((gcount, width), F32),
            in_specs=[vmem()] * 2, out_specs=vmem(), name="back",
        )(table, weighted)
    return pl.pallas_call(
        back_last_kernel,
        out_shape=jax.ShapeDtypeStruct((2, gcount, width // 2), BF16),
        in_specs=[vmem()] * 3, out_specs=vmem(), name="back_last",
    )(table, weighted, before)


def local(wavefunctions, miller, reciprocal, fractional, species, atom_order, radial_widths,
          onsite_base, coupling, occupations):
    chips = lax.axis_size("chip")
    bands = lax.axis_size("band")
    core = lax.axis_index("core")
    owner = lax.axis_index("chip") * 2 + core
    swap = [(0, 1), (1, 0)]
    nb = wavefunctions.shape[2]
    args = (wavefunctions, miller, reciprocal, fractional, species.reshape(1, -1), atom_order.reshape(1, -1),
            radial_widths)
    other, other_proj = tables((1 - core).reshape(1), BF16, *args)
    received = lax.ppermute(other_proj, "core", swap)
    mine, mine_proj = tables(core.reshape(1), F32, *args)
    chip_sum = (mine_proj + received.astype(F32)).astype(BF16).reshape(chips, -1, 2 * nb)
    parts = lax.all_to_all(chip_sum, "chip", 0, 0, tiled=True)
    mine_t, other_t, couple, base_rows = prepare(
        owner.reshape(1), species, atom_order, mine, other, coupling, onsite_base.reshape(-1, 64))

    weights = (occupations / (nb * bands)).reshape(1, -1)
    proj, occupancy = occupancy_step(parts, weights, bands)
    occupancy = lax.all_to_all(occupancy, "band", 0, 0, tiled=True)
    onsite, weighted = weigh(occupancy, proj, couple, base_rows, chips)
    weighted = lax.all_to_all(weighted, "chip", 0, 0, tiled=True).reshape(-1, 2 * nb)
    other_weighted = lax.ppermute(weighted, "core", swap)
    applied = back_project(mine_t, weighted)
    applied = back_project(other_t, other_weighted, applied)
    return applied, onsite.reshape(-1, 8, 8)


def solution(mesh):
    peers, bands = mesh.devices.shape
    inner = Mesh(mesh.devices.reshape(peers // 2, 2, bands), ("chip", "core", "band"))
    pw = ("chip", "core")
    placed = (P(None, pw, "band"), P(None, pw), P(), P(), P(), P(), P(), P(), P(), P("band"))
    return jax.shard_map(
        local,
        mesh=inner,
        in_specs=placed,
        out_specs=(P(None, pw, "band"), P(pw, None, None)),
        check_vma=False,
    )
```

time: 95.3 us -> 84.4 us (0.89)
  waiting for transfers between devices: 40.4 us -> 15.2 us
  blocking collectives: 0 us -> 15.1 us
  Pallas kernels: 0 us -> 14.7 us
  matrix products: 11.6 us -> 0 us
  other arithmetic: 5.78 us -> 1.36 us
    all_to_all x3 -> x2, waiting for transfers between devices: 40.4 us -> 15.2 us  [the longest x1 12.4 us: local(): parts = lax.all_to_all(chip_sum, 'chip', 0, 0, tiled=True)]
    all_to_all x0 -> x1, blocking collectives: none -> 15.1 us  [local(): lax.all_to_all(weighted, 'chip', 0, 0, tiled=True).reshape(-1, 2 * nb)]
    all_to_all x3 -> x2, starting transfers between devices: 29.2 us -> 14.4 us  [the longest x1 7.36 us: local(): parts = lax.all_to_all(chip_sum, 'chip', 0, 0, tiled=True)]
    pallas_call x0 -> x7, Pallas kernels: none -> 14.7 us  [the longest x2 4.15 us: tables(): pl.pallas_call(tables_kernel, out_shape=(jax.ShapeDtypeStruct((nrows, 2 *...]
    ppermute x0 -> x2, starting transfers between devices: none -> 14.5 us  [the longest x1 8.78 us: local(): received = lax.ppermute(other_proj, 'core', swap)]
    dot_general x16 -> x0, matrix products: 11.6 us -> none  [the longest x1 3.14 us: projector_tile(): phases = two_pi * jnp.dot(positions.T, miller_real, precision=HIGH)]
    unnamed x12 -> x40, local copies, waits for them, and re-layouts: 1.92 us -> 6.83 us
    another operation x4 -> x0, other arithmetic: 2.94 us -> none
  transfers between devices with their start and end apart: 3 -> 4, of which waited for: 3 -> 2; matrix products, arithmetic and copies ran while one was open for 1% -> 2% of each run, Pallas kernels for 0% -> 7%
where the time goes in v1:
time: 84.4 us; the launch traced here: 83.7 us
  starting transfers between devices  29 us (34%)
  waiting for transfers between devices  15.2 us (18%)
  blocking collectives  15.1 us (18%)
  Pallas kernels  14.7 us (17%)
  local copies, waits for them, and re-layouts  7.59 us (9%)
  other arithmetic  1.36 us (2%)
    all_to_all x1, blocking collectives, local(): lax.all_to_all(weighted, 'chip', 0, 0, tiled=True).reshape(-1, 2 * nb)  15.1 us
    all_to_all x1, waiting for transfers between devices, local(): parts = lax.all_to_all(chip_sum, 'chip', 0, 0, tiled=True)  12.4 us
    ppermute x1, starting transfers between devices, local(): received = lax.ppermute(other_proj, 'core', swap)  8.78 us
    all_to_all x1, starting transfers between devices, local(): parts = lax.all_to_all(chip_sum, 'chip', 0, 0, tiled=True)  7.36 us
    all_to_all x1, starting transfers between devices, local(): occupancy = lax.all_to_all(occupancy, 'band', 0, 0, tiled=True)  7.08 us
    unnamed x40, local copies, waits for them, and re-layouts  6.83 us
    ppermute x1, starting transfers between devices, local(): other_weighted = lax.ppermute(weighted, 'core', swap)  5.74 us
    pallas_call x2, Pallas kernels, tables(): pl.pallas_call(tables_kernel, out_shape=(jax.ShapeDtypeStruct((nrows, 2 *...  4.15 us
  transfers between devices with their start and end apart: 4, of which 2 were waited for; matrix products, arithmetic and copies ran while one was open for 2% of the time, Pallas kernels for 7%

profile of v1, /device:TPU:1, one launch (start us, length us, event | category | flops | bytes accessed | tf_op | source)
XLA Modules:
  0.0 83.7 jit_solution(18185037885340686630)
XLA Ops:
  0.7 0.6 copy-done.6
  1.4 0.9 %copy-done.2 = bf16[2,512,128]{2,1,0:T(8,128)(2,1)S(1)} copy-done((bf16[2,512,128]{2,1,0:T(8,128)(2,1)S(1)}, bf16[2,512,128]{2,1,0:T(8,128)(2,1)}, u32[]{:S(2)}) %copy-start.2) | copy-done | bytes 262168
  2.3 2.1 %tables.3 = (bf16[512,1024]{1,0:T(8,128)(2,1)S(1)}, bf16[512,256]{1,0:T(8,128)(2,1)S(1)}) custom-call(s32[1]{0:T(128)} %bitcast.4.core_ref, f32[3,3]{1,0:T(4,128)S(1)} %copy-done.8, f32[4,4]{1,0:T(4,128)S(1)} %copy-done.9, bf16[2,512,128]{2,1,0:T(8,128)(2,1)S(1)} %copy-done.2, s32[3,512]{1,0:T(4,128)S(1)} %copy-done.6, f32[3,128]{1,0:T(4,128)S(1)} %copy-done.10, ...), custom_call_target="tpu_custom_call" | custom-call | tf_op jit(solution)/shard_map/tables/pallas_call | solution.py:117
  4.4 8.8 %collective-permute-start = (bf16[512,256]{1,0:T(8,128)(2,1)S(1)}, bf16[512,256]{1,0:T(8,128)(2,1)S(1)}, u32[]{:S(2)}, u32[]{:S(2)}) collective-permute-start(bf16[512,256]{1,0:T(8,128)(2,1)S(1)} %get-tuple-element.18), channel_id=1, source_target_pairs={{0,16},{16,0},{1,17},{17,1},{2,18},{18,2},{3,19},{19,3},{4,20},{20... | collective-permute-start | bytes 786440 | tf_op jit(solution)/shard_map/ppermute | solution.py:259
  13.2 2.1 %tables.2 = (bf16[512,1024]{1,0:T(8,128)(2,1)S(1)}, f32[512,256]{1,0:T(8,128)S(1)}) custom-call(s32[1]{0:T(128)} %bitcast.1.core_ref, f32[3,3]{1,0:T(4,128)S(1)} %copy-done.8, f32[4,4]{1,0:T(4,128)S(1)} %copy-done.9, bf16[2,512,128]{2,1,0:T(8,128)(2,1)S(1)} %copy-done.3, s32[3,512]{1,0:T(4,128)S(1)} %copy-done.6, f32[3,128]{1,0:T(4,128)S(1)} %copy-done.10, ...), custom_call_target="tpu_custom_call" | custom-call | tf_op jit(solution)/shard_map/tables/pallas_call | solution.py:117
  15.3 0.8 add_convert_fusion
  16.1 7.4 %all-to-all-start = ((bf16[16,32,256]{2,1,0:T(8,128)(2,1)}), bf16[16,32,256]{2,1,0:T(8,128)(2,1)S(1)}, u32[]{:S(2)}, u32[]{:S(2)}) async-start(bf16[16,32,256]{2,1,0:T(8,128)(2,1)} %bitcast.5), calls=%async_computation | async-start | bytes 524288 | tf_op jit(solution)/shard_map/all_to_all | solution.py:262
  24.0 12.4 %all-to-all-done.parts_ref = bf16[16,32,256]{2,1,0:T(8,128)(2,1)S(1)} async-done(((bf16[16,32,256]{2,1,0:T(8,128)(2,1)}), bf16[16,32,256]{2,1,0:T(8,128)(2,1)S(1)}, u32[]{:S(2)}, u32[]{:S(2)}) %all-to-all-start) | async-done | bytes 262176 | tf_op jit(solution)/shard_map/all_to_all | solution.py:262
  36.4 0.7 copy-done.14
  37.1 2.1 %occupancy.1 = (f32[32,256]{1,0:T(8,128)}, f32[16,2,128]{2,1,0:T(2,128)}) custom-call(bf16[16,32,256]{2,1,0:T(8,128)(2,1)} %copy-done.14, f32[1,128]{1,0:T(1,128)} %multiply_bitcast_fusion.weights_ref), custom_call_target="tpu_custom_call" | custom-call | tf_op jit(solution)/shard_map/occupancy/pallas_call | solution.py:178
  39.2 7.1 %all-to-all-start.1 = ((f32[16,2,128]{2,1,0:T(2,128)}), f32[16,2,128]{2,1,0:T(2,128)S(1)}, u32[]{:S(2)}, u32[]{:S(2)}) async-start(f32[16,2,128]{2,1,0:T(2,128)} %get-tuple-element.19), calls=%async_computation.1 | async-start | bytes 32768 | tf_op jit(solution)/shard_map/all_to_all | solution.py:268
  46.4 1.2 %prepare.1 = (bf16[512,1024]{1,0:T(8,128)(2,1)S(1)}, bf16[512,1024]{1,0:T(8,128)(2,1)S(1)}, f32[64,256]{1,0:T(8,128)S(1)}, f32[32,64]{1,0:T(8,128)S(1)}) custom-call(s32[1]{0:T(128)} %bitcast.owner_ref, s32[128]{0:T(128)S(1)} %copy-done.11, s32[128]{0:T(128)S(1)} %copy-done.12, bf16[512,1024]{1,0:T(8,128)(2,1)S(1)} %get-tuple-element.14.mine_ref, ...), custom_call_target="tpu_custom_call" | custom-call | tf_op jit(solution)/shard_map/prepare/pallas_call | solution.py:147
  47.6 1.0 %copy-done = bf16[512,1024]{1,0:T(8,128)(2,1)} copy-done((bf16[512,1024]{1,0:T(8,128)(2,1)}, bf16[512,1024]{1,0:T(8,128)(2,1)S(1)}, u32[]{:S(2)}) %copy-start) | copy-done | bytes 1048600
  48.5 1.0 %copy-done.1 = bf16[512,1024]{1,0:T(8,128)(2,1)} copy-done((bf16[512,1024]{1,0:T(8,128)(2,1)}, bf16[512,1024]{1,0:T(8,128)(2,1)S(1)}, u32[]{:S(2)}) %copy-start.1) | copy-done | bytes 1048600
  49.5 0.6 copy-done.5
  50.7 2.9 %all-to-all-done.1.parts_ref = f32[16,2,128]{2,1,0:T(2,128)S(1)} async-done(((f32[16,2,128]{2,1,0:T(2,128)}), f32[16,2,128]{2,1,0:T(2,128)S(1)}, u32[]{:S(2)}, u32[]{:S(2)}) %all-to-all-start.1) | async-done | bytes 16416 | tf_op jit(solution)/shard_map/all_to_all | solution.py:268
  53.6 0.6 copy-done.16
  54.2 2.2 %weigh.1 = (f32[4,64]{1,0:T(4,128)}, bf16[16,32,256]{2,1,0:T(8,128)(2,1)}) custom-call(f32[16,2,128]{2,1,0:T(2,128)} %copy-done.16, f32[32,256]{1,0:T(8,128)} %get-tuple-element.20.proj_ref, f32[64,256]{1,0:T(8,128)} %copy-done.5, f32[32,64]{1,0:T(8,128)} %copy-done.7), custom_call_target="tpu_custom_call" | custom-call | tf_op jit(solution)/shard_map/weigh/pallas_call | solution.py:205
  56.4 15.1 %all_to_all.15 = bf16[16,32,256]{2,1,0:T(8,128)(2,1)S(1)} all-to-all(bf16[16,32,256]{2,1,0:T(8,128)(2,1)} %get-tuple-element.23), channel_id=1, replica_groups=mesh['chip'=16,'core'=2,'band'=16] {'chip'}, dimensions={0} | all-to-all | bytes 524288 | tf_op jit(solution)/shard_map/all_to_all | solution.py:270
  71.4 5.7 %collective-permute-start.1 = (bf16[512,256]{1,0:T(8,128)(2,1)S(1)}, bf16[512,256]{1,0:T(8,128)(2,1)S(1)}, u32[]{:S(2)}, u32[]{:S(2)}) collective-permute-start(bf16[512,256]{1,0:T(8,128)(2,1)S(1)} %bitcast.13), channel_id=1, source_target_pairs={{0,16},{16,0},{1,17},{17,1},{2,18},{18,2},{3,19},{19,3},{4,20},{20... | collective-permute-start | bytes 786440 | tf_op jit(solution)/shard_map/ppermute | solution.py:271
  77.2 0.7 reshape.43
  77.9 2.5 %back.1.before_ref = f32[512,256]{1,0:T(8,128)} custom-call(bf16[512,1024]{1,0:T(8,128)(2,1)} %copy-done, bf16[512,256]{1,0:T(8,128)(2,1)} %bitcast.14), custom_call_target="tpu_custom_call" | custom-call | tf_op jit(solution)/shard_map/back/pallas_call | solution.py:236
  80.4 0.7 copy-done.15
  81.1 2.6 %back_last.1 = bf16[2,512,128]{2,1,0:T(8,128)(2,1)} custom-call(bf16[512,1024]{1,0:T(8,128)(2,1)} %copy-done.1, bf16[512,256]{1,0:T(8,128)(2,1)} %copy-done.15, f32[512,256]{1,0:T(8,128)} %back.1.before_ref), custom_call_target="tpu_custom_call" | custom-call | tf_op jit(solution)/shard_map/back_last/pallas_call | solution.py:241
  (36 shorter events, 1.4 us)
Async XLA Ops:
  0.6 0.7 copy-start.6
  0.6 0.7 copy-start.10
  0.7 0.7 copy-start.9
  0.7 0.7 copy-start.8
  0.7 0.7 copy-start.11
  0.7 0.7 copy-start.12
  1.4 1.0 %copy-start.2 = (bf16[2,512,128]{2,1,0:T(8,128)(2,1)S(1)}, bf16[2,512,128]{2,1,0:T(8,128)(2,1)}, u32[]{:S(2)}) copy-start(bf16[2,512,128]{2,1,0:T(8,128)(2,1)} %wave_ref.3) | copy-start | bytes 786436
  2.3 10.9 %copy-start.3 = (bf16[2,512,128]{2,1,0:T(8,128)(2,1)S(1)}, bf16[2,512,128]{2,1,0:T(8,128)(2,1)}, u32[]{:S(2)}) copy-start(bf16[2,512,128]{2,1,0:T(8,128)(2,1)} %wave_ref.3) | copy-start | bytes 786436
  4.4 10.9 %collective-permute-start = (bf16[512,256]{1,0:T(8,128)(2,1)S(1)}, bf16[512,256]{1,0:T(8,128)(2,1)S(1)}, u32[]{:S(2)}, u32[]{:S(2)}) collective-permute-start(bf16[512,256]{1,0:T(8,128)(2,1)S(1)} %get-tuple-element.18), channel_id=1, source_target_pairs={{0,16},{16,0},{1,17},{17,1},{2,18},{18,2},{3,19},{19,3},{4,20},{20... | collective-permute-start | bytes 786440 | tf_op jit(solution)/shard_map/ppermute | solution.py:259
  16.0 7.4 %copy-start.19 = (f32[128]{0:T(128)S(1)}, f32[128]{0:T(128)}, u32[]{:S(2)}) copy-start(f32[128]{0:T(128)} %param.19) | copy-start | bytes 1540
  16.1 20.3 %all-to-all-start = ((bf16[16,32,256]{2,1,0:T(8,128)(2,1)}), bf16[16,32,256]{2,1,0:T(8,128)(2,1)S(1)}, u32[]{:S(2)}, u32[]{:S(2)}) async-start(bf16[16,32,256]{2,1,0:T(8,128)(2,1)} %bitcast.5), calls=%async_computation | async-start | bytes 524288 | tf_op jit(solution)/shard_map/all_to_all | solution.py:262
  24.0 22.3 %copy-start.4 = (f32[4,64,64]{2,1,0:T(8,128)S(1)}, f32[4,64,64]{2,1,0:T(8,128)}, u32[]{:S(2)}) copy-start(f32[4,64,64]{2,1,0:T(8,128)} %coupling_ref.1) | copy-start | bytes 196612
  36.4 0.7 copy-start.14
  39.2 7.1 %copy-start.17 = (f32[4,8,8]{2,1,0:T(8,128)S(1)}, f32[4,8,8]{2,1,0:T(8,128)}, u32[]{:S(2)}) copy-start(f32[4,8,8]{2,1,0:T(8,128)} %param.17) | copy-start | bytes 3076
  39.2 14.4 %all-to-all-start.1 = ((f32[16,2,128]{2,1,0:T(2,128)}), f32[16,2,128]{2,1,0:T(2,128)S(1)}, u32[]{:S(2)}, u32[]{:S(2)}) async-start(f32[16,2,128]{2,1,0:T(2,128)} %get-tuple-element.19), calls=%async_computation.1 | async-start | bytes 32768 | tf_op jit(solution)/shard_map/all_to_all | solution.py:268
  47.5 1.0 %copy-start = (bf16[512,1024]{1,0:T(8,128)(2,1)}, bf16[512,1024]{1,0:T(8,128)(2,1)S(1)}, u32[]{:S(2)}) copy-start(bf16[512,1024]{1,0:T(8,128)(2,1)S(1)} %get-tuple-element.24.table_ref) | copy-start | bytes 3145732
  48.5 1.0 %copy-start.1 = (bf16[512,1024]{1,0:T(8,128)(2,1)}, bf16[512,1024]{1,0:T(8,128)(2,1)S(1)}, u32[]{:S(2)}) copy-start(bf16[512,1024]{1,0:T(8,128)(2,1)S(1)} %get-tuple-element.16.table_ref) | copy-start | bytes 3145732
  49.5 0.6 copy-start.5
  50.1 0.6 copy-start.7
  53.6 0.6 copy-start.16
  71.4 6.5 %copy-start.13 = (bf16[16,32,256]{2,1,0:T(8,128)(2,1)}, bf16[16,32,256]{2,1,0:T(8,128)(2,1)S(1)}, u32[]{:S(2)}) copy-start(bf16[16,32,256]{2,1,0:T(8,128)(2,1)S(1)} %all_to_all.15) | copy-start | bytes 786436
  71.4 5.8 %copy-start.18 = (f32[4,64]{1,0:T(4,128)S(1)}, f32[4,64]{1,0:T(4,128)}, u32[]{:S(2)}) copy-start(f32[4,64]{1,0:T(4,128)} %get-tuple-element.25) | copy-start | bytes 3076
  71.4 9.0 %collective-permute-start.1 = (bf16[512,256]{1,0:T(8,128)(2,1)S(1)}, bf16[512,256]{1,0:T(8,128)(2,1)S(1)}, u32[]{:S(2)}, u32[]{:S(2)}) collective-permute-start(bf16[512,256]{1,0:T(8,128)(2,1)S(1)} %bitcast.13), channel_id=1, source_target_pairs={{0,16},{16,0},{1,17},{17,1},{2,18},{18,2},{3,19},{19,3},{4,20},{20... | collective-permute-start | bytes 786440 | tf_op jit(solution)/shard_map/ppermute | solution.py:271
  80.4 0.7 copy-start.15

commit v2 on v1

--- a/solution.py
+++ b/solution.py
@@ -1,3 +1,4 @@
+import functools
 import math
 
 import jax
@@ -16,7 +17,11 @@
 COS = (1.0, -19.73920440673828, 64.93911743164062, -85.45014190673828,
        60.16762924194336, -25.967599868774414, 6.528658390045166)
 NT = (((1,), (1,)), ((), ()))
+TN = (((0,), (0,)), ((), ()))
 NN = (((1,), (0,)), ((), ()))
+
+
+LIMIT = pltpu.CompilerParams(vmem_limit_bytes=16 << 20)
 
 
 def dot_high(left, right, dims):
@@ -42,8 +47,10 @@
     return pl.BlockSpec(memory_space=pltpu.SMEM)
 
 
-def tables_kernel(core_ref, recip_ref, widths_ref, wave_ref, miller_ref, frac_ref, species_ref,
-                  order_ref, beta_ref, proj_ref, rhs_ref):
+def tables_kernel(core_ref, recip_ref, widths_ref, wave_hbm, miller_ref, frac_ref, species_ref,
+                  order_ref, beta_ref, proj_ref, wave_ref, rhs_ref, copied):
+    load = pltpu.make_async_copy(wave_hbm, wave_ref, copied)
+    load.start()
     core = core_ref[0]
     gcount = miller_ref.shape[1]
     natoms = order_ref.shape[1]
@@ -102,6 +109,7 @@
         beta_ref[q * 32:q * 32 + 32, 0:gcount] = jnp.concatenate(re, axis=0).astype(BF16)
         beta_ref[q * 32:q * 32 + 32, gcount:] = jnp.concatenate(im, axis=0).astype(BF16)
 
+    load.wait()
     nb = wave_ref.shape[2]
     real, imag = wave_ref[0], wave_ref[1]
     rhs_ref[0:gcount, 0:nb] = real
@@ -111,47 +119,46 @@
     proj_ref[...] = jnp.dot(beta_ref[...], rhs_ref[...], preferred_element_type=F32).astype(proj_ref.dtype)
 
 
-def tables(core, kind, wavefunctions, miller, reciprocal, fractional, species, atom_order, radial_widths):
-    gcount, nb = wavefunctions.shape[1:]
-    nrows = atom_order.shape[1] * 4
-    return pl.pallas_call(
-        tables_kernel,
-        out_shape=(jax.ShapeDtypeStruct((nrows, 2 * gcount), BF16), jax.ShapeDtypeStruct((nrows, 2 * nb), kind)),
-        in_specs=[smem(), smem(), smem()] + [vmem()] * 5,
-        out_specs=(vmem(), vmem()),
-        scratch_shapes=[pltpu.VMEM((2 * gcount, 2 * nb), BF16)],
-        compiler_params=pltpu.CompilerParams(vmem_limit_bytes=32 << 20),
-        name="tables",
-    )(core, reciprocal, radial_widths, wavefunctions, miller, fractional, species, atom_order)
-
-
-def prepare_kernel(owner_ref, species_ref, order_ref, mine_ref, other_ref, coupling_ref, base_ref,
-                   mine_t_ref, other_t_ref, couple_ref, base_rows_ref):
-    for src, dst in ((mine_ref, mine_t_ref), (other_ref, other_t_ref)):
-        nrows, width = src.shape[0], src.shape[1] // 2
-        for part in range(2):
-            block = src[:, part * width:(part + 1) * width]
-            dst[:, part * nrows:(part + 1) * nrows] = block.T
+def own_tables_kernel(bands, core_ref, recip_ref, widths_ref, wave_hbm, miller_ref, frac_ref, species_ref,
+                      order_ref, owner_ref, species_smem, order_smem, coupling_ref, base_ref, occupations_ref,
+                      beta_ref, proj_ref, couple_ref, base_rows_ref, weights_ref, wave_ref, rhs_ref, copied):
+    tables_kernel(core_ref, recip_ref, widths_ref, wave_hbm, miller_ref, frac_ref, species_ref, order_ref,
+                  beta_ref, proj_ref, wave_ref, rhs_ref, copied)
     row = iota((32, 64), 0) % 4
     base = jnp.zeros((32, 64), F32)
     for a in range(4):
-        s = species_ref[order_ref[owner_ref[0] * 4 + a]]
+        s = species_smem[order_smem[owner_ref[0] * 4 + a]]
         couple_ref[:, a * 64:(a + 1) * 64] = coupling_ref[s]
         base = jnp.where(row == a, base_ref[pl.ds(s, 1), :], base)
     base_rows_ref[...] = base
-
-
-def prepare(owner, species, atom_order, mine, other, coupling, base):
-    nrows, width = mine.shape
-    turned = jax.ShapeDtypeStruct((width // 2, 2 * nrows), BF16)
-    return pl.pallas_call(
-        prepare_kernel,
-        out_shape=(turned, turned, jax.ShapeDtypeStruct((64, 256), F32), jax.ShapeDtypeStruct((32, 64), F32)),
-        in_specs=[smem(), smem(), smem()] + [vmem()] * 4,
-        out_specs=(vmem(),) * 4,
-        compiler_params=pltpu.CompilerParams(vmem_limit_bytes=32 << 20),
-        name="prepare",
-    )(owner, species, atom_order, mine, other, coupling, base)
+    w = occupations_ref[...] * (1.0 / (occupations_ref.shape[1] * bands))
+    weights_ref[...] = jnp.concatenate([w, w], axis=1)
+
+
+def tables(core, wavefunctions, miller, reciprocal, fractional, species, atom_order, radial_widths, own=None):
+    gcount, nb = wavefunctions.shape[1:]
+    nrows = atom_order.shape[0] * 4
+    kind = BF16 if own is None else F32
+    body, more, more_specs = tables_kernel, (), []
+    outs = [jax.ShapeDtypeStruct((nrows, 2 * gcount), BF16), jax.ShapeDtypeStruct((nrows, 2 * nb), kind)]
+    if own is not None:
+        bands, owner, coupling, base, occupations = own
+        body = functools.partial(own_tables_kernel, bands)
+        more = (owner, species, atom_order, coupling, base, occupations)
+        more_specs = [smem()] * 3 + [vmem()] * 3
+        outs += [jax.ShapeDtypeStruct((64, 256), F32), jax.ShapeDtypeStruct((32, 64), F32),
+                 jax.ShapeDtypeStruct((1, 2 * nb), F32)]
+    return pl.pallas_call(
+        body,
+        out_shape=tuple(outs),
+        in_specs=[smem()] * 3 + [pl.BlockSpec(memory_space=pltpu.HBM)] + [vmem()] * 4 + more_specs,
+        out_specs=(vmem(),) * len(outs),
+        scratch_shapes=[pltpu.VMEM((2, gcount, nb), BF16), pltpu.VMEM((2 * gcount, 2 * nb), BF16),
+                        pltpu.SemaphoreType.DMA],
+        compiler_params=LIMIT,
+        name="tables" if own is None else "own_tables",
+    )(core, reciprocal, radial_widths, pltpu.with_memory_space_constraint(wavefunctions, pltpu.HBM), miller,
+      fractional, species.reshape(1, -1), atom_order.reshape(1, -1), *more)
 
 
 def occupancy_kernel(parts_ref, weights_ref, proj_ref, send_ref):
@@ -159,8 +166,7 @@
     for k in range(1, parts_ref.shape[0]):
         total = total + parts_ref[k].astype(F32)
     proj_ref[...] = total
-    w = weights_ref[...]
-    gram = dot_high(total * jnp.concatenate([w, w], axis=1), total, NT)
+    gram = dot_high(total * weights_ref[...], total, NT)
     gram = jnp.where(iota((32, 32), 0) % 4 == iota((32, 32), 1) % 4, gram, 0.0)
     lane = iota((32, 128), 1)
     spread = (iota((32, 128), 0) // 4 == lane % 8).astype(F32)
@@ -180,6 +186,7 @@
         out_shape=(jax.ShapeDtypeStruct((nrows, width), F32), jax.ShapeDtypeStruct((peers, 2, 128), F32)),
         in_specs=[vmem(), vmem()],
         out_specs=(vmem(), vmem()),
+        compiler_params=LIMIT,
         name="occupancy",
     )(parts, weights)
 
@@ -190,10 +197,13 @@
     lane = iota((32, 256), 1)
     by_atom = jnp.where(lane // 64 == iota((32, 256), 0) % 4, flat, 0.0)
     onsite = dot_high(by_atom, couple_ref[...], NT) + base_ref[...]
-    onsite_ref[...] = onsite[0:4, :]
     row = iota((32, 64), 0)
     onsite = jnp.where(iota((32, 64), 1) // 8 == row // 4, onsite, 0.0)
     spread = (iota((64, 32), 0) % 8 == iota((64, 32), 1) // 4).astype(F32)
+    fold = (iota((64, 8), 0) % 8 == iota((64, 8), 1)).astype(F32)
+    square = dot_high(onsite, fold, NN)
+    for i in range(8):
+        onsite_ref[:, i, :] = square[i * 4:i * 4 + 4, :]
     full = dot_high(onsite, spread, NN)
     full = jnp.where(iota((32, 32), 0) % 4 == iota((32, 32), 1) % 4, full, 0.0)
     weighted = dot_high(full, proj_ref[...], NN).astype(BF16)
@@ -204,19 +214,21 @@
 def weigh(parts, proj, couple, base_rows, peers):
     return pl.pallas_call(
         weigh_kernel,
-        out_shape=(jax.ShapeDtypeStruct((4, 64), F32), jax.ShapeDtypeStruct((peers, *proj.shape), BF16)),
+        out_shape=(jax.ShapeDtypeStruct((4, 8, 8), F32), jax.ShapeDtypeStruct((peers, *proj.shape), BF16)),
         in_specs=[vmem()] * 4,
         out_specs=(vmem(), vmem()),
+        compiler_params=LIMIT,
         name="weigh",
     )(parts, proj, couple, base_rows)
 
 
 def product_with(table_ref, weighted_ref):
-    nrows, width = weighted_ref.shape
+    width = weighted_ref.shape[1]
+    gcount = table_ref.shape[1] // 2
     real, imag = weighted_ref[:, :width // 2], weighted_ref[:, width // 2:]
     turned = jnp.concatenate([-imag, real], axis=1)
-    return (jnp.dot(table_ref[:, :nrows], weighted_ref[...], preferred_element_type=F32)
-            + jnp.dot(table_ref[:, nrows:], turned, preferred_element_type=F32))
+    return (lax.dot_general(weighted_ref[...], table_ref[:, :gcount], TN, preferred_element_type=F32)
+            + lax.dot_general(turned, table_ref[:, gcount:], TN, preferred_element_type=F32))
 
 
 def back_kernel(table_ref, weighted_ref, out_ref):
@@ -225,23 +237,23 @@
 
 def back_last_kernel(table_ref, weighted_ref, before_ref, out_ref):
     total = before_ref[...] + product_with(table_ref, weighted_ref)
-    half = total.shape[1] // 2
-    out_ref[0] = total[:, :half].astype(BF16)
-    out_ref[1] = total[:, half:].astype(BF16)
+    half = total.shape[0] // 2
+    out_ref[0] = total[:half].T.astype(BF16)
+    out_ref[1] = total[half:].T.astype(BF16)
 
 
 def back_project(table, weighted, before=None):
-    gcount, width = table.shape[0], weighted.shape[1]
+    gcount, width = table.shape[1] // 2, weighted.shape[1]
     if before is None:
         return pl.pallas_call(
             back_kernel,
-            out_shape=jax.ShapeDtypeStruct((gcount, width), F32),
-            in_specs=[vmem()] * 2, out_specs=vmem(), name="back",
+            out_shape=jax.ShapeDtypeStruct((width, gcount), F32),
+            in_specs=[vmem()] * 2, out_specs=vmem(), compiler_params=LIMIT, name="back",
         )(table, weighted)
     return pl.pallas_call(
         back_last_kernel,
         out_shape=jax.ShapeDtypeStruct((2, gcount, width // 2), BF16),
-        in_specs=[vmem()] * 3, out_specs=vmem(), name="back_last",
+        in_specs=[vmem()] * 3, out_specs=vmem(), compiler_params=LIMIT, name="back_last",
     )(table, weighted, before)
 
 
@@ -253,25 +265,22 @@
     owner = lax.axis_index("chip") * 2 + core
     swap = [(0, 1), (1, 0)]
     nb = wavefunctions.shape[2]
-    args = (wavefunctions, miller, reciprocal, fractional, species.reshape(1, -1), atom_order.reshape(1, -1),
-            radial_widths)
-    other, other_proj = tables((1 - core).reshape(1), BF16, *args)
+    args = (wavefunctions, miller, reciprocal, fractional, species, atom_order, radial_widths)
+    other, other_proj = tables((1 - core).reshape(1), *args)
     received = lax.ppermute(other_proj, "core", swap)
-    mine, mine_proj = tables(core.reshape(1), F32, *args)
+    own = (bands, owner.reshape(1), coupling, onsite_base.reshape(-1, 64), occupations.reshape(1, -1))
+    mine, mine_proj, couple, base_rows, weights = tables(core.reshape(1), *args, own=own)
     chip_sum = (mine_proj + received.astype(F32)).astype(BF16).reshape(chips, -1, 2 * nb)
     parts = lax.all_to_all(chip_sum, "chip", 0, 0, tiled=True)
-    mine_t, other_t, couple, base_rows = prepare(
-        owner.reshape(1), species, atom_order, mine, other, coupling, onsite_base.reshape(-1, 64))
-
-    weights = (occupations / (nb * bands)).reshape(1, -1)
+
     proj, occupancy = occupancy_step(parts, weights, bands)
     occupancy = lax.all_to_all(occupancy, "band", 0, 0, tiled=True)
     onsite, weighted = weigh(occupancy, proj, couple, base_rows, chips)
     weighted = lax.all_to_all(weighted, "chip", 0, 0, tiled=True).reshape(-1, 2 * nb)
     other_weighted = lax.ppermute(weighted, "core", swap)
-    applied = back_project(mine_t, weighted)
-    applied = back_project(other_t, other_weighted, applied)
-    return applied, onsite.reshape(-1, 8, 8)
+    applied = back_project(mine, weighted)
+    applied = back_project(other, other_weighted, applied)
+    return applied, onsite
 
 
 def solution(mesh):

time: 84.4 us -> 74.2 us (0.88)
  blocking collectives: 15.1 us -> 48.9 us
  starting transfers between devices: 29 us -> 14.2 us
  waiting for transfers between devices: 15.2 us -> 0.67 us
  Pallas kernels: 14.7 us -> 7.76 us
  local copies, waits for them, and re-layouts: 7.59 us -> 1.42 us
  other arithmetic: 1.36 us -> 0.06 us
    all_to_all x0 -> x2, blocking collectives: none -> 34.1 us  [the longest x1 20 us: local(): parts = lax.all_to_all(chip_sum, 'chip', 0, 0, tiled=True)]
    all_to_all x2 -> x0, waiting for transfers between devices: 15.2 us -> none  [the longest x1 12.4 us: local(): parts = lax.all_to_all(chip_sum, 'chip', 0, 0, tiled=True)]
    all_to_all x2 -> x0, starting transfers between devices: 14.4 us -> none  [the longest x1 7.36 us: local(): parts = lax.all_to_all(chip_sum, 'chip', 0, 0, tiled=True)]
    unnamed x40 -> x18, local copies, waits for them, and re-layouts: 6.83 us -> 1.34 us
    pallas_call x5 -> x4, Pallas kernels: 10 us -> 6.01 us  [the longest x2 4.55 us: tables(): pl.pallas_call(body, out_shape=tuple(outs), in_specs=[smem()] * 3 + [pl.B...]
    pallas_call x1, Pallas kernels: 2.07 us -> 0.5 us  [occupancy_step(): pl.pallas_call(occupancy_kernel, out_shape=(jax.ShapeDtypeStruct((nrows,...]
    pallas_call x1, Pallas kernels: 2.59 us -> 1.25 us  [back_project(): pl.pallas_call(back_last_kernel, out_shape=jax.ShapeDtypeStruct((2, gcoun...]
  transfers between devices with their start and end apart: 4 -> 2, of which waited for: 2 -> 1; matrix products, arithmetic and copies ran while one was open for 2% -> 0% of each run, Pallas kernels for 7% -> 4%
where the time goes in v2:
time: 74.2 us; the launch traced here: 73.8 us
  blocking collectives  48.9 us (66%)
  starting transfers between devices  14.2 us (19%)
  Pallas kernels  7.76 us (10%)
  local copies, waits for them, and re-layouts  1.42 us (2%)
  between operations  0.77 us (1%)
    all_to_all x1, blocking collectives, local(): parts = lax.all_to_all(chip_sum, 'chip', 0, 0, tiled=True)  20 us
    all_to_all x1, blocking collectives, local(): lax.all_to_all(weighted, 'chip', 0, 0, tiled=True).reshape(-1, 2 * nb)  14.9 us
    all_to_all x1, blocking collectives, local(): occupancy = lax.all_to_all(occupancy, 'band', 0, 0, tiled=True)  14.1 us
    ppermute x1, starting transfers between devices, local(): received = lax.ppermute(other_proj, 'core', swap)  8.79 us
    ppermute x1, starting transfers between devices, local(): other_weighted = lax.ppermute(weighted, 'core', swap)  5.43 us
    pallas_call x2, Pallas kernels, tables(): pl.pallas_call(body, out_shape=tuple(outs), in_specs=[smem()] * 3 + [pl.B...  4.55 us
  transfers between devices with their start and end apart: 2, of which 1 were waited for; matrix products, arithmetic and copies ran while one was open for 0% of the time, Pallas kernels for 4%

profile of v2, /device:TPU:1, one launch (start us, length us, event | category | flops | bytes accessed | tf_op | source)
XLA Modules:
  0.0 73.8 jit_solution(1402660922242129246)
XLA Ops:
  0.6 0.0 copy-start.1
  0.6 0.0 copy-start.4
  0.7 0.0 copy-start.3
  0.7 0.0 copy-start.2
  0.7 0.6 copy-done.1
  1.3 0.0 copy-done.3
  1.3 0.0 copy-done.2
  1.4 0.0 copy-done.5
  1.4 2.3 %tables.1 = (bf16[512,1024]{1,0:T(8,128)(2,1)S(1)}, bf16[512,256]{1,0:T(8,128)(2,1)S(1)}) custom-call(s32[1]{0:T(128)} %bitcast.core_ref, f32[3,3]{1,0:T(4,128)S(1)} %copy-done.2, f32[4,4]{1,0:T(4,128)S(1)} %copy-done.3, bf16[2,512,128]{2,1,0:T(8,128)(2,1)} %wave_hbm.3, s32[3,512]{1,0:T(4,128)S(1)} %copy-done.1, f32[3,128]{1,0:T(4,128)S(1)} %copy-done.4, ...), custom_call_target="tpu_custom_call" | custom-call | tf_op jit(solution)/shard_map/tables/pallas_call | solution.py:151
  3.7 8.8 %collective-permute-start = (bf16[512,256]{1,0:T(8,128)(2,1)S(1)}, bf16[512,256]{1,0:T(8,128)(2,1)S(1)}, u32[]{:S(2)}, u32[]{:S(2)}) collective-permute-start(bf16[512,256]{1,0:T(8,128)(2,1)S(1)} %get-tuple-element.15), channel_id=1, source_target_pairs={{0,16},{16,0},{1,17},{17,1},{2,18},{18,2},{3,19},{19,3},{4,20},{20... | collective-permute-start | bytes 786440 | tf_op jit(solution)/shard_map/ppermute | solution.py:270
  12.5 0.1 reshape.38.base_ref
  12.6 0.7 copy-done.7
  13.3 2.2 %own_tables.1 = (bf16[512,1024]{1,0:T(8,128)(2,1)S(1)}, f32[512,256]{1,0:T(8,128)S(1)}, f32[64,256]{1,0:T(8,128)S(1)}, f32[32,64]{1,0:T(8,128)S(1)}, f32[1,256]{1,0:T(1,128)S(1)}) custom-call(s32[1]{0:T(128)} %bitcast.3.core_ref, f32[3,3]{1,0:T(4,128)S(1)} %copy-done.2, f32[4,4]{1,0:T(4,128)S(1)} %copy-done.3, bf16[2,512,128]{2,1,0:T(8,128)(2,1)} %wave_hbm.3, ...), custom_call_target="tpu_custom_call" | custom-call | tf_op jit(solution)/shard_map/own_tables/pallas_call | solution.py:151
  15.5 0.0 collective-permute-done
  15.5 0.1 add_convert_fusion
  15.6 20.0 %all_to_all.15.parts_ref = bf16[16,32,256]{2,1,0:T(8,128)(2,1)S(1)} all-to-all(bf16[16,32,256]{2,1,0:T(8,128)(2,1)S(1)} %bitcast.15), channel_id=1, replica_groups=mesh['chip'=16,'core'=2,'band'=16] {'chip'}, dimensions={0} | all-to-all | bytes 524288 | tf_op jit(solution)/shard_map/all_to_all | solution.py:274
  35.6 0.5 occupancy.1
  36.1 14.1 %all_to_all.16.parts_ref = f32[16,2,128]{2,1,0:T(2,128)S(1)} all-to-all(f32[16,2,128]{2,1,0:T(2,128)S(1)} %get-tuple-element.17), channel_id=1, replica_groups=mesh['chip'=16,'core'=2,'band'=16] {'band'}, dimensions={0} | all-to-all | bytes 32768 | tf_op jit(solution)/shard_map/all_to_all | solution.py:277
  50.1 1.0 %weigh.1 = (f32[4,8,8]{2,1,0:T(8,128)}, bf16[16,32,256]{2,1,0:T(8,128)(2,1)S(1)}) custom-call(f32[16,2,128]{2,1,0:T(2,128)S(1)} %all_to_all.16.parts_ref, f32[32,256]{1,0:T(8,128)S(1)} %get-tuple-element.18.proj_ref, f32[64,256]{1,0:T(8,128)S(1)} %get-tuple-element.19.couple_ref, f32[32,64]{1,0:T(8,128)S(1)} %get-tuple-element.20.base_ref), custom_call_target="tpu_custom_call" | custom-call | tf_op jit(solution)/shard_map/weigh/pallas_call | solution.py:215
  51.1 14.9 %all_to_all.17 = bf16[16,32,256]{2,1,0:T(8,128)(2,1)S(1)} all-to-all(bf16[16,32,256]{2,1,0:T(8,128)(2,1)S(1)} %get-tuple-element.21), channel_id=1, replica_groups=mesh['chip'=16,'core'=2,'band'=16] {'chip'}, dimensions={0} | all-to-all | bytes 524288 | tf_op jit(solution)/shard_map/all_to_all | solution.py:279
  66.0 5.4 %collective-permute-start.1 = (bf16[512,256]{1,0:T(8,128)(2,1)S(1)}, bf16[512,256]{1,0:T(8,128)(2,1)S(1)}, u32[]{:S(2)}, u32[]{:S(2)}) collective-permute-start(bf16[512,256]{1,0:T(8,128)(2,1)S(1)} %bitcast.8), channel_id=1, source_target_pairs={{0,16},{16,0},{1,17},{17,1},{2,18},{18,2},{3,19},{19,3},{4,20},{20... | collective-permute-start | bytes 786440 | tf_op jit(solution)/shard_map/ppermute | solution.py:280
  71.4 0.5 back.1.before_ref
  71.9 0.7 collective-permute-done.1.weighted_ref
  72.6 1.2 %back_last.1 = bf16[2,512,128]{2,1,0:T(8,128)(2,1)} custom-call(bf16[512,1024]{1,0:T(8,128)(2,1)S(1)} %get-tuple-element.13.table_ref, bf16[512,256]{1,0:T(8,128)(2,1)S(1)} %collective-permute-done.1.weighted_ref, f32[256,512]{1,0:T(8,128)S(1)} %back.1.before_ref), custom_call_target="tpu_custom_call" | custom-call | tf_op jit(solution)/shard_map/back_last/pallas_call | solution.py:253
  (9 shorter events, 0.0 us)
Async XLA Ops:
  0.6 0.7 copy-start.1
  0.6 0.7 copy-start.4
  0.7 0.7 copy-start.3
  0.7 0.7 copy-start.2
  0.7 0.7 copy-start.5
  0.7 0.7 copy-start.6
  1.4 11.2 %copy-start.8 = (f32[4,8,8]{2,1,0:T(8,128)S(1)}, f32[4,8,8]{2,1,0:T(8,128)}, u32[]{:S(2)}) copy-start(f32[4,8,8]{2,1,0:T(8,128)} %param.17) | copy-start | bytes 3076
  1.4 11.2 %copy-start = (f32[4,64,64]{2,1,0:T(8,128)S(1)}, f32[4,64,64]{2,1,0:T(8,128)}, u32[]{:S(2)}) copy-start(f32[4,64,64]{2,1,0:T(8,128)} %coupling_ref.1) | copy-start | bytes 196612
  3.7 11.8 %collective-permute-start = (bf16[512,256]{1,0:T(8,128)(2,1)S(1)}, bf16[512,256]{1,0:T(8,128)(2,1)S(1)}, u32[]{:S(2)}, u32[]{:S(2)}) collective-permute-start(bf16[512,256]{1,0:T(8,128)(2,1)S(1)} %get-tuple-element.15), channel_id=1, source_target_pairs={{0,16},{16,0},{1,17},{17,1},{2,18},{18,2},{3,19},{19,3},{4,20},{20... | collective-permute-start | bytes 786440 | tf_op jit(solution)/shard_map/ppermute | solution.py:270
  12.6 0.7 copy-start.7
  66.0 6.6 %collective-permute-start.1 = (bf16[512,256]{1,0:T(8,128)(2,1)S(1)}, bf16[512,256]{1,0:T(8,128)(2,1)S(1)}, u32[]{:S(2)}, u32[]{:S(2)}) collective-permute-start(bf16[512,256]{1,0:T(8,128)(2,1)S(1)} %bitcast.8), channel_id=1, source_target_pairs={{0,16},{16,0},{1,17},{17,1},{2,18},{18,2},{3,19},{19,3},{4,20},{20... | collective-permute-start | bytes 786440 | tf_op jit(solution)/shard_map/ppermute | solution.py:280

commit v3 on v2

--- a/solution.py
+++ b/solution.py
@@ -43,49 +43,30 @@
     return pl.BlockSpec(memory_space=pltpu.VMEM)
 
 
-def smem():
-    return pl.BlockSpec(memory_space=pltpu.SMEM)
-
-
-def tables_kernel(core_ref, recip_ref, widths_ref, wave_hbm, miller_ref, frac_ref, species_ref,
-                  order_ref, beta_ref, proj_ref, wave_ref, rhs_ref, copied):
-    load = pltpu.make_async_copy(wave_hbm, wave_ref, copied)
-    load.start()
-    core = core_ref[0]
-    gcount = miller_ref.shape[1]
-    natoms = order_ref.shape[1]
-    owners = beta_ref.shape[0] // 32
-    kinds = widths_ref.shape[0]
-    spec = species_ref[...]
-    rows = [frac_ref[d:d + 1, :] for d in range(3)]
-    for c in range(4):
-        row = jnp.zeros((1, natoms), F32)
-        for s in range(kinds):
-            row = jnp.where(spec == s, widths_ref[s, c], row)
-        rows.append(row)
-    rows.append(jnp.zeros((1, natoms), F32))
-    by_atom = jnp.concatenate(rows, axis=0)
-    pick = (iota((natoms, natoms), 0) == order_ref[...]).astype(F32)
-    by_slot = dot_high(by_atom, pick, NN)
-    row_id = iota((owners * 8, natoms), 0)
-    slot = (row_id // 8) * 8 + core * 4 + row_id % 4
-    expand = (iota((owners * 8, natoms), 1) == slot).astype(F32)
-    by_row = dot_high(expand, by_slot, NT)
-
-    mil = miller_ref[...].astype(F32)
-    m = [mil[d:d + 1, :] for d in range(3)]
-    two_pi = 2.0 * math.pi
-    g = [two_pi * (recip_ref[d, 0] * m[0] + recip_ref[d, 1] * m[1] + recip_ref[d, 2] * m[2]) for d in range(3)]
-    g2 = g[0] * g[0] + g[1] * g[1] + g[2] * g[2]
+def hbm():
+    return pl.BlockSpec(memory_space=pltpu.HBM)
+
+
+def in_hbm(array):
+    return pltpu.with_memory_space_constraint(array, pltpu.HBM)
+
+
+def fetch(pairs, copied):
+    copies = [pltpu.make_async_copy(src, dst, copied.at[k]) for k, (src, dst) in enumerate(pairs)]
+    for copy in copies:
+        copy.start()
+    return copies
+
+
+def project_rows(by_row, grid_ref, rhs_ref, beta_ref, proj_ref):
+    gcount = grid_ref.shape[1]
     wide = (8, gcount)
-    m = [jnp.broadcast_to(a, wide) for a in m]
-    g2 = jnp.broadcast_to(g2, wide)
-    g = [jnp.broadcast_to(a, wide) for a in g]
+    m, g = ([jnp.broadcast_to(grid_ref[d:d + 1, :], wide) for d in dims] for dims in ((0, 1, 2), (3, 4, 5)))
+    g2 = jnp.broadcast_to(grid_ref[6:7, :], wide)
     first = iota(wide, 0) < 4
     pair_g = (None, jnp.where(first, g[0], g[1]), jnp.where(first, g[2], g[0]), jnp.where(first, g[1], g[2]))
     first1 = iota((8, 1), 0) < 4
-
-    for q in range(owners):
+    for q in range(by_row.shape[0] // 8):
         par = by_row[q * 8:q * 8 + 8, :]
         col = [par[:, k:k + 1] for k in range(7)]
         turns = col[0] * m[0] + col[1] * m[1] + col[2] * m[2]
@@ -108,57 +89,111 @@
                 im.append(amp * cos)
         beta_ref[q * 32:q * 32 + 32, 0:gcount] = jnp.concatenate(re, axis=0).astype(BF16)
         beta_ref[q * 32:q * 32 + 32, gcount:] = jnp.concatenate(im, axis=0).astype(BF16)
-
-    load.wait()
+    proj_ref[...] = jnp.dot(beta_ref[...], rhs_ref[...], preferred_element_type=F32).astype(proj_ref.dtype)
+
+
+def other_tables_kernel(recip_hbm, widths_hbm, wave_hbm, miller_hbm, frac_hbm, species_hbm, order_hbm,
+                        beta_ref, proj_ref, own_row_ref, grid_ref, rhs_ref,
+                        recip_ref, widths_ref, wave_ref, miller_ref, frac_ref, species_ref, order_ref, copied):
+    loads = fetch(((wave_hbm, wave_ref), (recip_hbm, recip_ref), (widths_hbm, widths_ref), (miller_hbm, miller_ref),
+                   (frac_hbm, frac_ref), (species_hbm, species_ref), (order_hbm, order_ref)), copied)
+    for load in loads[1:]:
+        load.wait()
+    core = lax.axis_index("core")
+    gcount = miller_ref.shape[1]
+    natoms = order_ref.shape[1]
+    owners = natoms // 8
+    kinds = widths_ref.shape[0]
+    spec = species_ref[...]
+    rows = [frac_ref[d:d + 1, :] for d in range(3)]
+    for c in range(4):
+        row = jnp.zeros((1, natoms), F32)
+        for s in range(kinds):
+            row = jnp.where(spec == s, widths_ref[s:s + 1, c:c + 1], row)
+        rows.append(row)
+    rows.append(spec.astype(F32))
+    by_atom = jnp.concatenate(rows, axis=0)
+    pick = (iota((natoms, natoms), 0) == order_ref[...]).astype(F32)
+    by_slot = dot_high(by_atom, pick, NN)
+    row_id = iota((owners * 16, natoms), 0)
+    half = jnp.where(row_id < owners * 8, 1 - core, core)
+    slot = ((row_id // 8) % owners) * 8 + half * 4 + row_id % 4
+    expand = (iota((owners * 16, natoms), 1) == slot).astype(F32)
+    by_row = dot_high(expand, by_slot, NT)
+    own_row_ref[...] = by_row[owners * 8:, :]
+
+    mil = miller_ref[...].astype(F32)
+    m = [mil[d:d + 1, :] for d in range(3)]
+    two_pi = 2.0 * math.pi
+    g = [two_pi * (recip_ref[d:d + 1, 0:1] * m[0] + recip_ref[d:d + 1, 1:2] * m[1] + recip_ref[d:d + 1, 2:3] * m[2])
+         for d in range(3)]
+    g2 = g[0] * g[0] + g[1] * g[1] + g[2] * g[2]
+    grid_ref[...] = jnp.concatenate([*m, *g, g2, g2], axis=0)
+    loads[0].wait()
     nb = wave_ref.shape[2]
     real, imag = wave_ref[0], wave_ref[1]
     rhs_ref[0:gcount, 0:nb] = real
     rhs_ref[0:gcount, nb:] = imag
     rhs_ref[gcount:, 0:nb] = imag
     rhs_ref[gcount:, nb:] = -real
-    proj_ref[...] = jnp.dot(beta_ref[...], rhs_ref[...], preferred_element_type=F32).astype(proj_ref.dtype)
-
-
-def own_tables_kernel(bands, core_ref, recip_ref, widths_ref, wave_hbm, miller_ref, frac_ref, species_ref,
-                      order_ref, owner_ref, species_smem, order_smem, coupling_ref, base_ref, occupations_ref,
-                      beta_ref, proj_ref, couple_ref, base_rows_ref, weights_ref, wave_ref, rhs_ref, copied):
-    tables_kernel(core_ref, recip_ref, widths_ref, wave_hbm, miller_ref, frac_ref, species_ref, order_ref,
-                  beta_ref, proj_ref, wave_ref, rhs_ref, copied)
-    row = iota((32, 64), 0) % 4
-    base = jnp.zeros((32, 64), F32)
+    project_rows(by_row[:owners * 8, :], grid_ref, rhs_ref, beta_ref, proj_ref)
+
+
+def other_tables(wavefunctions, miller, reciprocal, fractional, species, atom_order, radial_widths):
+    gcount, nb = wavefunctions.shape[1:]
+    natoms = atom_order.shape[0]
+    args = (reciprocal, radial_widths, wavefunctions, miller, fractional, species.reshape(1, -1),
+            atom_order.reshape(1, -1))
+    return pl.pallas_call(
+        other_tables_kernel,
+        out_shape=(jax.ShapeDtypeStruct((natoms * 4, 2 * gcount), BF16),
+                   jax.ShapeDtypeStruct((natoms * 4, 2 * nb), BF16),
+                   jax.ShapeDtypeStruct((natoms, 8), F32), jax.ShapeDtypeStruct((8, gcount), F32),
+                   jax.ShapeDtypeStruct((2 * gcount, 2 * nb), BF16)),
+        in_specs=[hbm()] * len(args),
+        out_specs=(vmem(),) * 5,
+        scratch_shapes=[pltpu.VMEM(a.shape, a.dtype) for a in args] + [pltpu.SemaphoreType.DMA((len(args),))],
+        compiler_params=LIMIT,
+        name="other_tables",
+    )(*(in_hbm(a) for a in args))
+
+
+def own_tables_kernel(bands, own_row_ref, grid_ref, rhs_ref, base_ref, coupling_hbm, occupations_hbm,
+                      beta_ref, proj_ref, couple_ref, base_rows_ref, weights_ref,
+                      coupling_ref, occupations_ref, copied):
+    loads = fetch(((coupling_hbm, coupling_ref), (occupations_hbm, occupations_ref)), copied)
+    project_rows(own_row_ref[...], grid_ref, rhs_ref, beta_ref, proj_ref)
+    for load in loads:
+        load.wait()
+    spec = own_row_ref[pl.ds(pl.multiple_of(lax.axis_index("chip") * 8, 8), 8), 7:8]
+    kinds = base_ref.shape[0]
+    base = jnp.broadcast_to(base_ref[0:1, :], (8, 64))
+    for s in range(1, kinds):
+        base = jnp.where(spec == s, base_ref[s:s + 1, :], base)
+    base_rows_ref[...] = jnp.concatenate([base] * 4, axis=0)
     for a in range(4):
-        s = species_smem[order_smem[owner_ref[0] * 4 + a]]
-        couple_ref[:, a * 64:(a + 1) * 64] = coupling_ref[s]
-        base = jnp.where(row == a, base_ref[pl.ds(s, 1), :], base)
-    base_rows_ref[...] = base
+        block = coupling_ref[0]
+        for s in range(1, kinds):
+            block = jnp.where(spec[a:a + 1, :] == s, coupling_ref[s], block)
+        couple_ref[:, a * 64:(a + 1) * 64] = block
     w = occupations_ref[...] * (1.0 / (occupations_ref.shape[1] * bands))
     weights_ref[...] = jnp.concatenate([w, w], axis=1)
 
 
-def tables(core, wavefunctions, miller, reciprocal, fractional, species, atom_order, radial_widths, own=None):
-    gcount, nb = wavefunctions.shape[1:]
-    nrows = atom_order.shape[0] * 4
-    kind = BF16 if own is None else F32
-    body, more, more_specs = tables_kernel, (), []
-    outs = [jax.ShapeDtypeStruct((nrows, 2 * gcount), BF16), jax.ShapeDtypeStruct((nrows, 2 * nb), kind)]
-    if own is not None:
-        bands, owner, coupling, base, occupations = own
-        body = functools.partial(own_tables_kernel, bands)
-        more = (owner, species, atom_order, coupling, base, occupations)
-        more_specs = [smem()] * 3 + [vmem()] * 3
-        outs += [jax.ShapeDtypeStruct((64, 256), F32), jax.ShapeDtypeStruct((32, 64), F32),
-                 jax.ShapeDtypeStruct((1, 2 * nb), F32)]
-    return pl.pallas_call(
-        body,
-        out_shape=tuple(outs),
-        in_specs=[smem()] * 3 + [pl.BlockSpec(memory_space=pltpu.HBM)] + [vmem()] * 4 + more_specs,
-        out_specs=(vmem(),) * len(outs),
-        scratch_shapes=[pltpu.VMEM((2, gcount, nb), BF16), pltpu.VMEM((2 * gcount, 2 * nb), BF16),
-                        pltpu.SemaphoreType.DMA],
+def own_tables(bands, own_row, grid, rhs, base, coupling, occupations):
+    nrows = own_row.shape[0] * 4
+    return pl.pallas_call(
+        functools.partial(own_tables_kernel, bands),
+        out_shape=(jax.ShapeDtypeStruct((nrows, rhs.shape[0]), BF16), jax.ShapeDtypeStruct((nrows, rhs.shape[1]), F32),
+                   jax.ShapeDtypeStruct((64, 256), F32), jax.ShapeDtypeStruct((32, 64), F32),
+                   jax.ShapeDtypeStruct((1, rhs.shape[1]), F32)),
+        in_specs=[vmem()] * 4 + [hbm()] * 2,
+        out_specs=(vmem(),) * 5,
+        scratch_shapes=[pltpu.VMEM(coupling.shape, F32), pltpu.VMEM(occupations.shape, F32),
+                        pltpu.SemaphoreType.DMA((2,))],
         compiler_params=LIMIT,
-        name="tables" if own is None else "own_tables",
-    )(core, reciprocal, radial_widths, pltpu.with_memory_space_constraint(wavefunctions, pltpu.HBM), miller,
-      fractional, species.reshape(1, -1), atom_order.reshape(1, -1), *more)
+        name="own_tables",
+    )(own_row, grid, rhs, base, in_hbm(coupling), in_hbm(occupations))
 
 
 def occupancy_kernel(parts_ref, weights_ref, proj_ref, send_ref):
@@ -261,15 +296,13 @@
           onsite_base, coupling, occupations):
     chips = lax.axis_size("chip")
     bands = lax.axis_size("band")
-    core = lax.axis_index("core")
-    owner = lax.axis_index("chip") * 2 + core
     swap = [(0, 1), (1, 0)]
     nb = wavefunctions.shape[2]
-    args = (wavefunctions, miller, reciprocal, fractional, species, atom_order, radial_widths)
-    other, other_proj = tables((1 - core).reshape(1), *args)
+    other, other_proj, own_row, grid, rhs = other_tables(
+        wavefunctions, miller, reciprocal, fractional, species, atom_order, radial_widths)
     received = lax.ppermute(other_proj, "core", swap)
-    own = (bands, owner.reshape(1), coupling, onsite_base.reshape(-1, 64), occupations.reshape(1, -1))
-    mine, mine_proj, couple, base_rows, weights = tables(core.reshape(1), *args, own=own)
+    mine, mine_proj, couple, base_rows, weights = own_tables(
+        bands, own_row, grid, rhs, onsite_base.reshape(-1, 64), coupling, occupations.reshape(1, -1))
     chip_sum = (mine_proj + received.astype(F32)).astype(BF16).reshape(chips, -1, 2 * nb)
     parts = lax.all_to_all(chip_sum, "chip", 0, 0, tiled=True)
 

time: 74.2 us -> 71.7 us (0.966)
  local copies, waits for them, and re-layouts: 1.42 us -> 0.08 us
  Pallas kernels: 7.76 us -> 6.92 us
    unnamed x18 -> x2, local copies, waits for them, and re-layouts: 1.34 us -> 0.01 us
    pallas_call x2, Pallas kernels: 4.55 us -> 3.72 us  [the longest x1 2.52 us: other_tables(): pl.pallas_call(other_tables_kernel, out_shape=(jax.ShapeDtypeStruct((nato...]
  transfers between devices with their start and end apart: 2 -> 2, of which waited for: 1 -> 1; matrix products, arithmetic and copies ran while one was open for 0% -> 0% of each run, Pallas kernels for 4% -> 2%
where the time goes in v3:
time: 71.7 us; the launch traced here: 71.4 us
  blocking collectives  48.6 us (68%)
  starting transfers between devices  14.4 us (20%)
  Pallas kernels  6.92 us (10%)
    all_to_all x1, blocking collectives, local(): parts = lax.all_to_all(chip_sum, 'chip', 0, 0, tiled=True)  19.8 us
    all_to_all x1, blocking collectives, local(): lax.all_to_all(weighted, 'chip', 0, 0, tiled=True).reshape(-1, 2 * nb)  14.7 us
    all_to_all x1, blocking collectives, local(): occupancy = lax.all_to_all(occupancy, 'band', 0, 0, tiled=True)  14.1 us
    ppermute x1, starting transfers between devices, local(): received = lax.ppermute(other_proj, 'core', swap)  8.78 us
    ppermute x1, starting transfers between devices, local(): other_weighted = lax.ppermute(weighted, 'core', swap)  5.6 us
    pallas_call x1, Pallas kernels, other_tables(): pl.pallas_call(other_tables_kernel, out_shape=(jax.ShapeDtypeStruct((nato...  2.52 us
  transfers between devices with their start and end apart: 2, of which 1 were waited for; matrix products, arithmetic and copies ran while one was open for 0% of the time, Pallas kernels for 2%

profile of v3, /device:TPU:1, one launch (start us, length us, event | category | flops | bytes accessed | tf_op | source)
XLA Modules:
  0.0 71.4 jit_solution(3444976705602442029)
XLA Ops:
  0.6 0.0 copy-start
  0.6 2.5 %other_tables.1 = (bf16[512,1024]{1,0:T(8,128)(2,1)S(1)}, bf16[512,256]{1,0:T(8,128)(2,1)S(1)}, f32[128,8]{1,0:T(8,128)S(1)}, f32[8,512]{1,0:T(8,128)S(1)}, bf16[1024,256]{1,0:T(8,128)(2,1)S(1)}) custom-call(f32[3,3]{1,0:T(4,128)} %recip_hbm.1, f32[4,4]{1,0:T(4,128)} %widths_hbm.1, bf16[2,512,128]{2,1,0:T(8,128)(2,1)} %wave_hbm.1, s32[3,512]{1,0:T(4,128)} %miller_hbm.1, ...), custom_call_target="tpu_custom_call" | custom-call | tf_op jit(solution)/shard_map/other_tables/pallas_call | solution.py:147
  3.2 8.8 %collective-permute-start = (bf16[512,256]{1,0:T(8,128)(2,1)S(1)}, bf16[512,256]{1,0:T(8,128)(2,1)S(1)}, u32[]{:S(2)}, u32[]{:S(2)}) collective-permute-start(bf16[512,256]{1,0:T(8,128)(2,1)S(1)} %get-tuple-element.21), channel_id=1, source_target_pairs={{0,16},{16,0},{1,17},{17,1},{2,18},{18,2},{3,19},{19,3},{4,20},{20... | collective-permute-start | bytes 786440 | tf_op jit(solution)/shard_map/ppermute | solution.py:303
  12.0 0.0 copy-done
  12.0 0.1 reshape.24.base_ref
  12.1 1.2 %own_tables.1 = (bf16[512,1024]{1,0:T(8,128)(2,1)S(1)}, f32[512,256]{1,0:T(8,128)S(1)}, f32[64,256]{1,0:T(8,128)S(1)}, f32[32,64]{1,0:T(8,128)S(1)}, f32[1,256]{1,0:T(1,128)S(1)}) custom-call(f32[128,8]{1,0:T(8,128)S(1)} %get-tuple-element.17.own_row_ref, f32[8,512]{1,0:T(8,128)S(1)} %get-tuple-element.18.grid_ref, ...), custom_call_target="tpu_custom_call" | custom-call | tf_op jit(solution)/shard_map/own_tables/pallas_call | solution.py:185
  13.3 0.0 collective-permute-done
  13.3 0.1 add_convert_fusion
  13.3 19.8 %all_to_all.15.parts_ref = bf16[16,32,256]{2,1,0:T(8,128)(2,1)S(1)} all-to-all(bf16[16,32,256]{2,1,0:T(8,128)(2,1)S(1)} %bitcast.7), channel_id=1, replica_groups=mesh['chip'=16,'core'=2,'band'=16] {'chip'}, dimensions={0} | all-to-all | bytes 524288 | tf_op jit(solution)/shard_map/all_to_all | solution.py:307
  33.1 0.5 occupancy.1
  33.6 14.1 %all_to_all.16.parts_ref = f32[16,2,128]{2,1,0:T(2,128)S(1)} all-to-all(f32[16,2,128]{2,1,0:T(2,128)S(1)} %get-tuple-element.23), channel_id=1, replica_groups=mesh['chip'=16,'core'=2,'band'=16] {'band'}, dimensions={0} | all-to-all | bytes 32768 | tf_op jit(solution)/shard_map/all_to_all | solution.py:310
  47.7 1.0 %weigh.1 = (f32[4,8,8]{2,1,0:T(8,128)}, bf16[16,32,256]{2,1,0:T(8,128)(2,1)S(1)}) custom-call(f32[16,2,128]{2,1,0:T(2,128)S(1)} %all_to_all.16.parts_ref, f32[32,256]{1,0:T(8,128)S(1)} %get-tuple-element.24.proj_ref, f32[64,256]{1,0:T(8,128)S(1)} %get-tuple-element.25.couple_ref, f32[32,64]{1,0:T(8,128)S(1)} %get-tuple-element.26.base_ref), custom_call_target="tpu_custom_call" | custom-call | tf_op jit(solution)/shard_map/weigh/pallas_call | solution.py:250
  48.7 14.7 %all_to_all.17 = bf16[16,32,256]{2,1,0:T(8,128)(2,1)S(1)} all-to-all(bf16[16,32,256]{2,1,0:T(8,128)(2,1)S(1)} %get-tuple-element.27), channel_id=1, replica_groups=mesh['chip'=16,'core'=2,'band'=16] {'chip'}, dimensions={0} | all-to-all | bytes 524288 | tf_op jit(solution)/shard_map/all_to_all | solution.py:312
  63.4 5.6 %collective-permute-start.1 = (bf16[512,256]{1,0:T(8,128)(2,1)S(1)}, bf16[512,256]{1,0:T(8,128)(2,1)S(1)}, u32[]{:S(2)}, u32[]{:S(2)}) collective-permute-start(bf16[512,256]{1,0:T(8,128)(2,1)S(1)} %bitcast.5), channel_id=1, source_target_pairs={{0,16},{16,0},{1,17},{17,1},{2,18},{18,2},{3,19},{19,3},{4,20},{20... | collective-permute-start | bytes 786440 | tf_op jit(solution)/shard_map/ppermute | solution.py:313
  69.0 0.5 back.1.before_ref
  69.5 0.7 collective-permute-done.1.weighted_ref
  70.2 1.3 %back_last.1 = bf16[2,512,128]{2,1,0:T(8,128)(2,1)} custom-call(bf16[512,1024]{1,0:T(8,128)(2,1)S(1)} %get-tuple-element.16.table_ref, bf16[512,256]{1,0:T(8,128)(2,1)S(1)} %collective-permute-done.1.weighted_ref, f32[256,512]{1,0:T(8,128)S(1)} %back.1.before_ref), custom_call_target="tpu_custom_call" | custom-call | tf_op jit(solution)/shard_map/back_last/pallas_call | solution.py:288
Async XLA Ops:
  0.6 11.3 %copy-start = (f32[4,8,8]{2,1,0:T(8,128)S(1)}, f32[4,8,8]{2,1,0:T(8,128)}, u32[]{:S(2)}) copy-start(f32[4,8,8]{2,1,0:T(8,128)} %param.17) | copy-start | bytes 3076
  3.2 10.1 %collective-permute-start = (bf16[512,256]{1,0:T(8,128)(2,1)S(1)}, bf16[512,256]{1,0:T(8,128)(2,1)S(1)}, u32[]{:S(2)}, u32[]{:S(2)}) collective-permute-start(bf16[512,256]{1,0:T(8,128)(2,1)S(1)} %get-tuple-element.21), channel_id=1, source_target_pairs={{0,16},{16,0},{1,17},{17,1},{2,18},{18,2},{3,19},{19,3},{4,20},{20... | collective-permute-start | bytes 786440 | tf_op jit(solution)/shard_map/ppermute | solution.py:303
  63.4 6.7 %collective-permute-start.1 = (bf16[512,256]{1,0:T(8,128)(2,1)S(1)}, bf16[512,256]{1,0:T(8,128)(2,1)S(1)}, u32[]{:S(2)}, u32[]{:S(2)}) collective-permute-start(bf16[512,256]{1,0:T(8,128)(2,1)S(1)} %bitcast.5), channel_id=1, source_target_pairs={{0,16},{16,0},{1,17},{17,1},{2,18},{18,2},{3,19},{19,3},{4,20},{20... | collective-permute-start | bytes 786440 | tf_op jit(solution)/shard_map/ppermute | solution.py:313

commit v4 on v3

--- a/solution.py
+++ b/solution.py
@@ -12,6 +12,9 @@
 HIGH = lax.Precision.HIGHEST
 F32 = jnp.float32
 BF16 = jnp.bfloat16
+OTHER_ENDS = (8, 12, 16)
+OWN_ENDS = (12, 16)
+CHUNKS = 2
 SIN = (6.283185005187988, -41.341590881347656, 81.59994506835938,
        -76.61447143554688, 41.3428840637207, -12.471243858337402)
 COS = (1.0, -19.73920440673828, 64.93911743164062, -85.45014190673828,
@@ -32,6 +35,21 @@
     return lax.broadcasted_iota(jnp.int32, shape, dim)
 
 
+def in_parts(array):
+    high = array.astype(BF16).astype(F32)
+    rest = array - high
+    middle = rest.astype(BF16).astype(F32)
+    return high, middle, rest - middle
+
+
+def gather_lanes(array, order):
+    rows, lanes = array.shape
+    parts = jnp.concatenate(in_parts(array), axis=0).astype(BF16)
+    chosen = (iota((lanes, lanes), 0) == order).astype(F32).astype(BF16)
+    picked = jnp.dot(parts, chosen, preferred_element_type=F32)
+    return picked[:rows] + picked[rows:2 * rows] + picked[2 * rows:]
+
+
 def horner(coefficients, z):
     total = jnp.full_like(z, coefficients[-1])
     for c in coefficients[-2::-1]:
@@ -58,7 +76,8 @@
     return copies
 
 
-def project_rows(by_row, grid_ref, rhs_ref, beta_ref, proj_ref):
+def project_rows(by_row, grid_ref, rhs_ref, beta_ref, proj_ref, ends, before_first):
+    done = 0
     gcount = grid_ref.shape[1]
     wide = (8, gcount)
     m, g = ([jnp.broadcast_to(grid_ref[d:d + 1, :], wide) for d in dims] for dims in ((0, 1, 2), (3, 4, 5)))
@@ -89,7 +108,13 @@
                 im.append(amp * cos)
         beta_ref[q * 32:q * 32 + 32, 0:gcount] = jnp.concatenate(re, axis=0).astype(BF16)
         beta_ref[q * 32:q * 32 + 32, gcount:] = jnp.concatenate(im, axis=0).astype(BF16)
-    proj_ref[...] = jnp.dot(beta_ref[...], rhs_ref[...], preferred_element_type=F32).astype(proj_ref.dtype)
+        if q + 1 in ends:
+            if done == 0:
+                before_first()
+            rows = slice(done * 32, (q + 1) * 32)
+            proj_ref[rows, :] = jnp.dot(beta_ref[rows, :], rhs_ref[...],
+                                        preferred_element_type=F32).astype(proj_ref.dtype)
+            done = q + 1
 
 
 def other_tables_kernel(recip_hbm, widths_hbm, wave_hbm, miller_hbm, frac_hbm, species_hbm, order_hbm,
@@ -112,15 +137,18 @@
             row = jnp.where(spec == s, widths_ref[s:s + 1, c:c + 1], row)
         rows.append(row)
     rows.append(spec.astype(F32))
-    by_atom = jnp.concatenate(rows, axis=0)
-    pick = (iota((natoms, natoms), 0) == order_ref[...]).astype(F32)
-    by_slot = dot_high(by_atom, pick, NN)
-    row_id = iota((owners * 16, natoms), 0)
-    half = jnp.where(row_id < owners * 8, 1 - core, core)
-    slot = ((row_id // 8) % owners) * 8 + half * 4 + row_id % 4
-    expand = (iota((owners * 16, natoms), 1) == slot).astype(F32)
-    by_row = dot_high(expand, by_slot, NT)
-    own_row_ref[...] = by_row[owners * 8:, :]
+    by_slot = gather_lanes(jnp.concatenate(rows, axis=0), order_ref[...]).T
+    low = iota((8, 8), 0) < 4
+    first_four, last_four = [], []
+    for q in range(owners):
+        here = by_slot[q * 8:q * 8 + 8, :]
+        turned = pltpu.roll(here, 4, 0)
+        first_four.append(jnp.where(low, here, turned))
+        last_four.append(jnp.where(low, turned, here))
+    first_four = jnp.concatenate(first_four, axis=0)
+    last_four = jnp.concatenate(last_four, axis=0)
+    by_row = jnp.where(core == 0, last_four, first_four)
+    own_row_ref[...] = jnp.where(core == 0, first_four, last_four)
 
     mil = miller_ref[...].astype(F32)
     m = [mil[d:d + 1, :] for d in range(3)]
@@ -129,14 +157,17 @@
          for d in range(3)]
     g2 = g[0] * g[0] + g[1] * g[1] + g[2] * g[2]
     grid_ref[...] = jnp.concatenate([*m, *g, g2, g2], axis=0)
-    loads[0].wait()
-    nb = wave_ref.shape[2]
-    real, imag = wave_ref[0], wave_ref[1]
-    rhs_ref[0:gcount, 0:nb] = real
-    rhs_ref[0:gcount, nb:] = imag
-    rhs_ref[gcount:, 0:nb] = imag
-    rhs_ref[gcount:, nb:] = -real
-    project_rows(by_row[:owners * 8, :], grid_ref, rhs_ref, beta_ref, proj_ref)
+
+    def make_rhs():
+        loads[0].wait()
+        nb = wave_ref.shape[2]
+        real, imag = wave_ref[0], wave_ref[1]
+        rhs_ref[0:gcount, 0:nb] = real
+        rhs_ref[0:gcount, nb:] = imag
+        rhs_ref[gcount:, 0:nb] = imag
+        rhs_ref[gcount:, nb:] = -real
+
+    project_rows(by_row, grid_ref, rhs_ref, beta_ref, proj_ref, OTHER_ENDS, make_rhs)
 
 
 def other_tables(wavefunctions, miller, reciprocal, fractional, species, atom_order, radial_widths):
@@ -162,22 +193,30 @@
                       beta_ref, proj_ref, couple_ref, base_rows_ref, weights_ref,
                       coupling_ref, occupations_ref, copied):
     loads = fetch(((coupling_hbm, coupling_ref), (occupations_hbm, occupations_ref)), copied)
-    project_rows(own_row_ref[...], grid_ref, rhs_ref, beta_ref, proj_ref)
-    for load in loads:
-        load.wait()
-    spec = own_row_ref[pl.ds(pl.multiple_of(lax.axis_index("chip") * 8, 8), 8), 7:8]
-    kinds = base_ref.shape[0]
-    base = jnp.broadcast_to(base_ref[0:1, :], (8, 64))
-    for s in range(1, kinds):
-        base = jnp.where(spec == s, base_ref[s:s + 1, :], base)
-    base_rows_ref[...] = jnp.concatenate([base] * 4, axis=0)
-    for a in range(4):
-        block = coupling_ref[0]
+    chip = lax.axis_index("chip")
+
+    def of_owned_atoms():
+        for load in loads:
+            load.wait()
+        spec = own_row_ref[pl.ds(pl.multiple_of(chip * 8, 8), 8), 7:8]
+        kinds = base_ref.shape[0]
+        base = jnp.broadcast_to(base_ref[0:1, :], (8, 64))
         for s in range(1, kinds):
-            block = jnp.where(spec[a:a + 1, :] == s, coupling_ref[s], block)
-        couple_ref[:, a * 64:(a + 1) * 64] = block
-    w = occupations_ref[...] * (1.0 / (occupations_ref.shape[1] * bands))
-    weights_ref[...] = jnp.concatenate([w, w], axis=1)
+            base = jnp.where(spec == s, base_ref[s:s + 1, :], base)
+        base_rows_ref[...] = base
+        by_kind = [coupling_ref[s].T for s in range(kinds)]
+        for a in range(4):
+            for i in range(8):
+                rows = slice(i * 8, i * 8 + 8)
+                block = by_kind[0][rows]
+                for s in range(1, kinds):
+                    block = jnp.where(spec[a:a + 1, :] == s, by_kind[s][rows], block)
+                to = ((i % 2) * 4 + i // 2) * 32 + a * 8
+                couple_ref[to:to + 8, :] = block
+        w = occupations_ref[...] * (1.0 / (occupations_ref.shape[1] * bands))
+        weights_ref[...] = jnp.concatenate([w, w], axis=1)
+
+    project_rows(own_row_ref[...], grid_ref, rhs_ref, beta_ref, proj_ref, OWN_ENDS, of_owned_atoms)
 
 
 def own_tables(bands, own_row, grid, rhs, base, coupling, occupations):
@@ -185,7 +224,7 @@
     return pl.pallas_call(
         functools.partial(own_tables_kernel, bands),
         out_shape=(jax.ShapeDtypeStruct((nrows, rhs.shape[0]), BF16), jax.ShapeDtypeStruct((nrows, rhs.shape[1]), F32),
-                   jax.ShapeDtypeStruct((64, 256), F32), jax.ShapeDtypeStruct((32, 64), F32),
+                   jax.ShapeDtypeStruct((256, 64), F32), jax.ShapeDtypeStruct((8, 64), F32),
                    jax.ShapeDtypeStruct((1, rhs.shape[1]), F32)),
         in_specs=[vmem()] * 4 + [hbm()] * 2,
         out_specs=(vmem(),) * 5,
@@ -200,16 +239,13 @@
     total = parts_ref[0].astype(F32)
     for k in range(1, parts_ref.shape[0]):
         total = total + parts_ref[k].astype(F32)
-    proj_ref[...] = total
-    gram = dot_high(total * weights_ref[...], total, NT)
-    gram = jnp.where(iota((32, 32), 0) % 4 == iota((32, 32), 1) % 4, gram, 0.0)
-    lane = iota((32, 128), 1)
-    spread = (iota((32, 128), 0) // 4 == lane % 8).astype(F32)
-    wide = dot_high(gram, spread, NN)
-    row = iota((32, 128), 0)
-    wide = jnp.where(((lane // 8) % 8 == row // 4) & (lane // 64 == (row % 4) % 2), wide, 0.0)
-    fold = ((iota((8, 32), 1) % 4) // 2 == iota((8, 32), 0)).astype(F32)
-    flat = dot_high(fold, wide, NN)[0:2, :]
+    nb = proj_ref.shape[2]
+    proj_ref[0] = total[:, :nb]
+    proj_ref[1] = total[:, nb:]
+    by_atom = jnp.concatenate([jnp.concatenate(
+        [proj_ref[h, pl.ds(a, 8, stride=4), :] for a in range(4)], axis=0) for h in range(2)], axis=1)
+    gram = dot_high(total * weights_ref[...], by_atom, NT)
+    flat = jnp.concatenate([gram[k * 8:k * 8 + 8, :] for k in range(4)], axis=1)
     for k in range(send_ref.shape[0]):
         send_ref[k] = flat
 
@@ -218,7 +254,7 @@
     _, nrows, width = parts.shape
     return pl.pallas_call(
         occupancy_kernel,
-        out_shape=(jax.ShapeDtypeStruct((nrows, width), F32), jax.ShapeDtypeStruct((peers, 2, 128), F32)),
+        out_shape=(jax.ShapeDtypeStruct((2, nrows, width // 2), F32), jax.ShapeDtypeStruct((peers, 8, 128), F32)),
         in_specs=[vmem(), vmem()],
         out_specs=(vmem(), vmem()),
         compiler_params=LIMIT,
@@ -227,21 +263,26 @@
 
 
 def weigh_kernel(parts_ref, proj_ref, couple_ref, base_ref, onsite_ref, send_ref):
-    occ = jnp.sum(parts_ref[...], axis=0)
-    flat = jnp.concatenate([occ[0:1, :], occ[1:2, :]], axis=1)
-    lane = iota((32, 256), 1)
-    by_atom = jnp.where(lane // 64 == iota((32, 256), 0) % 4, flat, 0.0)
-    onsite = dot_high(by_atom, couple_ref[...], NT) + base_ref[...]
-    row = iota((32, 64), 0)
-    onsite = jnp.where(iota((32, 64), 1) // 8 == row // 4, onsite, 0.0)
-    spread = (iota((64, 32), 0) % 8 == iota((64, 32), 1) // 4).astype(F32)
-    fold = (iota((64, 8), 0) % 8 == iota((64, 8), 1)).astype(F32)
-    square = dot_high(onsite, fold, NN)
-    for i in range(8):
-        onsite_ref[:, i, :] = square[i * 4:i * 4 + 4, :]
-    full = dot_high(onsite, spread, NN)
-    full = jnp.where(iota((32, 32), 0) % 4 == iota((32, 32), 1) % 4, full, 0.0)
-    weighted = dot_high(full, proj_ref[...], NN).astype(BF16)
+    occ = parts_ref[0]
+    for k in range(1, parts_ref.shape[0]):
+        occ = occ + parts_ref[k]
+    row, lane = iota((8, 128), 0), iota((8, 128), 1)
+    occ = jnp.where((lane // 8) % 4 == row % 4, occ, 0.0)
+    by_parity = jnp.concatenate([jnp.where(row < 4, occ, 0.0), jnp.where(row < 4, 0.0, occ)], axis=1)
+    response = dot_high(by_parity, couple_ref[...], NN)
+    onsite = response + pltpu.roll(response, 4, 0) + base_ref[...]
+    onsite_ref[...] = onsite
+    pair = jnp.where(iota((8, 64), 0) < 4, onsite, jnp.concatenate([onsite[:, 8:], onsite[:, :8]], axis=1))
+    low = iota((8, 2 * proj_ref.shape[2]), 0) < 4
+    total = [None] * 4
+    for k in range(4):
+        here = jnp.concatenate([proj_ref[h, k * 8:k * 8 + 8, :] for h in range(2)], axis=1)
+        turned = pltpu.roll(here, 4, 0)
+        for j, both in ((2 * k, jnp.where(low, here, turned)), (2 * k + 1, jnp.where(low, turned, here))):
+            for t in range(4):
+                term = pair[:, 16 * t + j:16 * t + j + 1] * both
+                total[t] = term if total[t] is None else total[t] + term
+    weighted = jnp.concatenate(total, axis=0).astype(BF16)
     for k in range(send_ref.shape[0]):
         send_ref[k] = weighted
 
@@ -249,7 +290,7 @@
 def weigh(parts, proj, couple, base_rows, peers):
     return pl.pallas_call(
         weigh_kernel,
-        out_shape=(jax.ShapeDtypeStruct((4, 8, 8), F32), jax.ShapeDtypeStruct((peers, *proj.shape), BF16)),
+        out_shape=(jax.ShapeDtypeStruct((8, 64), F32), jax.ShapeDtypeStruct((peers, proj.shape[1], 2 * proj.shape[2]), BF16)),
         in_specs=[vmem()] * 4,
         out_specs=(vmem(), vmem()),
         compiler_params=LIMIT,
@@ -257,38 +298,63 @@
     )(parts, proj, couple, base_rows)
 
 
-def product_with(table_ref, weighted_ref):
-    width = weighted_ref.shape[1]
+def turned_by_i(weighted):
+    half = weighted.shape[1] // 2
+    return jnp.concatenate([-weighted[:, half:], weighted[:, :half]], axis=1)
+
+
+def back_kernel(table_ref, weighted_ref, other_ref, onsite_ref, out_ref, other_t_ref, square_ref):
+    for i in range(8):
+        square_ref[:, i, :] = onsite_ref[0:4, i * 8:i * 8 + 8]
     gcount = table_ref.shape[1] // 2
-    real, imag = weighted_ref[:, :width // 2], weighted_ref[:, width // 2:]
-    turned = jnp.concatenate([-imag, real], axis=1)
-    return (lax.dot_general(weighted_ref[...], table_ref[:, :gcount], TN, preferred_element_type=F32)
-            + lax.dot_general(turned, table_ref[:, gcount:], TN, preferred_element_type=F32))
-
-
-def back_kernel(table_ref, weighted_ref, out_ref):
-    out_ref[...] = product_with(table_ref, weighted_ref)
-
-
-def back_last_kernel(table_ref, weighted_ref, before_ref, out_ref):
-    total = before_ref[...] + product_with(table_ref, weighted_ref)
-    half = total.shape[0] // 2
-    out_ref[0] = total[:half].T.astype(BF16)
-    out_ref[1] = total[half:].T.astype(BF16)
-
-
-def back_project(table, weighted, before=None):
-    gcount, width = table.shape[1] // 2, weighted.shape[1]
-    if before is None:
-        return pl.pallas_call(
-            back_kernel,
-            out_shape=jax.ShapeDtypeStruct((width, gcount), F32),
-            in_specs=[vmem()] * 2, out_specs=vmem(), compiler_params=LIMIT, name="back",
-        )(table, weighted)
+    nrows = other_ref.shape[0]
+    weighted = weighted_ref[...]
+    total = (lax.dot_general(weighted, table_ref[:, :gcount], TN, preferred_element_type=F32)
+             + lax.dot_general(turned_by_i(weighted), table_ref[:, gcount:], TN, preferred_element_type=F32))
+    out_ref[...] = total.T
+    other_t_ref[:, :nrows] = other_ref[:, :gcount].T
+    other_t_ref[:, nrows:] = other_ref[:, gcount:].T
+
+
+def back(table, weighted, other, onsite):
+    gcount = table.shape[1] // 2
+    return pl.pallas_call(
+        back_kernel,
+        out_shape=(jax.ShapeDtypeStruct((gcount, weighted.shape[1]), F32),
+                   jax.ShapeDtypeStruct((gcount, 2 * other.shape[0]), BF16), jax.ShapeDtypeStruct((4, 8, 8), F32)),
+        in_specs=[vmem()] * 4, out_specs=(vmem(),) * 3, compiler_params=LIMIT, name="back",
+    )(table, weighted, other, onsite)
+
+
+def back_last_kernel(table_ref, weighted_ref, before_ref, out_hbm, out_ref, copied):
+    nrows, width = weighted_ref.shape
+    half = width // 2
+    weighted = weighted_ref[...]
+    turned = turned_by_i(weighted)
+    chunks = copied.shape[0]
+    size = table_ref.shape[0] // chunks
+    copies = []
+    for k in range(chunks):
+        rows = slice(k * size, (k + 1) * size)
+        total = (before_ref[rows, :] + jnp.dot(table_ref[rows, :nrows], weighted, preferred_element_type=F32)
+                 + jnp.dot(table_ref[rows, nrows:], turned, preferred_element_type=F32))
+        out_ref[k, 0] = total[:, :half].astype(BF16)
+        out_ref[k, 1] = total[:, half:].astype(BF16)
+        copies.append(pltpu.make_async_copy(out_ref.at[k], out_hbm.at[:, pl.ds(k * size, size), :], copied.at[k]))
+        copies[-1].start()
+    for copy in copies:
+        copy.wait()
+
+
+def back_last(table, weighted, before):
+    gcount, width = before.shape
     return pl.pallas_call(
         back_last_kernel,
         out_shape=jax.ShapeDtypeStruct((2, gcount, width // 2), BF16),
-        in_specs=[vmem()] * 3, out_specs=vmem(), compiler_params=LIMIT, name="back_last",
+        in_specs=[vmem()] * 3, out_specs=hbm(),
+        scratch_shapes=[pltpu.VMEM((CHUNKS, 2, gcount // CHUNKS, width // 2), BF16),
+                        pltpu.SemaphoreType.DMA((CHUNKS,))],
+        compiler_params=LIMIT, name="back_last",
     )(table, weighted, before)
 
 
@@ -311,8 +377,8 @@
     onsite, weighted = weigh(occupancy, proj, couple, base_rows, chips)
     weighted = lax.all_to_all(weighted, "chip", 0, 0, tiled=True).reshape(-1, 2 * nb)
     other_weighted = lax.ppermute(weighted, "core", swap)
-    applied = back_project(mine, weighted)
-    applied = back_project(other, other_weighted, applied)
+    before, other_t, onsite = back(mine, weighted, other, onsite)
+    applied = back_last(other_t, other_weighted, before)
     return applied, onsite
 
 

time: 71.7 us -> 71 us (level)
  transfers between devices with their start and end apart: 2 -> 2, of which waited for: 1 -> 1; matrix products, arithmetic and copies ran while one was open for 0% -> 0% of each run, Pallas kernels for 2% -> 3%
where the time goes in v4:
time: 71 us; the launch traced here: 70.7 us
  blocking collectives  49 us (69%)
  starting transfers between devices  14.2 us (20%)
  Pallas kernels  6.35 us (9%)
  between operations  0.71 us (1%)
    all_to_all x1, blocking collectives, local(): parts = lax.all_to_all(chip_sum, 'chip', 0, 0, tiled=True)  20 us
    all_to_all x1, blocking collectives, local(): lax.all_to_all(weighted, 'chip', 0, 0, tiled=True).reshape(-1, 2 * nb)  14.9 us
    all_to_all x1, blocking collectives, local(): occupancy = lax.all_to_all(occupancy, 'band', 0, 0, tiled=True)  14.1 us
    ppermute x1, starting transfers between devices, local(): received = lax.ppermute(other_proj, 'core', swap)  8.79 us
    ppermute x1, starting transfers between devices, local(): other_weighted = lax.ppermute(weighted, 'core', swap)  5.43 us
    pallas_call x1, Pallas kernels, other_tables(): pl.pallas_call(other_tables_kernel, out_shape=(jax.ShapeDtypeStruct((nato...  2.22 us
    pallas_call x1, Pallas kernels, own_tables(): pl.pallas_call(functools.partial(own_tables_kernel, bands), out_shape=(ja...  1.48 us
  transfers between devices with their start and end apart: 2, of which 1 were waited for; matrix products, arithmetic and copies ran while one was open for 0% of the time, Pallas kernels for 3%

profile of v4, /device:TPU:1, one launch (start us, length us, event | category | flops | bytes accessed | tf_op | source)
XLA Modules:
  0.0 70.7 jit_solution(16368283228425700139)
XLA Ops:
  0.6 0.0 copy-start
  0.6 2.2 %other_tables.1 = (bf16[512,1024]{1,0:T(8,128)(2,1)S(1)}, bf16[512,256]{1,0:T(8,128)(2,1)S(1)}, f32[128,8]{1,0:T(8,128)S(1)}, f32[8,512]{1,0:T(8,128)S(1)}, bf16[1024,256]{1,0:T(8,128)(2,1)S(1)}) custom-call(f32[3,3]{1,0:T(4,128)} %recip_hbm.1, f32[4,4]{1,0:T(4,128)} %widths_hbm.1, bf16[2,512,128]{2,1,0:T(8,128)(2,1)} %wave_hbm.1, s32[3,512]{1,0:T(4,128)} %miller_hbm.1, ...), custom_call_target="tpu_custom_call" | custom-call | tf_op jit(solution)/shard_map/other_tables/pallas_call | solution.py:178
  2.9 8.8 %collective-permute-start = (bf16[512,256]{1,0:T(8,128)(2,1)S(1)}, bf16[512,256]{1,0:T(8,128)(2,1)S(1)}, u32[]{:S(2)}, u32[]{:S(2)}) collective-permute-start(bf16[512,256]{1,0:T(8,128)(2,1)S(1)} %get-tuple-element.24), channel_id=1, source_target_pairs={{0,16},{16,0},{1,17},{17,1},{2,18},{18,2},{3,19},{19,3},{4,20},{20... | collective-permute-start | bytes 786440 | tf_op jit(solution)/shard_map/ppermute | solution.py:369
  11.7 0.0 copy-done
  11.7 0.1 reshape.24.base_ref
  11.8 1.5 %own_tables.1 = (bf16[512,1024]{1,0:T(8,128)(2,1)S(1)}, f32[512,256]{1,0:T(8,128)S(1)}, f32[256,64]{1,0:T(8,128)S(1)}, f32[8,64]{1,0:T(8,128)S(1)}, f32[1,256]{1,0:T(1,128)S(1)}) custom-call(f32[128,8]{1,0:T(8,128)S(1)} %get-tuple-element.19.own_row_ref, f32[8,512]{1,0:T(8,128)S(1)} %get-tuple-element.20.grid_ref, ...), custom_call_target="tpu_custom_call" | custom-call | tf_op jit(solution)/shard_map/own_tables/pallas_call | solution.py:224
  13.2 0.0 collective-permute-done
  13.3 0.1 add_convert_fusion
  13.3 20.0 %all_to_all.15.parts_ref = bf16[16,32,256]{2,1,0:T(8,128)(2,1)S(1)} all-to-all(bf16[16,32,256]{2,1,0:T(8,128)(2,1)S(1)} %bitcast.7), channel_id=1, replica_groups=mesh['chip'=16,'core'=2,'band'=16] {'chip'}, dimensions={0} | all-to-all | bytes 524288 | tf_op jit(solution)/shard_map/all_to_all | solution.py:373
  33.3 0.3 occupancy.1
  33.6 14.1 %all_to_all.16.parts_ref = f32[16,8,128]{2,1,0:T(8,128)S(1)} all-to-all(f32[16,8,128]{2,1,0:T(8,128)S(1)} %get-tuple-element.26), channel_id=1, replica_groups=mesh['chip'=16,'core'=2,'band'=16] {'band'}, dimensions={0} | all-to-all | bytes 131072 | tf_op jit(solution)/shard_map/all_to_all | solution.py:376
  47.7 0.4 weigh.1
  48.1 14.9 %all_to_all.17 = bf16[16,32,256]{2,1,0:T(8,128)(2,1)S(1)} all-to-all(bf16[16,32,256]{2,1,0:T(8,128)(2,1)S(1)} %get-tuple-element.30), channel_id=1, replica_groups=mesh['chip'=16,'core'=2,'band'=16] {'chip'}, dimensions={0} | all-to-all | bytes 524288 | tf_op jit(solution)/shard_map/all_to_all | solution.py:378
  63.0 5.4 %collective-permute-start.1 = (bf16[512,256]{1,0:T(8,128)(2,1)S(1)}, bf16[512,256]{1,0:T(8,128)(2,1)S(1)}, u32[]{:S(2)}, u32[]{:S(2)}) collective-permute-start(bf16[512,256]{1,0:T(8,128)(2,1)S(1)} %bitcast.5), channel_id=1, source_target_pairs={{0,16},{16,0},{1,17},{17,1},{2,18},{18,2},{3,19},{19,3},{4,20},{20... | collective-permute-start | bytes 786440 | tf_op jit(solution)/shard_map/ppermute | solution.py:379
  68.4 0.8 %back.1 = (f32[512,256]{1,0:T(8,128)S(1)}, bf16[512,1024]{1,0:T(8,128)(2,1)S(1)}, f32[4,8,8]{2,1,0:T(8,128)}) custom-call(bf16[512,1024]{1,0:T(8,128)(2,1)S(1)} %get-tuple-element.22.table_ref, bf16[512,256]{1,0:T(8,128)(2,1)S(1)} %bitcast.6, bf16[512,1024]{1,0:T(8,128)(2,1)S(1)} %get-tuple-element.31.other_ref, f32[8,64]{1,0:T(8,128)S(1)} %get-tuple-element.32.onsite_ref), custom_call_target="tpu_custom_call" | custom-call | tf_op jit(solution)/shard_map/back/pallas_call | solution.py:321
  69.2 0.3 collective-permute-done.1.weighted_ref
  69.6 1.2 %back_last.1 = bf16[2,512,128]{2,1,0:T(8,128)(2,1)} custom-call(bf16[512,1024]{1,0:T(8,128)(2,1)S(1)} %get-tuple-element.33.table_ref, bf16[512,256]{1,0:T(8,128)(2,1)S(1)} %collective-permute-done.1.weighted_ref, f32[512,256]{1,0:T(8,128)S(1)} %get-tuple-element.34.before_ref), custom_call_target="tpu_custom_call" | custom-call | tf_op jit(solution)/shard_map/back_last/pallas_call | solution.py:351
Async XLA Ops:
  0.6 11.0 %copy-start = (f32[4,8,8]{2,1,0:T(8,128)S(1)}, f32[4,8,8]{2,1,0:T(8,128)}, u32[]{:S(2)}) copy-start(f32[4,8,8]{2,1,0:T(8,128)} %param.17) | copy-start | bytes 3076
  2.9 10.4 %collective-permute-start = (bf16[512,256]{1,0:T(8,128)(2,1)S(1)}, bf16[512,256]{1,0:T(8,128)(2,1)S(1)}, u32[]{:S(2)}, u32[]{:S(2)}) collective-permute-start(bf16[512,256]{1,0:T(8,128)(2,1)S(1)} %get-tuple-element.24), channel_id=1, source_target_pairs={{0,16},{16,0},{1,17},{17,1},{2,18},{18,2},{3,19},{19,3},{4,20},{20... | collective-permute-start | bytes 786440 | tf_op jit(solution)/shard_map/ppermute | solution.py:369
  63.0 6.6 %collective-permute-start.1 = (bf16[512,256]{1,0:T(8,128)(2,1)S(1)}, bf16[512,256]{1,0:T(8,128)(2,1)S(1)}, u32[]{:S(2)}, u32[]{:S(2)}) collective-permute-start(bf16[512,256]{1,0:T(8,128)(2,1)S(1)} %bitcast.5), channel_id=1, source_target_pairs={{0,16},{16,0},{1,17},{17,1},{2,18},{18,2},{3,19},{19,3},{4,20},{20... | collective-permute-start | bytes 786440 | tf_op jit(solution)/shard_map/ppermute | solution.py:379

commit v5 on v4

--- a/solution.py
+++ b/solution.py
@@ -12,9 +12,9 @@
 HIGH = lax.Precision.HIGHEST
 F32 = jnp.float32
 BF16 = jnp.bfloat16
-OTHER_ENDS = (8, 12, 16)
+OTHER_ENDS = (8, 14, 16)
 OWN_ENDS = (12, 16)
-CHUNKS = 2
+CHUNKS = 4
 SIN = (6.283185005187988, -41.341590881347656, 81.59994506835938,
        -76.61447143554688, 41.3428840637207, -12.471243858337402)
 COS = (1.0, -19.73920440673828, 64.93911743164062, -85.45014190673828,
@@ -112,8 +112,11 @@
             if done == 0:
                 before_first()
             rows = slice(done * 32, (q + 1) * 32)
-            proj_ref[rows, :] = jnp.dot(beta_ref[rows, :], rhs_ref[...],
-                                        preferred_element_type=F32).astype(proj_ref.dtype)
+            by_real = jnp.dot(beta_ref[rows, :gcount], rhs_ref[...], preferred_element_type=F32)
+            by_imag = jnp.dot(beta_ref[rows, gcount:], rhs_ref[...], preferred_element_type=F32)
+            half = rhs_ref.shape[1] // 2
+            proj_ref[rows, :half] = (by_real[:, :half] + by_imag[:, half:]).astype(proj_ref.dtype)
+            proj_ref[rows, half:] = (by_real[:, half:] - by_imag[:, :half]).astype(proj_ref.dtype)
             done = q + 1
 
 
@@ -161,11 +164,8 @@
     def make_rhs():
         loads[0].wait()
         nb = wave_ref.shape[2]
-        real, imag = wave_ref[0], wave_ref[1]
-        rhs_ref[0:gcount, 0:nb] = real
-        rhs_ref[0:gcount, nb:] = imag
-        rhs_ref[gcount:, 0:nb] = imag
-        rhs_ref[gcount:, nb:] = -real
+        rhs_ref[:, :nb] = wave_ref[0]
+        rhs_ref[:, nb:] = wave_ref[1]
 
     project_rows(by_row, grid_ref, rhs_ref, beta_ref, proj_ref, OTHER_ENDS, make_rhs)
 
@@ -180,7 +180,7 @@
         out_shape=(jax.ShapeDtypeStruct((natoms * 4, 2 * gcount), BF16),
                    jax.ShapeDtypeStruct((natoms * 4, 2 * nb), BF16),
                    jax.ShapeDtypeStruct((natoms, 8), F32), jax.ShapeDtypeStruct((8, gcount), F32),
-                   jax.ShapeDtypeStruct((2 * gcount, 2 * nb), BF16)),
+                   jax.ShapeDtypeStruct((gcount, 2 * nb), BF16)),
         in_specs=[hbm()] * len(args),
         out_specs=(vmem(),) * 5,
         scratch_shapes=[pltpu.VMEM(a.shape, a.dtype) for a in args] + [pltpu.SemaphoreType.DMA((len(args),))],
@@ -223,7 +223,7 @@
     nrows = own_row.shape[0] * 4
     return pl.pallas_call(
         functools.partial(own_tables_kernel, bands),
-        out_shape=(jax.ShapeDtypeStruct((nrows, rhs.shape[0]), BF16), jax.ShapeDtypeStruct((nrows, rhs.shape[1]), F32),
+        out_shape=(jax.ShapeDtypeStruct((nrows, 2 * rhs.shape[0]), BF16), jax.ShapeDtypeStruct((nrows, rhs.shape[1]), F32),
                    jax.ShapeDtypeStruct((256, 64), F32), jax.ShapeDtypeStruct((8, 64), F32),
                    jax.ShapeDtypeStruct((1, rhs.shape[1]), F32)),
         in_specs=[vmem()] * 4 + [hbm()] * 2,
@@ -246,6 +246,10 @@
         [proj_ref[h, pl.ds(a, 8, stride=4), :] for a in range(4)], axis=0) for h in range(2)], axis=1)
     gram = dot_high(total * weights_ref[...], by_atom, NT)
     flat = jnp.concatenate([gram[k * 8:k * 8 + 8, :] for k in range(4)], axis=1)
+    flat = jnp.where((iota((8, 128), 1) // 8) % 4 == iota((8, 128), 0) % 4, flat, 0.0)
+    flat = flat + pltpu.roll(flat, 1, 0)
+    flat = flat + pltpu.roll(flat, 2, 0)
+    flat = jnp.concatenate([flat[3:4, :], flat[7:8, :]], axis=0)
     for k in range(send_ref.shape[0]):
         send_ref[k] = flat
 
@@ -254,7 +258,7 @@
     _, nrows, width = parts.shape
     return pl.pallas_call(
         occupancy_kernel,
-        out_shape=(jax.ShapeDtypeStruct((2, nrows, width // 2), F32), jax.ShapeDtypeStruct((peers, 8, 128), F32)),
+        out_shape=(jax.ShapeDtypeStruct((2, nrows, width // 2), F32), jax.ShapeDtypeStruct((peers, 2, 128), F32)),
         in_specs=[vmem(), vmem()],
         out_specs=(vmem(), vmem()),
         compiler_params=LIMIT,
@@ -266,11 +270,9 @@
     occ = parts_ref[0]
     for k in range(1, parts_ref.shape[0]):
         occ = occ + parts_ref[k]
-    row, lane = iota((8, 128), 0), iota((8, 128), 1)
-    occ = jnp.where((lane // 8) % 4 == row % 4, occ, 0.0)
-    by_parity = jnp.concatenate([jnp.where(row < 4, occ, 0.0), jnp.where(row < 4, 0.0, occ)], axis=1)
-    response = dot_high(by_parity, couple_ref[...], NN)
-    onsite = response + pltpu.roll(response, 4, 0) + base_ref[...]
+    occ = jnp.concatenate([occ[0:1, :], occ[1:2, :]], axis=1)
+    own_atom = (iota((8, 256), 1) // 8) % 4 == iota((8, 256), 0) % 4
+    onsite = dot_high(jnp.where(own_atom, occ, 0.0), couple_ref[...], NN) + base_ref[...]
     onsite_ref[...] = onsite
     pair = jnp.where(iota((8, 64), 0) < 4, onsite, jnp.concatenate([onsite[:, 8:], onsite[:, :8]], axis=1))
     low = iota((8, 2 * proj_ref.shape[2]), 0) < 4
@@ -307,13 +309,12 @@
     for i in range(8):
         square_ref[:, i, :] = onsite_ref[0:4, i * 8:i * 8 + 8]
     gcount = table_ref.shape[1] // 2
-    nrows = other_ref.shape[0]
     weighted = weighted_ref[...]
     total = (lax.dot_general(weighted, table_ref[:, :gcount], TN, preferred_element_type=F32)
              + lax.dot_general(turned_by_i(weighted), table_ref[:, gcount:], TN, preferred_element_type=F32))
     out_ref[...] = total.T
-    other_t_ref[:, :nrows] = other_ref[:, :gcount].T
-    other_t_ref[:, nrows:] = other_ref[:, gcount:].T
+    other_t_ref[0] = other_ref[:, :gcount].T
+    other_t_ref[1] = other_ref[:, gcount:].T
 
 
 def back(table, weighted, other, onsite):
@@ -321,25 +322,23 @@
     return pl.pallas_call(
         back_kernel,
         out_shape=(jax.ShapeDtypeStruct((gcount, weighted.shape[1]), F32),
-                   jax.ShapeDtypeStruct((gcount, 2 * other.shape[0]), BF16), jax.ShapeDtypeStruct((4, 8, 8), F32)),
+                   jax.ShapeDtypeStruct((2, gcount, other.shape[0]), BF16), jax.ShapeDtypeStruct((4, 8, 8), F32)),
         in_specs=[vmem()] * 4, out_specs=(vmem(),) * 3, compiler_params=LIMIT, name="back",
     )(table, weighted, other, onsite)
 
 
 def back_last_kernel(table_ref, weighted_ref, before_ref, out_hbm, out_ref, copied):
-    nrows, width = weighted_ref.shape
-    half = width // 2
+    half = weighted_ref.shape[1] // 2
     weighted = weighted_ref[...]
-    turned = turned_by_i(weighted)
     chunks = copied.shape[0]
-    size = table_ref.shape[0] // chunks
+    size = table_ref.shape[1] // chunks
     copies = []
     for k in range(chunks):
         rows = slice(k * size, (k + 1) * size)
-        total = (before_ref[rows, :] + jnp.dot(table_ref[rows, :nrows], weighted, preferred_element_type=F32)
-                 + jnp.dot(table_ref[rows, nrows:], turned, preferred_element_type=F32))
-        out_ref[k, 0] = total[:, :half].astype(BF16)
-        out_ref[k, 1] = total[:, half:].astype(BF16)
+        by_real = jnp.dot(table_ref[0, rows, :], weighted, preferred_element_type=F32)
+        by_imag = jnp.dot(table_ref[1, rows, :], weighted, preferred_element_type=F32)
+        out_ref[k, 0] = (before_ref[rows, :half] + (by_real[:, :half] - by_imag[:, half:])).astype(BF16)
+        out_ref[k, 1] = (before_ref[rows, half:] + (by_real[:, half:] + by_imag[:, :half])).astype(BF16)
         copies.append(pltpu.make_async_copy(out_ref.at[k], out_hbm.at[:, pl.ds(k * size, size), :], copied.at[k]))
         copies[-1].start()
     for copy in copies:

time: 71 us -> 70.9 us (level)
  no operation moved by 1% of the time
where the time goes in v5:
time: 70.9 us; the launch traced here: 70.6 us
  blocking collectives  48.9 us (69%)
  starting transfers between devices  14.2 us (20%)
  Pallas kernels  6.23 us (9%)
  between operations  0.72 us (1%)
    all_to_all x1, blocking collectives, local(): parts = lax.all_to_all(chip_sum, 'chip', 0, 0, tiled=True)  20 us
    all_to_all x1, blocking collectives, local(): lax.all_to_all(weighted, 'chip', 0, 0, tiled=True).reshape(-1, 2 * nb)  14.9 us
    all_to_all x1, blocking collectives, local(): occupancy = lax.all_to_all(occupancy, 'band', 0, 0, tiled=True)  14.1 us
    ppermute x1, starting transfers between devices, local(): received = lax.ppermute(other_proj, 'core', swap)  8.79 us
    ppermute x1, starting transfers between devices, local(): other_weighted = lax.ppermute(weighted, 'core', swap)  5.43 us
    pallas_call x1, Pallas kernels, other_tables(): pl.pallas_call(other_tables_kernel, out_shape=(jax.ShapeDtypeStruct((nato...  2.18 us
    pallas_call x1, Pallas kernels, own_tables(): pl.pallas_call(functools.partial(own_tables_kernel, bands), out_shape=(ja...  1.46 us
  transfers between devices with their start and end apart: 2, of which 1 were waited for; matrix products, arithmetic and copies ran while one was open for 0% of the time, Pallas kernels for 3%

profile of v5, /device:TPU:1, one launch (start us, length us, event | category | flops | bytes accessed | tf_op | source)
XLA Modules:
  0.0 70.6 jit_solution(16880098007432021856)
XLA Ops:
  0.6 0.0 copy-start
  0.6 2.2 %other_tables.1 = (bf16[512,1024]{1,0:T(8,128)(2,1)S(1)}, bf16[512,256]{1,0:T(8,128)(2,1)S(1)}, f32[128,8]{1,0:T(8,128)S(1)}, f32[8,512]{1,0:T(8,128)S(1)}, bf16[512,256]{1,0:T(8,128)(2,1)S(1)}) custom-call(f32[3,3]{1,0:T(4,128)} %recip_hbm.1, f32[4,4]{1,0:T(4,128)} %widths_hbm.1, bf16[2,512,128]{2,1,0:T(8,128)(2,1)} %wave_hbm.1, s32[3,512]{1,0:T(4,128)} %miller_hbm.1, ...), custom_call_target="tpu_custom_call" | custom-call | tf_op jit(solution)/shard_map/other_tables/pallas_call | solution.py:178
  2.8 8.8 %collective-permute-start = (bf16[512,256]{1,0:T(8,128)(2,1)S(1)}, bf16[512,256]{1,0:T(8,128)(2,1)S(1)}, u32[]{:S(2)}, u32[]{:S(2)}) collective-permute-start(bf16[512,256]{1,0:T(8,128)(2,1)S(1)} %get-tuple-element.24), channel_id=1, source_target_pairs={{0,16},{16,0},{1,17},{17,1},{2,18},{18,2},{3,19},{19,3},{4,20},{20... | collective-permute-start | bytes 786440 | tf_op jit(solution)/shard_map/ppermute | solution.py:368
  11.6 0.0 copy-done
  11.6 0.1 reshape.24.base_ref
  11.7 1.5 %own_tables.1 = (bf16[512,1024]{1,0:T(8,128)(2,1)S(1)}, f32[512,256]{1,0:T(8,128)S(1)}, f32[256,64]{1,0:T(8,128)S(1)}, f32[8,64]{1,0:T(8,128)S(1)}, f32[1,256]{1,0:T(1,128)S(1)}) custom-call(f32[128,8]{1,0:T(8,128)S(1)} %get-tuple-element.19.own_row_ref, f32[8,512]{1,0:T(8,128)S(1)} %get-tuple-element.20.grid_ref, ...), custom_call_target="tpu_custom_call" | custom-call | tf_op jit(solution)/shard_map/own_tables/pallas_call | solution.py:224
  13.2 0.0 collective-permute-done
  13.2 0.1 add_convert_fusion
  13.3 20.0 %all_to_all.15.parts_ref = bf16[16,32,256]{2,1,0:T(8,128)(2,1)S(1)} all-to-all(bf16[16,32,256]{2,1,0:T(8,128)(2,1)S(1)} %bitcast.7), channel_id=1, replica_groups=mesh['chip'=16,'core'=2,'band'=16] {'chip'}, dimensions={0} | all-to-all | bytes 524288 | tf_op jit(solution)/shard_map/all_to_all | solution.py:372
  33.3 0.3 occupancy.1
  33.5 14.1 %all_to_all.16.parts_ref = f32[16,2,128]{2,1,0:T(2,128)S(1)} all-to-all(f32[16,2,128]{2,1,0:T(2,128)S(1)} %get-tuple-element.26), channel_id=1, replica_groups=mesh['chip'=16,'core'=2,'band'=16] {'band'}, dimensions={0} | all-to-all | bytes 32768 | tf_op jit(solution)/shard_map/all_to_all | solution.py:375
  47.6 0.4 weigh.1
  48.0 14.9 %all_to_all.17 = bf16[16,32,256]{2,1,0:T(8,128)(2,1)S(1)} all-to-all(bf16[16,32,256]{2,1,0:T(8,128)(2,1)S(1)} %get-tuple-element.30), channel_id=1, replica_groups=mesh['chip'=16,'core'=2,'band'=16] {'chip'}, dimensions={0} | all-to-all | bytes 524288 | tf_op jit(solution)/shard_map/all_to_all | solution.py:377
  62.9 5.4 %collective-permute-start.1 = (bf16[512,256]{1,0:T(8,128)(2,1)S(1)}, bf16[512,256]{1,0:T(8,128)(2,1)S(1)}, u32[]{:S(2)}, u32[]{:S(2)}) collective-permute-start(bf16[512,256]{1,0:T(8,128)(2,1)S(1)} %bitcast.5), channel_id=1, source_target_pairs={{0,16},{16,0},{1,17},{17,1},{2,18},{18,2},{3,19},{19,3},{4,20},{20... | collective-permute-start | bytes 786440 | tf_op jit(solution)/shard_map/ppermute | solution.py:378
  68.3 0.8 %back.1 = (f32[512,256]{1,0:T(8,128)S(1)}, bf16[2,512,512]{2,1,0:T(8,128)(2,1)S(1)}, f32[4,8,8]{2,1,0:T(8,128)}) custom-call(bf16[512,1024]{1,0:T(8,128)(2,1)S(1)} %get-tuple-element.22.table_ref, bf16[512,256]{1,0:T(8,128)(2,1)S(1)} %bitcast.6, bf16[512,1024]{1,0:T(8,128)(2,1)S(1)} %get-tuple-element.31.other_ref, f32[8,64]{1,0:T(8,128)S(1)} %get-tuple-element.32.onsite_ref), custom_call_target="tpu_custom_call" | custom-call | tf_op jit(solution)/shard_map/back/pallas_call | solution.py:322
  69.1 0.3 collective-permute-done.1.weighted_ref
  69.5 1.1 %back_last.1 = bf16[2,512,128]{2,1,0:T(8,128)(2,1)} custom-call(bf16[2,512,512]{2,1,0:T(8,128)(2,1)S(1)} %get-tuple-element.33.table_ref, bf16[512,256]{1,0:T(8,128)(2,1)S(1)} %collective-permute-done.1.weighted_ref, f32[512,256]{1,0:T(8,128)S(1)} %get-tuple-element.34.before_ref), custom_call_target="tpu_custom_call" | custom-call | tf_op jit(solution)/shard_map/back_last/pallas_call | solution.py:350
Async XLA Ops:
  0.6 11.0 %copy-start = (f32[4,8,8]{2,1,0:T(8,128)S(1)}, f32[4,8,8]{2,1,0:T(8,128)}, u32[]{:S(2)}) copy-start(f32[4,8,8]{2,1,0:T(8,128)} %param.17) | copy-start | bytes 3076
  2.8 10.4 %collective-permute-start = (bf16[512,256]{1,0:T(8,128)(2,1)S(1)}, bf16[512,256]{1,0:T(8,128)(2,1)S(1)}, u32[]{:S(2)}, u32[]{:S(2)}) collective-permute-start(bf16[512,256]{1,0:T(8,128)(2,1)S(1)} %get-tuple-element.24), channel_id=1, source_target_pairs={{0,16},{16,0},{1,17},{17,1},{2,18},{18,2},{3,19},{19,3},{4,20},{20... | collective-permute-start | bytes 786440 | tf_op jit(solution)/shard_map/ppermute | solution.py:368
  62.9 6.6 %collective-permute-start.1 = (bf16[512,256]{1,0:T(8,128)(2,1)S(1)}, bf16[512,256]{1,0:T(8,128)(2,1)S(1)}, u32[]{:S(2)}, u32[]{:S(2)}) collective-permute-start(bf16[512,256]{1,0:T(8,128)(2,1)S(1)} %bitcast.5), channel_id=1, source_target_pairs={{0,16},{16,0},{1,17},{17,1},{2,18},{18,2},{3,19},{19,3},{4,20},{20... | collective-permute-start | bytes 786440 | tf_op jit(solution)/shard_map/ppermute | solution.py:378

commit v6 on v5

--- a/solution.py
+++ b/solution.py
@@ -76,7 +76,7 @@
     return copies
 
 
-def project_rows(by_row, grid_ref, rhs_ref, beta_ref, proj_ref, ends, before_first):
+def project_rows(owners, by_row, grid_ref, rhs_ref, beta_ref, proj_ref, ends, before_first):
     done = 0
     gcount = grid_ref.shape[1]
     wide = (8, gcount)
@@ -85,8 +85,8 @@
     first = iota(wide, 0) < 4
     pair_g = (None, jnp.where(first, g[0], g[1]), jnp.where(first, g[2], g[0]), jnp.where(first, g[1], g[2]))
     first1 = iota((8, 1), 0) < 4
-    for q in range(by_row.shape[0] // 8):
-        par = by_row[q * 8:q * 8 + 8, :]
+    for q, chip in enumerate(owners):
+        par = by_row[chip * 8:chip * 8 + 8, :]
         col = [par[:, k:k + 1] for k in range(7)]
         turns = col[0] * m[0] + col[1] * m[1] + col[2] * m[2]
         r = turns - jnp.round(turns)
@@ -120,7 +120,7 @@
             done = q + 1
 
 
-def other_tables_kernel(recip_hbm, widths_hbm, wave_hbm, miller_hbm, frac_hbm, species_hbm, order_hbm,
+def other_tables_kernel(owners, recip_hbm, widths_hbm, wave_hbm, miller_hbm, frac_hbm, species_hbm, order_hbm,
                         beta_ref, proj_ref, own_row_ref, grid_ref, rhs_ref,
                         recip_ref, widths_ref, wave_ref, miller_ref, frac_ref, species_ref, order_ref, copied):
     loads = fetch(((wave_hbm, wave_ref), (recip_hbm, recip_ref), (widths_hbm, widths_ref), (miller_hbm, miller_ref),
@@ -130,7 +130,6 @@
     core = lax.axis_index("core")
     gcount = miller_ref.shape[1]
     natoms = order_ref.shape[1]
-    owners = natoms // 8
     kinds = widths_ref.shape[0]
     spec = species_ref[...]
     rows = [frac_ref[d:d + 1, :] for d in range(3)]
@@ -143,7 +142,7 @@
     by_slot = gather_lanes(jnp.concatenate(rows, axis=0), order_ref[...]).T
     low = iota((8, 8), 0) < 4
     first_four, last_four = [], []
-    for q in range(owners):
+    for q in range(len(owners)):
         here = by_slot[q * 8:q * 8 + 8, :]
         turned = pltpu.roll(here, 4, 0)
         first_four.append(jnp.where(low, here, turned))
@@ -167,16 +166,16 @@
         rhs_ref[:, :nb] = wave_ref[0]
         rhs_ref[:, nb:] = wave_ref[1]
 
-    project_rows(by_row, grid_ref, rhs_ref, beta_ref, proj_ref, OTHER_ENDS, make_rhs)
-
-
-def other_tables(wavefunctions, miller, reciprocal, fractional, species, atom_order, radial_widths):
+    project_rows(owners, by_row, grid_ref, rhs_ref, beta_ref, proj_ref, OTHER_ENDS, make_rhs)
+
+
+def other_tables(owners, wavefunctions, miller, reciprocal, fractional, species, atom_order, radial_widths):
     gcount, nb = wavefunctions.shape[1:]
     natoms = atom_order.shape[0]
     args = (reciprocal, radial_widths, wavefunctions, miller, fractional, species.reshape(1, -1),
             atom_order.reshape(1, -1))
     return pl.pallas_call(
-        other_tables_kernel,
+        functools.partial(other_tables_kernel, owners),
         out_shape=(jax.ShapeDtypeStruct((natoms * 4, 2 * gcount), BF16),
                    jax.ShapeDtypeStruct((natoms * 4, 2 * nb), BF16),
                    jax.ShapeDtypeStruct((natoms, 8), F32), jax.ShapeDtypeStruct((8, gcount), F32),
@@ -189,7 +188,7 @@
     )(*(in_hbm(a) for a in args))
 
 
-def own_tables_kernel(bands, own_row_ref, grid_ref, rhs_ref, base_ref, coupling_hbm, occupations_hbm,
+def own_tables_kernel(bands, owners, own_row_ref, grid_ref, rhs_ref, base_ref, coupling_hbm, occupations_hbm,
                       beta_ref, proj_ref, couple_ref, base_rows_ref, weights_ref,
                       coupling_ref, occupations_ref, copied):
     loads = fetch(((coupling_hbm, coupling_ref), (occupations_hbm, occupations_ref)), copied)
@@ -216,13 +215,13 @@
         w = occupations_ref[...] * (1.0 / (occupations_ref.shape[1] * bands))
         weights_ref[...] = jnp.concatenate([w, w], axis=1)
 
-    project_rows(own_row_ref[...], grid_ref, rhs_ref, beta_ref, proj_ref, OWN_ENDS, of_owned_atoms)
-
-
-def own_tables(bands, own_row, grid, rhs, base, coupling, occupations):
+    project_rows(owners, own_row_ref[...], grid_ref, rhs_ref, beta_ref, proj_ref, OWN_ENDS, of_owned_atoms)
+
+
+def own_tables(bands, owners, own_row, grid, rhs, base, coupling, occupations):
     nrows = own_row.shape[0] * 4
     return pl.pallas_call(
-        functools.partial(own_tables_kernel, bands),
+        functools.partial(own_tables_kernel, bands, owners),
         out_shape=(jax.ShapeDtypeStruct((nrows, 2 * rhs.shape[0]), BF16), jax.ShapeDtypeStruct((nrows, rhs.shape[1]), F32),
                    jax.ShapeDtypeStruct((256, 64), F32), jax.ShapeDtypeStruct((8, 64), F32),
                    jax.ShapeDtypeStruct((1, rhs.shape[1]), F32)),
@@ -357,24 +356,38 @@
     )(table, weighted, before)
 
 
+def farthest_first(places, extents, first):
+    def distance(i):
+        steps = [abs(a - b) for a, b in zip(places[i], places[first])]
+        return sum(min(s, n - s) for s, n in zip(steps, extents))
+    others = [i for i in range(len(places)) if i != first]
+    return [first] + sorted(others, key=lambda i: (-distance(i), (i - first) % len(places)))
+
+
+def exchange(blocks, axis, members):
+    return lax.all_to_all(blocks, axis, 0, 0, axis_index_groups=[members], tiled=True)
+
+
 def local(wavefunctions, miller, reciprocal, fractional, species, atom_order, radial_widths,
           onsite_base, coupling, occupations):
     chips = lax.axis_size("chip")
     bands = lax.axis_size("band")
     swap = [(0, 1), (1, 0)]
     nb = wavefunctions.shape[2]
+    owners = farthest_first([(i // 2, i % 2 * 2) for i in range(chips)], (chips // 2, 4), chips // 2 + 1)
+    blocks = farthest_first([(i % (bands // 2), i * 2 // bands) for i in range(bands)], (bands // 2, 4), bands * 3 // 4)
     other, other_proj, own_row, grid, rhs = other_tables(
-        wavefunctions, miller, reciprocal, fractional, species, atom_order, radial_widths)
+        owners, wavefunctions, miller, reciprocal, fractional, species, atom_order, radial_widths)
     received = lax.ppermute(other_proj, "core", swap)
     mine, mine_proj, couple, base_rows, weights = own_tables(
-        bands, own_row, grid, rhs, onsite_base.reshape(-1, 64), coupling, occupations.reshape(1, -1))
+        bands, owners, own_row, grid, rhs, onsite_base.reshape(-1, 64), coupling, occupations.reshape(1, -1))
     chip_sum = (mine_proj + received.astype(F32)).astype(BF16).reshape(chips, -1, 2 * nb)
-    parts = lax.all_to_all(chip_sum, "chip", 0, 0, tiled=True)
+    parts = exchange(chip_sum, "chip", owners)
 
     proj, occupancy = occupancy_step(parts, weights, bands)
-    occupancy = lax.all_to_all(occupancy, "band", 0, 0, tiled=True)
+    occupancy = exchange(occupancy, "band", blocks)
     onsite, weighted = weigh(occupancy, proj, couple, base_rows, chips)
-    weighted = lax.all_to_all(weighted, "chip", 0, 0, tiled=True).reshape(-1, 2 * nb)
+    weighted = exchange(weighted, "chip", owners).reshape(-1, 2 * nb)
     other_weighted = lax.ppermute(weighted, "core", swap)
     before, other_t, onsite = back(mine, weighted, other, onsite)
     applied = back_last(other_t, other_weighted, before)

time: 70.9 us -> 63.2 us (0.89)
  blocking collectives: 48.9 us -> 43 us
  starting transfers between devices: 14.2 us -> 12.4 us
    all_to_all x3, blocking collectives: 48.9 us -> 43 us  [exchange(): lax.all_to_all(blocks, axis, 0, 0, axis_index_groups=[members], tiled=True)]
    ppermute x1, starting transfers between devices: 5.43 us -> 3.66 us  [local(): other_weighted = lax.ppermute(weighted, 'core', swap)]
  transfers between devices with their start and end apart: 2 -> 2, of which waited for: 1 -> 1; matrix products, arithmetic and copies ran while one was open for 0% -> 0% of each run, Pallas kernels for 3% -> 4%
where the time goes in v6:
time: 63.2 us; the launch traced here: 62.9 us
  blocking collectives  43 us (68%)
  starting transfers between devices  12.4 us (20%)
  Pallas kernels  6.23 us (10%)
  between operations  0.72 us (1%)
    all_to_all x3, blocking collectives, exchange(): lax.all_to_all(blocks, axis, 0, 0, axis_index_groups=[members], tiled=True)  43 us
    ppermute x1, starting transfers between devices, local(): received = lax.ppermute(other_proj, 'core', swap)  8.79 us
    ppermute x1, starting transfers between devices, local(): other_weighted = lax.ppermute(weighted, 'core', swap)  3.66 us
    pallas_call x1, Pallas kernels, other_tables(): pl.pallas_call(functools.partial(other_tables_kernel, owners), out_shape=...  2.18 us
    pallas_call x1, Pallas kernels, own_tables(): pl.pallas_call(functools.partial(own_tables_kernel, bands, owners), out_s...  1.46 us
  transfers between devices with their start and end apart: 2, of which 1 were waited for; matrix products, arithmetic and copies ran while one was open for 0% of the time, Pallas kernels for 4%

profile of v6, /device:TPU:1, one launch (start us, length us, event | category | flops | bytes accessed | tf_op | source)
XLA Modules:
  0.0 62.9 jit_solution(17822885292241256824)
XLA Ops:
  0.6 0.0 copy-start
  0.6 2.2 %other_tables.1 = (bf16[512,1024]{1,0:T(8,128)(2,1)S(1)}, bf16[512,256]{1,0:T(8,128)(2,1)S(1)}, f32[128,8]{1,0:T(8,128)S(1)}, f32[8,512]{1,0:T(8,128)S(1)}, bf16[512,256]{1,0:T(8,128)(2,1)S(1)}) custom-call(f32[3,3]{1,0:T(4,128)} %recip_hbm.1, f32[4,4]{1,0:T(4,128)} %widths_hbm.1, bf16[2,512,128]{2,1,0:T(8,128)(2,1)} %wave_hbm.1, s32[3,512]{1,0:T(4,128)} %miller_hbm.1, ...), custom_call_target="tpu_custom_call" | custom-call | tf_op jit(solution)/shard_map/other_tables/pallas_call | solution.py:177
  2.8 8.8 %collective-permute-start = (bf16[512,256]{1,0:T(8,128)(2,1)S(1)}, bf16[512,256]{1,0:T(8,128)(2,1)S(1)}, u32[]{:S(2)}, u32[]{:S(2)}) collective-permute-start(bf16[512,256]{1,0:T(8,128)(2,1)S(1)} %get-tuple-element.24), channel_id=1, source_target_pairs={{0,16},{16,0},{1,17},{17,1},{2,18},{18,2},{3,19},{19,3},{4,20},{20... | collective-permute-start | bytes 786440 | tf_op jit(solution)/shard_map/ppermute | solution.py:381
  11.6 0.0 copy-done
  11.6 0.1 reshape.24.base_ref
  11.7 1.5 %own_tables.1 = (bf16[512,1024]{1,0:T(8,128)(2,1)S(1)}, f32[512,256]{1,0:T(8,128)S(1)}, f32[256,64]{1,0:T(8,128)S(1)}, f32[8,64]{1,0:T(8,128)S(1)}, f32[1,256]{1,0:T(1,128)S(1)}) custom-call(f32[128,8]{1,0:T(8,128)S(1)} %get-tuple-element.19.own_row_ref, f32[8,512]{1,0:T(8,128)S(1)} %get-tuple-element.20.grid_ref, ...), custom_call_target="tpu_custom_call" | custom-call | tf_op jit(solution)/shard_map/own_tables/pallas_call | solution.py:223
  13.2 0.0 collective-permute-done
  13.2 0.1 add_convert_fusion
  13.3 16.3 %all_to_all.15.parts_ref = bf16[16,32,256]{2,1,0:T(8,128)(2,1)S(1)} all-to-all(bf16[16,32,256]{2,1,0:T(8,128)(2,1)S(1)} %bitcast.7), channel_id=1, replica_groups={{288,0,448,64,384,32,128,320,480,96,192,416,160,256,352,224},{289,1,449..., dimensions={0} | all-to-all | bytes 524288 | tf_op jit(solution)/shard_map/all_to_all | solution.py:368
  29.5 0.3 occupancy.1
  29.8 10.7 %all_to_all.16.parts_ref = f32[16,2,128]{2,1,0:T(2,128)S(1)} all-to-all(f32[16,2,128]{2,1,0:T(2,128)S(1)} %get-tuple-element.26), channel_id=1, replica_groups={{12,0,1,7,8,15,2,6,9,14,3,5,10,13,4,11},{28,16,17,23,24,31,18,22,25,30,..., dimensions={0} | all-to-all | bytes 32768 | tf_op jit(solution)/shard_map/all_to_all | solution.py:368
  40.5 0.4 weigh.1
  40.9 16.1 %all_to_all.17 = bf16[16,32,256]{2,1,0:T(8,128)(2,1)S(1)} all-to-all(bf16[16,32,256]{2,1,0:T(8,128)(2,1)S(1)} %get-tuple-element.30), channel_id=1, replica_groups={{288,0,448,64,384,32,128,320,480,96,192,416,160,256,352,224},{289,1,449..., dimensions={0} | all-to-all | bytes 524288 | tf_op jit(solution)/shard_map/all_to_all | solution.py:368
  57.0 3.7 %collective-permute-start.1 = (bf16[512,256]{1,0:T(8,128)(2,1)S(1)}, bf16[512,256]{1,0:T(8,128)(2,1)S(1)}, u32[]{:S(2)}, u32[]{:S(2)}) collective-permute-start(bf16[512,256]{1,0:T(8,128)(2,1)S(1)} %bitcast.5), channel_id=1, source_target_pairs={{0,16},{16,0},{1,17},{17,1},{2,18},{18,2},{3,19},{19,3},{4,20},{20... | collective-permute-start | bytes 786440 | tf_op jit(solution)/shard_map/ppermute | solution.py:391
  60.6 0.8 %back.1 = (f32[512,256]{1,0:T(8,128)S(1)}, bf16[2,512,512]{2,1,0:T(8,128)(2,1)S(1)}, f32[4,8,8]{2,1,0:T(8,128)}) custom-call(bf16[512,1024]{1,0:T(8,128)(2,1)S(1)} %get-tuple-element.22.table_ref, bf16[512,256]{1,0:T(8,128)(2,1)S(1)} %bitcast.6, bf16[512,1024]{1,0:T(8,128)(2,1)S(1)} %get-tuple-element.31.other_ref, f32[8,64]{1,0:T(8,128)S(1)} %get-tuple-element.32.onsite_ref), custom_call_target="tpu_custom_call" | custom-call | tf_op jit(solution)/shard_map/back/pallas_call | solution.py:321
  61.5 0.3 collective-permute-done.1.weighted_ref
  61.8 1.1 %back_last.1 = bf16[2,512,128]{2,1,0:T(8,128)(2,1)} custom-call(bf16[2,512,512]{2,1,0:T(8,128)(2,1)S(1)} %get-tuple-element.33.table_ref, bf16[512,256]{1,0:T(8,128)(2,1)S(1)} %collective-permute-done.1.weighted_ref, f32[512,256]{1,0:T(8,128)S(1)} %get-tuple-element.34.before_ref), custom_call_target="tpu_custom_call" | custom-call | tf_op jit(solution)/shard_map/back_last/pallas_call | solution.py:349
Async XLA Ops:
  0.6 11.0 %copy-start = (f32[4,8,8]{2,1,0:T(8,128)S(1)}, f32[4,8,8]{2,1,0:T(8,128)}, u32[]{:S(2)}) copy-start(f32[4,8,8]{2,1,0:T(8,128)} %param.17) | copy-start | bytes 3076
  2.8 10.3 %collective-permute-start = (bf16[512,256]{1,0:T(8,128)(2,1)S(1)}, bf16[512,256]{1,0:T(8,128)(2,1)S(1)}, u32[]{:S(2)}, u32[]{:S(2)}) collective-permute-start(bf16[512,256]{1,0:T(8,128)(2,1)S(1)} %get-tuple-element.24), channel_id=1, source_target_pairs={{0,16},{16,0},{1,17},{17,1},{2,18},{18,2},{3,19},{19,3},{4,20},{20... | collective-permute-start | bytes 786440 | tf_op jit(solution)/shard_map/ppermute | solution.py:381
  57.0 4.8 %collective-permute-start.1 = (bf16[512,256]{1,0:T(8,128)(2,1)S(1)}, bf16[512,256]{1,0:T(8,128)(2,1)S(1)}, u32[]{:S(2)}, u32[]{:S(2)}) collective-permute-start(bf16[512,256]{1,0:T(8,128)(2,1)S(1)} %bitcast.5), channel_id=1, source_target_pairs={{0,16},{16,0},{1,17},{17,1},{2,18},{18,2},{3,19},{19,3},{4,20},{20... | collective-permute-start | bytes 786440 | tf_op jit(solution)/shard_map/ppermute | solution.py:391

commit v7 on v6

--- a/solution.py
+++ b/solution.py
@@ -12,8 +12,8 @@
 HIGH = lax.Precision.HIGHEST
 F32 = jnp.float32
 BF16 = jnp.bfloat16
-OTHER_ENDS = (8, 14, 16)
-OWN_ENDS = (12, 16)
+OTHER_ENDS = (10, 16)
+OWN_ENDS = (14, 16)
 CHUNKS = 4
 SIN = (6.283185005187988, -41.341590881347656, 81.59994506835938,
        -76.61447143554688, 41.3428840637207, -12.471243858337402)
@@ -87,13 +87,19 @@
     first1 = iota((8, 1), 0) < 4
     for q, chip in enumerate(owners):
         par = by_row[chip * 8:chip * 8 + 8, :]
+        if q % 2 == 0:
+            here = [par[:, k:k + 1] for k in range(3)]
+            after = by_row[owners[q + 1] * 8:owners[q + 1] * 8 + 8, :]
+            spot = [jnp.where(first1, here[k], after[:, k:k + 1]) for k in range(3)]
+            turns = spot[0] * m[0] + spot[1] * m[1] + spot[2] * m[2]
+            r = turns - jnp.round(turns)
+            z = r * r
+            both = [(v, pltpu.roll(v, 4, 0)) for v in (horner(SIN, z) * r, horner(COS, z))]
+            sin, cos = (jnp.where(first, v, turned) for v, turned in both)
+        else:
+            sin, cos = (jnp.where(first, turned, v) for v, turned in both)
+        minus_sin = -sin
         col = [par[:, k:k + 1] for k in range(7)]
-        turns = col[0] * m[0] + col[1] * m[1] + col[2] * m[2]
-        r = turns - jnp.round(turns)
-        z = r * r
-        sin = horner(SIN, z) * r
-        cos = horner(COS, z)
-        minus_sin = -sin
         pair_w = (jnp.where(first1, col[3], col[4]), col[5], jnp.where(first1, col[5], col[6]), col[6])
         re, im = [], []
         for p in range(4):

time: 63.2 us -> 63.1 us (level)
  no operation moved by 1% of the time
where the time goes in v7:
time: 63.1 us; the launch traced here: 62.8 us
  blocking collectives  43 us (68%)
  starting transfers between devices  12.5 us (20%)
  Pallas kernels  6.1 us (10%)
  between operations  0.72 us (1%)
    all_to_all x3, blocking collectives, exchange(): lax.all_to_all(blocks, axis, 0, 0, axis_index_groups=[members], tiled=True)  43 us
    ppermute x1, starting transfers between devices, local(): received = lax.ppermute(other_proj, 'core', swap)  8.79 us
    ppermute x1, starting transfers between devices, local(): other_weighted = lax.ppermute(weighted, 'core', swap)  3.66 us
    pallas_call x1, Pallas kernels, other_tables(): pl.pallas_call(functools.partial(other_tables_kernel, owners), out_shape=...  2.08 us
    pallas_call x1, Pallas kernels, own_tables(): pl.pallas_call(functools.partial(own_tables_kernel, bands, owners), out_s...  1.42 us
  transfers between devices with their start and end apart: 2, of which 1 were waited for; matrix products, arithmetic and copies ran while one was open for 0% of the time, Pallas kernels for 4%

profile of v7, /device:TPU:1, one launch (start us, length us, event | category | flops | bytes accessed | tf_op | source)
XLA Modules:
  0.0 62.8 jit_solution(16320323456186647809)
XLA Ops:
  0.6 0.0 copy-start
  0.6 2.1 %other_tables.1 = (bf16[512,1024]{1,0:T(8,128)(2,1)S(1)}, bf16[512,256]{1,0:T(8,128)(2,1)S(1)}, f32[128,8]{1,0:T(8,128)S(1)}, f32[8,512]{1,0:T(8,128)S(1)}, bf16[512,256]{1,0:T(8,128)(2,1)S(1)}) custom-call(f32[3,3]{1,0:T(4,128)} %recip_hbm.1, f32[4,4]{1,0:T(4,128)} %widths_hbm.1, bf16[2,512,128]{2,1,0:T(8,128)(2,1)} %wave_hbm.1, s32[3,512]{1,0:T(4,128)} %miller_hbm.1, ...), custom_call_target="tpu_custom_call" | custom-call | tf_op jit(solution)/shard_map/other_tables/pallas_call | solution.py:183
  2.7 8.8 %collective-permute-start = (bf16[512,256]{1,0:T(8,128)(2,1)S(1)}, bf16[512,256]{1,0:T(8,128)(2,1)S(1)}, u32[]{:S(2)}, u32[]{:S(2)}) collective-permute-start(bf16[512,256]{1,0:T(8,128)(2,1)S(1)} %get-tuple-element.24), channel_id=1, source_target_pairs={{0,16},{16,0},{1,17},{17,1},{2,18},{18,2},{3,19},{19,3},{4,20},{20... | collective-permute-start | bytes 786440 | tf_op jit(solution)/shard_map/ppermute | solution.py:387
  11.5 0.0 copy-done
  11.5 0.1 reshape.24.base_ref
  11.6 1.4 %own_tables.1 = (bf16[512,1024]{1,0:T(8,128)(2,1)S(1)}, f32[512,256]{1,0:T(8,128)S(1)}, f32[256,64]{1,0:T(8,128)S(1)}, f32[8,64]{1,0:T(8,128)S(1)}, f32[1,256]{1,0:T(1,128)S(1)}) custom-call(f32[128,8]{1,0:T(8,128)S(1)} %get-tuple-element.19.own_row_ref, f32[8,512]{1,0:T(8,128)S(1)} %get-tuple-element.20.grid_ref, ...), custom_call_target="tpu_custom_call" | custom-call | tf_op jit(solution)/shard_map/own_tables/pallas_call | solution.py:229
  13.0 0.0 collective-permute-done
  13.1 0.1 add_convert_fusion
  13.1 16.3 %all_to_all.15.parts_ref = bf16[16,32,256]{2,1,0:T(8,128)(2,1)S(1)} all-to-all(bf16[16,32,256]{2,1,0:T(8,128)(2,1)S(1)} %bitcast.7), channel_id=1, replica_groups={{288,0,448,64,384,32,128,320,480,96,192,416,160,256,352,224},{289,1,449..., dimensions={0} | all-to-all | bytes 524288 | tf_op jit(solution)/shard_map/all_to_all | solution.py:374
  29.4 0.3 occupancy.1
  29.7 10.7 %all_to_all.16.parts_ref = f32[16,2,128]{2,1,0:T(2,128)S(1)} all-to-all(f32[16,2,128]{2,1,0:T(2,128)S(1)} %get-tuple-element.26), channel_id=1, replica_groups={{12,0,1,7,8,15,2,6,9,14,3,5,10,13,4,11},{28,16,17,23,24,31,18,22,25,30,..., dimensions={0} | all-to-all | bytes 32768 | tf_op jit(solution)/shard_map/all_to_all | solution.py:374
  40.4 0.4 weigh.1
  40.8 16.1 %all_to_all.17 = bf16[16,32,256]{2,1,0:T(8,128)(2,1)S(1)} all-to-all(bf16[16,32,256]{2,1,0:T(8,128)(2,1)S(1)} %get-tuple-element.30), channel_id=1, replica_groups={{288,0,448,64,384,32,128,320,480,96,192,416,160,256,352,224},{289,1,449..., dimensions={0} | all-to-all | bytes 524288 | tf_op jit(solution)/shard_map/all_to_all | solution.py:374
  56.8 3.7 %collective-permute-start.1 = (bf16[512,256]{1,0:T(8,128)(2,1)S(1)}, bf16[512,256]{1,0:T(8,128)(2,1)S(1)}, u32[]{:S(2)}, u32[]{:S(2)}) collective-permute-start(bf16[512,256]{1,0:T(8,128)(2,1)S(1)} %bitcast.5), channel_id=1, source_target_pairs={{0,16},{16,0},{1,17},{17,1},{2,18},{18,2},{3,19},{19,3},{4,20},{20... | collective-permute-start | bytes 786440 | tf_op jit(solution)/shard_map/ppermute | solution.py:397
  60.5 0.8 %back.1 = (f32[512,256]{1,0:T(8,128)S(1)}, bf16[2,512,512]{2,1,0:T(8,128)(2,1)S(1)}, f32[4,8,8]{2,1,0:T(8,128)}) custom-call(bf16[512,1024]{1,0:T(8,128)(2,1)S(1)} %get-tuple-element.22.table_ref, bf16[512,256]{1,0:T(8,128)(2,1)S(1)} %bitcast.6, bf16[512,1024]{1,0:T(8,128)(2,1)S(1)} %get-tuple-element.31.other_ref, f32[8,64]{1,0:T(8,128)S(1)} %get-tuple-element.32.onsite_ref), custom_call_target="tpu_custom_call" | custom-call | tf_op jit(solution)/shard_map/back/pallas_call | solution.py:327
  61.3 0.3 collective-permute-done.1.weighted_ref
  61.7 1.1 %back_last.1 = bf16[2,512,128]{2,1,0:T(8,128)(2,1)} custom-call(bf16[2,512,512]{2,1,0:T(8,128)(2,1)S(1)} %get-tuple-element.33.table_ref, bf16[512,256]{1,0:T(8,128)(2,1)S(1)} %collective-permute-done.1.weighted_ref, f32[512,256]{1,0:T(8,128)S(1)} %get-tuple-element.34.before_ref), custom_call_target="tpu_custom_call" | custom-call | tf_op jit(solution)/shard_map/back_last/pallas_call | solution.py:355
Async XLA Ops:
  0.6 10.9 %copy-start = (f32[4,8,8]{2,1,0:T(8,128)S(1)}, f32[4,8,8]{2,1,0:T(8,128)}, u32[]{:S(2)}) copy-start(f32[4,8,8]{2,1,0:T(8,128)} %param.17) | copy-start | bytes 3076
  2.7 10.3 %collective-permute-start = (bf16[512,256]{1,0:T(8,128)(2,1)S(1)}, bf16[512,256]{1,0:T(8,128)(2,1)S(1)}, u32[]{:S(2)}, u32[]{:S(2)}) collective-permute-start(bf16[512,256]{1,0:T(8,128)(2,1)S(1)} %get-tuple-element.24), channel_id=1, source_target_pairs={{0,16},{16,0},{1,17},{17,1},{2,18},{18,2},{3,19},{19,3},{4,20},{20... | collective-permute-start | bytes 786440 | tf_op jit(solution)/shard_map/ppermute | solution.py:387
  56.8 4.8 %collective-permute-start.1 = (bf16[512,256]{1,0:T(8,128)(2,1)S(1)}, bf16[512,256]{1,0:T(8,128)(2,1)S(1)}, u32[]{:S(2)}, u32[]{:S(2)}) collective-permute-start(bf16[512,256]{1,0:T(8,128)(2,1)S(1)} %bitcast.5), channel_id=1, source_target_pairs={{0,16},{16,0},{1,17},{17,1},{2,18},{18,2},{3,19},{19,3},{4,20},{20... | collective-permute-start | bytes 786440 | tf_op jit(solution)/shard_map/ppermute | solution.py:397

commit v8 on v7

--- a/solution.py
+++ b/solution.py
@@ -129,9 +129,10 @@
 def other_tables_kernel(owners, recip_hbm, widths_hbm, wave_hbm, miller_hbm, frac_hbm, species_hbm, order_hbm,
                         beta_ref, proj_ref, own_row_ref, grid_ref, rhs_ref,
                         recip_ref, widths_ref, wave_ref, miller_ref, frac_ref, species_ref, order_ref, copied):
-    loads = fetch(((wave_hbm, wave_ref), (recip_hbm, recip_ref), (widths_hbm, widths_ref), (miller_hbm, miller_ref),
-                   (frac_hbm, frac_ref), (species_hbm, species_ref), (order_hbm, order_ref)), copied)
-    for load in loads[1:]:
+    *loads, wave_load = fetch(
+        ((order_hbm, order_ref), (species_hbm, species_ref), (widths_hbm, widths_ref), (frac_hbm, frac_ref),
+         (recip_hbm, recip_ref), (miller_hbm, miller_ref), (wave_hbm, wave_ref)), copied)
+    for load in loads:
         load.wait()
     core = lax.axis_index("core")
     gcount = miller_ref.shape[1]
@@ -167,7 +168,7 @@
     grid_ref[...] = jnp.concatenate([*m, *g, g2, g2], axis=0)
 
     def make_rhs():
-        loads[0].wait()
+        wave_load.wait()
         nb = wave_ref.shape[2]
         rhs_ref[:, :nb] = wave_ref[0]
         rhs_ref[:, nb:] = wave_ref[1]
@@ -380,8 +381,8 @@
     bands = lax.axis_size("band")
     swap = [(0, 1), (1, 0)]
     nb = wavefunctions.shape[2]
-    owners = farthest_first([(i // 2, i % 2 * 2) for i in range(chips)], (chips // 2, 4), chips // 2 + 1)
-    blocks = farthest_first([(i % (bands // 2), i * 2 // bands) for i in range(bands)], (bands // 2, 4), bands * 3 // 4)
+    owners = farthest_first([(i // 2, i % 2 * 2) for i in range(chips)], (chips // 2, 4), chips * 3 // 4 + 1)
+    blocks = farthest_first([(i % (bands // 2), i * 2 // bands) for i in range(bands)], (bands // 2, 4), bands * 3 // 4 + 1)
     other, other_proj, own_row, grid, rhs = other_tables(
         owners, wavefunctions, miller, reciprocal, fractional, species, atom_order, radial_widths)
     received = lax.ppermute(other_proj, "core", swap)

time: 63.1 us -> 62.9 us (level)
  blocking collectives: 43 us -> 41.4 us
  starting transfers between devices: 12.5 us -> 13.9 us
    all_to_all x3, blocking collectives: 43 us -> 41.4 us  [exchange(): lax.all_to_all(blocks, axis, 0, 0, axis_index_groups=[members], tiled=True)]
    ppermute x1, starting transfers between devices: 3.66 us -> 5.14 us  [local(): other_weighted = lax.ppermute(weighted, 'core', swap)]
where the time goes in v8:
time: 62.9 us; the launch traced here: 62.6 us
  blocking collectives  41.4 us (66%)
  starting transfers between devices  13.9 us (22%)
  Pallas kernels  6.06 us (10%)
  between operations  0.72 us (1%)
    all_to_all x3, blocking collectives, exchange(): lax.all_to_all(blocks, axis, 0, 0, axis_index_groups=[members], tiled=True)  41.4 us
    ppermute x1, starting transfers between devices, local(): received = lax.ppermute(other_proj, 'core', swap)  8.79 us
    ppermute x1, starting transfers between devices, local(): other_weighted = lax.ppermute(weighted, 'core', swap)  5.14 us
    pallas_call x1, Pallas kernels, other_tables(): pl.pallas_call(functools.partial(other_tables_kernel, owners), out_shape=...  2.04 us
    pallas_call x1, Pallas kernels, own_tables(): pl.pallas_call(functools.partial(own_tables_kernel, bands, owners), out_s...  1.43 us
  transfers between devices with their start and end apart: 2, of which 1 were waited for; matrix products, arithmetic and copies ran while one was open for 0% of the time, Pallas kernels for 4%

profile of v8, /device:TPU:1, one launch (start us, length us, event | category | flops | bytes accessed | tf_op | source)
XLA Modules:
  0.0 62.6 jit_solution(15873022505830391132)
XLA Ops:
  0.6 0.0 copy-start
  0.6 2.0 %other_tables.1 = (bf16[512,1024]{1,0:T(8,128)(2,1)S(1)}, bf16[512,256]{1,0:T(8,128)(2,1)S(1)}, f32[128,8]{1,0:T(8,128)S(1)}, f32[8,512]{1,0:T(8,128)S(1)}, bf16[512,256]{1,0:T(8,128)(2,1)S(1)}) custom-call(f32[3,3]{1,0:T(4,128)} %recip_hbm.1, f32[4,4]{1,0:T(4,128)} %widths_hbm.1, bf16[2,512,128]{2,1,0:T(8,128)(2,1)} %wave_hbm.1, s32[3,512]{1,0:T(4,128)} %miller_hbm.1, ...), custom_call_target="tpu_custom_call" | custom-call | tf_op jit(solution)/shard_map/other_tables/pallas_call | solution.py:184
  2.7 8.8 %collective-permute-start = (bf16[512,256]{1,0:T(8,128)(2,1)S(1)}, bf16[512,256]{1,0:T(8,128)(2,1)S(1)}, u32[]{:S(2)}, u32[]{:S(2)}) collective-permute-start(bf16[512,256]{1,0:T(8,128)(2,1)S(1)} %get-tuple-element.24), channel_id=1, source_target_pairs={{0,16},{16,0},{1,17},{17,1},{2,18},{18,2},{3,19},{19,3},{4,20},{20... | collective-permute-start | bytes 786440 | tf_op jit(solution)/shard_map/ppermute | solution.py:388
  11.5 0.0 copy-done
  11.5 0.1 reshape.24.base_ref
  11.6 1.4 %own_tables.1 = (bf16[512,1024]{1,0:T(8,128)(2,1)S(1)}, f32[512,256]{1,0:T(8,128)S(1)}, f32[256,64]{1,0:T(8,128)S(1)}, f32[8,64]{1,0:T(8,128)S(1)}, f32[1,256]{1,0:T(1,128)S(1)}) custom-call(f32[128,8]{1,0:T(8,128)S(1)} %get-tuple-element.19.own_row_ref, f32[8,512]{1,0:T(8,128)S(1)} %get-tuple-element.20.grid_ref, ...), custom_call_target="tpu_custom_call" | custom-call | tf_op jit(solution)/shard_map/own_tables/pallas_call | solution.py:230
  13.0 0.0 collective-permute-done
  13.0 0.1 add_convert_fusion
  13.1 16.0 %all_to_all.15.parts_ref = bf16[16,32,256]{2,1,0:T(8,128)(2,1)S(1)} all-to-all(bf16[16,32,256]{2,1,0:T(8,128)(2,1)S(1)} %bitcast.7), channel_id=1, replica_groups={{416,128,64,192,0,160,256,448,96,224,320,32,288,384,480,352},{417,129,6..., dimensions={0} | all-to-all | bytes 524288 | tf_op jit(solution)/shard_map/all_to_all | solution.py:375
  29.1 0.3 occupancy.1
  29.3 10.6 %all_to_all.16.parts_ref = f32[16,2,128]{2,1,0:T(2,128)S(1)} all-to-all(f32[16,2,128]{2,1,0:T(2,128)S(1)} %get-tuple-element.26), channel_id=1, replica_groups={{13,1,0,2,9,3,7,8,10,15,4,6,11,14,5,12},{29,17,16,18,25,19,23,24,26,31,..., dimensions={0} | all-to-all | bytes 32768 | tf_op jit(solution)/shard_map/all_to_all | solution.py:375
  39.9 0.4 weigh.1
  40.3 14.8 %all_to_all.17 = bf16[16,32,256]{2,1,0:T(8,128)(2,1)S(1)} all-to-all(bf16[16,32,256]{2,1,0:T(8,128)(2,1)S(1)} %get-tuple-element.30), channel_id=1, replica_groups={{416,128,64,192,0,160,256,448,96,224,320,32,288,384,480,352},{417,129,6..., dimensions={0} | all-to-all | bytes 524288 | tf_op jit(solution)/shard_map/all_to_all | solution.py:375
  55.2 5.1 %collective-permute-start.1 = (bf16[512,256]{1,0:T(8,128)(2,1)S(1)}, bf16[512,256]{1,0:T(8,128)(2,1)S(1)}, u32[]{:S(2)}, u32[]{:S(2)}) collective-permute-start(bf16[512,256]{1,0:T(8,128)(2,1)S(1)} %bitcast.5), channel_id=1, source_target_pairs={{0,16},{16,0},{1,17},{17,1},{2,18},{18,2},{3,19},{19,3},{4,20},{20... | collective-permute-start | bytes 786440 | tf_op jit(solution)/shard_map/ppermute | solution.py:398
  60.3 0.8 %back.1 = (f32[512,256]{1,0:T(8,128)S(1)}, bf16[2,512,512]{2,1,0:T(8,128)(2,1)S(1)}, f32[4,8,8]{2,1,0:T(8,128)}) custom-call(bf16[512,1024]{1,0:T(8,128)(2,1)S(1)} %get-tuple-element.22.table_ref, bf16[512,256]{1,0:T(8,128)(2,1)S(1)} %bitcast.6, bf16[512,1024]{1,0:T(8,128)(2,1)S(1)} %get-tuple-element.31.other_ref, f32[8,64]{1,0:T(8,128)S(1)} %get-tuple-element.32.onsite_ref), custom_call_target="tpu_custom_call" | custom-call | tf_op jit(solution)/shard_map/back/pallas_call | solution.py:328
  61.1 0.3 collective-permute-done.1.weighted_ref
  61.5 1.1 %back_last.1 = bf16[2,512,128]{2,1,0:T(8,128)(2,1)} custom-call(bf16[2,512,512]{2,1,0:T(8,128)(2,1)S(1)} %get-tuple-element.33.table_ref, bf16[512,256]{1,0:T(8,128)(2,1)S(1)} %collective-permute-done.1.weighted_ref, f32[512,256]{1,0:T(8,128)S(1)} %get-tuple-element.34.before_ref), custom_call_target="tpu_custom_call" | custom-call | tf_op jit(solution)/shard_map/back_last/pallas_call | solution.py:356
Async XLA Ops:
  0.6 10.9 %copy-start = (f32[4,8,8]{2,1,0:T(8,128)S(1)}, f32[4,8,8]{2,1,0:T(8,128)}, u32[]{:S(2)}) copy-start(f32[4,8,8]{2,1,0:T(8,128)} %param.17) | copy-start | bytes 3076
  2.7 10.3 %collective-permute-start = (bf16[512,256]{1,0:T(8,128)(2,1)S(1)}, bf16[512,256]{1,0:T(8,128)(2,1)S(1)}, u32[]{:S(2)}, u32[]{:S(2)}) collective-permute-start(bf16[512,256]{1,0:T(8,128)(2,1)S(1)} %get-tuple-element.24), channel_id=1, source_target_pairs={{0,16},{16,0},{1,17},{17,1},{2,18},{18,2},{3,19},{19,3},{4,20},{20... | collective-permute-start | bytes 786440 | tf_op jit(solution)/shard_map/ppermute | solution.py:388
  55.2 6.3 %collective-permute-start.1 = (bf16[512,256]{1,0:T(8,128)(2,1)S(1)}, bf16[512,256]{1,0:T(8,128)(2,1)S(1)}, u32[]{:S(2)}, u32[]{:S(2)}) collective-permute-start(bf16[512,256]{1,0:T(8,128)(2,1)S(1)} %bitcast.5), channel_id=1, source_target_pairs={{0,16},{16,0},{1,17},{17,1},{2,18},{18,2},{3,19},{19,3},{4,20},{20... | collective-permute-start | bytes 786440 | tf_op jit(solution)/shard_map/ppermute | solution.py:398

commit v9 on v8

--- a/solution.py
+++ b/solution.py
@@ -195,10 +195,10 @@
     )(*(in_hbm(a) for a in args))
 
 
-def own_tables_kernel(bands, owners, own_row_ref, grid_ref, rhs_ref, base_ref, coupling_hbm, occupations_hbm,
+def own_tables_kernel(bands, owners, own_row_ref, grid_ref, rhs_ref, base_hbm, coupling_hbm, occupations_hbm,
                       beta_ref, proj_ref, couple_ref, base_rows_ref, weights_ref,
-                      coupling_ref, occupations_ref, copied):
-    loads = fetch(((coupling_hbm, coupling_ref), (occupations_hbm, occupations_ref)), copied)
+                      base_ref, coupling_ref, occupations_ref, copied):
+    loads = fetch(((coupling_hbm, coupling_ref), (occupations_hbm, occupations_ref), (base_hbm, base_ref)), copied)
     chip = lax.axis_index("chip")
 
     def of_owned_atoms():
@@ -206,9 +206,10 @@
             load.wait()
         spec = own_row_ref[pl.ds(pl.multiple_of(chip * 8, 8), 8), 7:8]
         kinds = base_ref.shape[0]
-        base = jnp.broadcast_to(base_ref[0:1, :], (8, 64))
+        flat = [jnp.concatenate([base_ref[s, i:i + 1, :] for i in range(8)], axis=1) for s in range(kinds)]
+        base = jnp.broadcast_to(flat[0], (8, 64))
         for s in range(1, kinds):
-            base = jnp.where(spec == s, base_ref[s:s + 1, :], base)
+            base = jnp.where(spec == s, flat[s], base)
         base_rows_ref[...] = base
         by_kind = [coupling_ref[s].T for s in range(kinds)]
         for a in range(4):
@@ -232,13 +233,13 @@
         out_shape=(jax.ShapeDtypeStruct((nrows, 2 * rhs.shape[0]), BF16), jax.ShapeDtypeStruct((nrows, rhs.shape[1]), F32),
                    jax.ShapeDtypeStruct((256, 64), F32), jax.ShapeDtypeStruct((8, 64), F32),
                    jax.ShapeDtypeStruct((1, rhs.shape[1]), F32)),
-        in_specs=[vmem()] * 4 + [hbm()] * 2,
+        in_specs=[vmem()] * 3 + [hbm()] * 3,
         out_specs=(vmem(),) * 5,
-        scratch_shapes=[pltpu.VMEM(coupling.shape, F32), pltpu.VMEM(occupations.shape, F32),
-                        pltpu.SemaphoreType.DMA((2,))],
+        scratch_shapes=[pltpu.VMEM(base.shape, F32), pltpu.VMEM(coupling.shape, F32),
+                        pltpu.VMEM(occupations.shape, F32), pltpu.SemaphoreType.DMA((3,))],
         compiler_params=LIMIT,
         name="own_tables",
-    )(own_row, grid, rhs, base, in_hbm(coupling), in_hbm(occupations))
+    )(own_row, grid, rhs, in_hbm(base), in_hbm(coupling), in_hbm(occupations))
 
 
 def occupancy_kernel(parts_ref, weights_ref, proj_ref, send_ref):
@@ -387,7 +388,7 @@
         owners, wavefunctions, miller, reciprocal, fractional, species, atom_order, radial_widths)
     received = lax.ppermute(other_proj, "core", swap)
     mine, mine_proj, couple, base_rows, weights = own_tables(
-        bands, owners, own_row, grid, rhs, onsite_base.reshape(-1, 64), coupling, occupations.reshape(1, -1))
+        bands, owners, own_row, grid, rhs, onsite_base, coupling, occupations.reshape(1, -1))
     chip_sum = (mine_proj + received.astype(F32)).astype(BF16).reshape(chips, -1, 2 * nb)
     parts = exchange(chip_sum, "chip", owners)
 

time: 62.9 us -> 62.8 us (level)
  no operation moved by 1% of the time
where the time goes in v9:
time: 62.8 us; the launch traced here: 62.5 us
  blocking collectives  41.4 us (66%)
  starting transfers between devices  13.9 us (22%)
  Pallas kernels  6.07 us (10%)
  between operations  0.7 us (1%)
    all_to_all x3, blocking collectives, exchange(): lax.all_to_all(blocks, axis, 0, 0, axis_index_groups=[members], tiled=True)  41.4 us
    ppermute x1, starting transfers between devices, local(): received = lax.ppermute(other_proj, 'core', swap)  8.79 us
    ppermute x1, starting transfers between devices, local(): other_weighted = lax.ppermute(weighted, 'core', swap)  5.15 us
    pallas_call x1, Pallas kernels, other_tables(): pl.pallas_call(functools.partial(other_tables_kernel, owners), out_shape=...  2.05 us
    pallas_call x1, Pallas kernels, own_tables(): pl.pallas_call(functools.partial(own_tables_kernel, bands, owners), out_s...  1.43 us
  transfers between devices with their start and end apart: 2, of which 1 were waited for; matrix products, arithmetic and copies ran while one was open for 0% of the time, Pallas kernels for 4%

profile of v9, /device:TPU:1, one launch (start us, length us, event | category | flops | bytes accessed | tf_op | source)
XLA Modules:
  0.0 62.5 jit_solution(7501268944718393704)
XLA Ops:
  0.6 2.0 %other_tables.1 = (bf16[512,1024]{1,0:T(8,128)(2,1)S(1)}, bf16[512,256]{1,0:T(8,128)(2,1)S(1)}, f32[128,8]{1,0:T(8,128)S(1)}, f32[8,512]{1,0:T(8,128)S(1)}, bf16[512,256]{1,0:T(8,128)(2,1)S(1)}) custom-call(f32[3,3]{1,0:T(4,128)} %recip_hbm.1, f32[4,4]{1,0:T(4,128)} %widths_hbm.1, bf16[2,512,128]{2,1,0:T(8,128)(2,1)} %wave_hbm.1, s32[3,512]{1,0:T(4,128)} %miller_hbm.1, ...), custom_call_target="tpu_custom_call" | custom-call | tf_op jit(solution)/shard_map/other_tables/pallas_call | solution.py:184
  2.7 8.8 %collective-permute-start = (bf16[512,256]{1,0:T(8,128)(2,1)S(1)}, bf16[512,256]{1,0:T(8,128)(2,1)S(1)}, u32[]{:S(2)}, u32[]{:S(2)}) collective-permute-start(bf16[512,256]{1,0:T(8,128)(2,1)S(1)} %get-tuple-element.24), channel_id=1, source_target_pairs={{0,16},{16,0},{1,17},{17,1},{2,18},{18,2},{3,19},{19,3},{4,20},{20... | collective-permute-start | bytes 786440 | tf_op jit(solution)/shard_map/ppermute | solution.py:389
  11.5 1.4 %own_tables.1 = (bf16[512,1024]{1,0:T(8,128)(2,1)S(1)}, f32[512,256]{1,0:T(8,128)S(1)}, f32[256,64]{1,0:T(8,128)S(1)}, f32[8,64]{1,0:T(8,128)S(1)}, f32[1,256]{1,0:T(1,128)S(1)}) custom-call(f32[128,8]{1,0:T(8,128)S(1)} %get-tuple-element.19.own_row_ref, f32[8,512]{1,0:T(8,128)S(1)} %get-tuple-element.20.grid_ref, ...), custom_call_target="tpu_custom_call" | custom-call | tf_op jit(solution)/shard_map/own_tables/pallas_call | solution.py:231
  12.9 0.0 collective-permute-done
  12.9 0.1 add_convert_fusion
  13.0 15.9 %all_to_all.15.parts_ref = bf16[16,32,256]{2,1,0:T(8,128)(2,1)S(1)} all-to-all(bf16[16,32,256]{2,1,0:T(8,128)(2,1)S(1)} %bitcast.7), channel_id=1, replica_groups={{416,128,64,192,0,160,256,448,96,224,320,32,288,384,480,352},{417,129,6..., dimensions={0} | all-to-all | bytes 524288 | tf_op jit(solution)/shard_map/all_to_all | solution.py:376
  28.9 0.3 occupancy.1
  29.2 10.6 %all_to_all.16.parts_ref = f32[16,2,128]{2,1,0:T(2,128)S(1)} all-to-all(f32[16,2,128]{2,1,0:T(2,128)S(1)} %get-tuple-element.26), channel_id=1, replica_groups={{13,1,0,2,9,3,7,8,10,15,4,6,11,14,5,12},{29,17,16,18,25,19,23,24,26,31,..., dimensions={0} | all-to-all | bytes 32768 | tf_op jit(solution)/shard_map/all_to_all | solution.py:376
  39.8 0.4 weigh.1
  40.2 14.9 %all_to_all.17 = bf16[16,32,256]{2,1,0:T(8,128)(2,1)S(1)} all-to-all(bf16[16,32,256]{2,1,0:T(8,128)(2,1)S(1)} %get-tuple-element.30), channel_id=1, replica_groups={{416,128,64,192,0,160,256,448,96,224,320,32,288,384,480,352},{417,129,6..., dimensions={0} | all-to-all | bytes 524288 | tf_op jit(solution)/shard_map/all_to_all | solution.py:376
  55.1 5.1 %collective-permute-start.1 = (bf16[512,256]{1,0:T(8,128)(2,1)S(1)}, bf16[512,256]{1,0:T(8,128)(2,1)S(1)}, u32[]{:S(2)}, u32[]{:S(2)}) collective-permute-start(bf16[512,256]{1,0:T(8,128)(2,1)S(1)} %bitcast.5), channel_id=1, source_target_pairs={{0,16},{16,0},{1,17},{17,1},{2,18},{18,2},{3,19},{19,3},{4,20},{20... | collective-permute-start | bytes 786440 | tf_op jit(solution)/shard_map/ppermute | solution.py:399
  60.2 0.8 %back.1 = (f32[512,256]{1,0:T(8,128)S(1)}, bf16[2,512,512]{2,1,0:T(8,128)(2,1)S(1)}, f32[4,8,8]{2,1,0:T(8,128)}) custom-call(bf16[512,1024]{1,0:T(8,128)(2,1)S(1)} %get-tuple-element.22.table_ref, bf16[512,256]{1,0:T(8,128)(2,1)S(1)} %bitcast.6, bf16[512,1024]{1,0:T(8,128)(2,1)S(1)} %get-tuple-element.31.other_ref, f32[8,64]{1,0:T(8,128)S(1)} %get-tuple-element.32.onsite_ref), custom_call_target="tpu_custom_call" | custom-call | tf_op jit(solution)/shard_map/back/pallas_call | solution.py:329
  61.0 0.3 collective-permute-done.1.weighted_ref
  61.4 1.1 %back_last.1 = bf16[2,512,128]{2,1,0:T(8,128)(2,1)} custom-call(bf16[2,512,512]{2,1,0:T(8,128)(2,1)S(1)} %get-tuple-element.33.table_ref, bf16[512,256]{1,0:T(8,128)(2,1)S(1)} %collective-permute-done.1.weighted_ref, f32[512,256]{1,0:T(8,128)S(1)} %get-tuple-element.34.before_ref), custom_call_target="tpu_custom_call" | custom-call | tf_op jit(solution)/shard_map/back_last/pallas_call | solution.py:357
Async XLA Ops:
  2.7 10.2 %collective-permute-start = (bf16[512,256]{1,0:T(8,128)(2,1)S(1)}, bf16[512,256]{1,0:T(8,128)(2,1)S(1)}, u32[]{:S(2)}, u32[]{:S(2)}) collective-permute-start(bf16[512,256]{1,0:T(8,128)(2,1)S(1)} %get-tuple-element.24), channel_id=1, source_target_pairs={{0,16},{16,0},{1,17},{17,1},{2,18},{18,2},{3,19},{19,3},{4,20},{20... | collective-permute-start | bytes 786440 | tf_op jit(solution)/shard_map/ppermute | solution.py:389
  55.1 6.3 %collective-permute-start.1 = (bf16[512,256]{1,0:T(8,128)(2,1)S(1)}, bf16[512,256]{1,0:T(8,128)(2,1)S(1)}, u32[]{:S(2)}, u32[]{:S(2)}) collective-permute-start(bf16[512,256]{1,0:T(8,128)(2,1)S(1)} %bitcast.5), channel_id=1, source_target_pairs={{0,16},{16,0},{1,17},{17,1},{2,18},{18,2},{3,19},{19,3},{4,20},{20... | collective-permute-start | bytes 786440 | tf_op jit(solution)/shard_map/ppermute | solution.py:399

commit v10 on v8

--- a/solution.py
+++ b/solution.py
@@ -12,8 +12,8 @@
 HIGH = lax.Precision.HIGHEST
 F32 = jnp.float32
 BF16 = jnp.bfloat16
-OTHER_ENDS = (10, 16)
-OWN_ENDS = (14, 16)
+OTHER_ENDS = (10, 14, 16)
+OWN_ENDS = (16,)
 CHUNKS = 4
 SIN = (6.283185005187988, -41.341590881347656, 81.59994506835938,
        -76.61447143554688, 41.3428840637207, -12.471243858337402)

time: 62.9 us -> 62.8 us (level)
  transfers between devices with their start and end apart: 2 -> 2, of which waited for: 1 -> 1; matrix products, arithmetic and copies ran while one was open for 0% -> 0% of each run, Pallas kernels for 4% -> 3%
where the time goes in v10:
time: 62.8 us; the launch traced here: 62.5 us
  blocking collectives  41.4 us (66%)
  starting transfers between devices  13.9 us (22%)
  Pallas kernels  6 us (10%)
  between operations  0.72 us (1%)
    all_to_all x3, blocking collectives, exchange(): lax.all_to_all(blocks, axis, 0, 0, axis_index_groups=[members], tiled=True)  41.4 us
    ppermute x1, starting transfers between devices, local(): received = lax.ppermute(other_proj, 'core', swap)  8.79 us
    ppermute x1, starting transfers between devices, local(): other_weighted = lax.ppermute(weighted, 'core', swap)  5.15 us
    pallas_call x1, Pallas kernels, other_tables(): pl.pallas_call(functools.partial(other_tables_kernel, owners), out_shape=...  2.03 us
    pallas_call x1, Pallas kernels, own_tables(): pl.pallas_call(functools.partial(own_tables_kernel, bands, owners), out_s...  1.38 us
  transfers between devices with their start and end apart: 2, of which 1 were waited for; matrix products, arithmetic and copies ran while one was open for 0% of the time, Pallas kernels for 3%

profile of v10, /device:TPU:1, one launch (start us, length us, event | category | flops | bytes accessed | tf_op | source)
XLA Modules:
  0.0 62.5 jit_solution(4129273788931619261)
XLA Ops:
  0.6 0.0 copy-start
  0.6 2.0 %other_tables.1 = (bf16[512,1024]{1,0:T(8,128)(2,1)S(1)}, bf16[512,256]{1,0:T(8,128)(2,1)S(1)}, f32[128,8]{1,0:T(8,128)S(1)}, f32[8,512]{1,0:T(8,128)S(1)}, bf16[512,256]{1,0:T(8,128)(2,1)S(1)}) custom-call(f32[3,3]{1,0:T(4,128)} %recip_hbm.1, f32[4,4]{1,0:T(4,128)} %widths_hbm.1, bf16[2,512,128]{2,1,0:T(8,128)(2,1)} %wave_hbm.1, s32[3,512]{1,0:T(4,128)} %miller_hbm.1, ...), custom_call_target="tpu_custom_call" | custom-call | tf_op jit(solution)/shard_map/other_tables/pallas_call | solution.py:184
  2.7 8.8 %collective-permute-start = (bf16[512,256]{1,0:T(8,128)(2,1)S(1)}, bf16[512,256]{1,0:T(8,128)(2,1)S(1)}, u32[]{:S(2)}, u32[]{:S(2)}) collective-permute-start(bf16[512,256]{1,0:T(8,128)(2,1)S(1)} %get-tuple-element.24), channel_id=1, source_target_pairs={{0,16},{16,0},{1,17},{17,1},{2,18},{18,2},{3,19},{19,3},{4,20},{20... | collective-permute-start | bytes 786440 | tf_op jit(solution)/shard_map/ppermute | solution.py:388
  11.5 0.0 copy-done
  11.5 0.1 reshape.24.base_ref
  11.6 1.4 %own_tables.1 = (bf16[512,1024]{1,0:T(8,128)(2,1)S(1)}, f32[512,256]{1,0:T(8,128)S(1)}, f32[256,64]{1,0:T(8,128)S(1)}, f32[8,64]{1,0:T(8,128)S(1)}, f32[1,256]{1,0:T(1,128)S(1)}) custom-call(f32[128,8]{1,0:T(8,128)S(1)} %get-tuple-element.19.own_row_ref, f32[8,512]{1,0:T(8,128)S(1)} %get-tuple-element.20.grid_ref, ...), custom_call_target="tpu_custom_call" | custom-call | tf_op jit(solution)/shard_map/own_tables/pallas_call | solution.py:230
  13.0 0.0 collective-permute-done
  13.0 0.1 add_convert_fusion
  13.0 16.0 %all_to_all.15.parts_ref = bf16[16,32,256]{2,1,0:T(8,128)(2,1)S(1)} all-to-all(bf16[16,32,256]{2,1,0:T(8,128)(2,1)S(1)} %bitcast.7), channel_id=1, replica_groups={{416,128,64,192,0,160,256,448,96,224,320,32,288,384,480,352},{417,129,6..., dimensions={0} | all-to-all | bytes 524288 | tf_op jit(solution)/shard_map/all_to_all | solution.py:375
  29.0 0.3 occupancy.1
  29.3 10.6 %all_to_all.16.parts_ref = f32[16,2,128]{2,1,0:T(2,128)S(1)} all-to-all(f32[16,2,128]{2,1,0:T(2,128)S(1)} %get-tuple-element.26), channel_id=1, replica_groups={{13,1,0,2,9,3,7,8,10,15,4,6,11,14,5,12},{29,17,16,18,25,19,23,24,26,31,..., dimensions={0} | all-to-all | bytes 32768 | tf_op jit(solution)/shard_map/all_to_all | solution.py:375
  39.8 0.4 weigh.1
  40.2 14.9 %all_to_all.17 = bf16[16,32,256]{2,1,0:T(8,128)(2,1)S(1)} all-to-all(bf16[16,32,256]{2,1,0:T(8,128)(2,1)S(1)} %get-tuple-element.30), channel_id=1, replica_groups={{416,128,64,192,0,160,256,448,96,224,320,32,288,384,480,352},{417,129,6..., dimensions={0} | all-to-all | bytes 524288 | tf_op jit(solution)/shard_map/all_to_all | solution.py:375
  55.1 5.1 %collective-permute-start.1 = (bf16[512,256]{1,0:T(8,128)(2,1)S(1)}, bf16[512,256]{1,0:T(8,128)(2,1)S(1)}, u32[]{:S(2)}, u32[]{:S(2)}) collective-permute-start(bf16[512,256]{1,0:T(8,128)(2,1)S(1)} %bitcast.5), channel_id=1, source_target_pairs={{0,16},{16,0},{1,17},{17,1},{2,18},{18,2},{3,19},{19,3},{4,20},{20... | collective-permute-start | bytes 786440 | tf_op jit(solution)/shard_map/ppermute | solution.py:398
  60.3 0.8 %back.1 = (f32[512,256]{1,0:T(8,128)S(1)}, bf16[2,512,512]{2,1,0:T(8,128)(2,1)S(1)}, f32[4,8,8]{2,1,0:T(8,128)}) custom-call(bf16[512,1024]{1,0:T(8,128)(2,1)S(1)} %get-tuple-element.22.table_ref, bf16[512,256]{1,0:T(8,128)(2,1)S(1)} %bitcast.6, bf16[512,1024]{1,0:T(8,128)(2,1)S(1)} %get-tuple-element.31.other_ref, f32[8,64]{1,0:T(8,128)S(1)} %get-tuple-element.32.onsite_ref), custom_call_target="tpu_custom_call" | custom-call | tf_op jit(solution)/shard_map/back/pallas_call | solution.py:328
  61.1 0.3 collective-permute-done.1.weighted_ref
  61.4 1.1 %back_last.1 = bf16[2,512,128]{2,1,0:T(8,128)(2,1)} custom-call(bf16[2,512,512]{2,1,0:T(8,128)(2,1)S(1)} %get-tuple-element.33.table_ref, bf16[512,256]{1,0:T(8,128)(2,1)S(1)} %collective-permute-done.1.weighted_ref, f32[512,256]{1,0:T(8,128)S(1)} %get-tuple-element.34.before_ref), custom_call_target="tpu_custom_call" | custom-call | tf_op jit(solution)/shard_map/back_last/pallas_call | solution.py:356
Async XLA Ops:
  0.6 10.8 %copy-start = (f32[4,8,8]{2,1,0:T(8,128)S(1)}, f32[4,8,8]{2,1,0:T(8,128)}, u32[]{:S(2)}) copy-start(f32[4,8,8]{2,1,0:T(8,128)} %param.17) | copy-start | bytes 3076
  2.7 10.3 %collective-permute-start = (bf16[512,256]{1,0:T(8,128)(2,1)S(1)}, bf16[512,256]{1,0:T(8,128)(2,1)S(1)}, u32[]{:S(2)}, u32[]{:S(2)}) collective-permute-start(bf16[512,256]{1,0:T(8,128)(2,1)S(1)} %get-tuple-element.24), channel_id=1, source_target_pairs={{0,16},{16,0},{1,17},{17,1},{2,18},{18,2},{3,19},{19,3},{4,20},{20... | collective-permute-start | bytes 786440 | tf_op jit(solution)/shard_map/ppermute | solution.py:388
  55.1 6.3 %collective-permute-start.1 = (bf16[512,256]{1,0:T(8,128)(2,1)S(1)}, bf16[512,256]{1,0:T(8,128)(2,1)S(1)}, u32[]{:S(2)}, u32[]{:S(2)}) collective-permute-start(bf16[512,256]{1,0:T(8,128)(2,1)S(1)} %bitcast.5), channel_id=1, source_target_pairs={{0,16},{16,0},{1,17},{17,1},{2,18},{18,2},{3,19},{19,3},{4,20},{20... | collective-permute-start | bytes 786440 | tf_op jit(solution)/shard_map/ppermute | solution.py:398
